TPU v7x, 32 devices: a whole 2x2x4 slice. The times are simulated.
32 devices in a mesh: row: 4 (over y, x), col: 8 (over z, core).
Axes of the slice: x: 2, y: 2, z: 4, core: 2. Of those that a mesh axis runs over, the one named last changes fastest.
Arguments:
- tokens: bfloat16 [16384, 1024], P(('row', 'col')), may hold values from -6 to 6
- blocks: int32 [16384], P(('row', 'col')), may hold values from 0 to 127, never falling along the last dimension, each value on 1 to 256 neighbouring positions
- w_qkv: bfloat16 [1024, 3, 1024], P('row', None, 'col'), may hold values from -0.25 to 0.25
- b_qv: bfloat16 [2, 1024], P(None, 'col'), may hold values from -1.5 to 1.5
- w_out: bfloat16 [1024, 1024], P('col', 'row'), may hold values from -0.5 to 0.5
- b_out: bfloat16 [1024], replicated, may hold values from -3 to 3
- w_up: bfloat16 [4096, 1024], P('col', 'row'), may hold values from -0.1875 to 0.1875
- b_up: bfloat16 [4096], P('col'), may hold values from -3 to 3
- w_down: bfloat16 [4096, 1024], P('col', 'row'), may hold values from -0.09375 to 0.09375
- b_down: bfloat16 [1024], replicated, may hold values from -3 to 3
- gain1: bfloat16 [1024], replicated, may hold values from 0.5 to 1.5
- shift1: bfloat16 [1024], replicated, may hold values from -1.5 to 1.5
- gain2: bfloat16 [1024], replicated, may hold values from 0.5 to 1.5
- shift2: bfloat16 [1024], replicated, may hold values from -1.5 to 1.5
- grad_out: bfloat16 [16384, 1024], P(('row', 'col')), may hold values from -9 to 9
Outputs:
- output: bfloat16 [16384, 1024], P(('row', 'col'))
- grad_tokens: float32 [16384, 1024], P(('row', 'col'))
- grad_w_qkv: float32 [1024, 3, 1024], P('row', None, 'col')
- grad_b_qv: float32 [2, 1024], P(None, 'col')
- grad_w_out: float32 [1024, 1024], P('col', 'row')
- grad_b_out: float32 [1024], replicated
- grad_w_up: float32 [4096, 1024], P('col', 'row')
- grad_b_up: float32 [4096], P('col')
- grad_w_down: float32 [4096, 1024], P('col', 'row')
- grad_b_down: float32 [1024], replicated
- grad_gain1: float32 [1024], replicated
- grad_shift1: float32 [1024], replicated
- grad_gain2: float32 [1024], replicated
- grad_shift2: float32 [1024], replicated
Inputs may be any that keep to these rules, and one draw needn't show every extreme that they name: `blocks`: block indices never fall along the tokens and every index from the least to the largest occurs; each block holds 1 to 256 tokens, and one holds exactly 256. A block may run across the end of a sequence.
All inputs are finite; a program needn't handle non-finite values.
Results may differ from a plain program's by a relative error of at most 0.012.
The roundings to bfloat16 on the way count: a program that leaves them out, or rounds other values in their place, can miss the bound.
Values may be sent and summed in bfloat16 or wider, within the bound.
A program may use at most 256 MiB of HBM per device.

v0:
```python
import jax
import jax.numpy as jnp
from jax import lax
from jax.sharding import PartitionSpec as P

HD = 64
SEQ_LEN = 4096


EPS = 1e-05


def norm(values_in, gain, shift):
    center = jnp.mean(values_in, axis=-1, keepdims=True)
    centered = values_in - center
    spread = jnp.mean(centered * centered, axis=-1, keepdims=True)
    return centered * lax.rsqrt(spread + EPS) * gain + shift


def gelu_tanh(values_in):
    return jax.nn.gelu(values_in, approximate=True)


def gather_tokens(rows_in):
    return lax.all_gather(rows_in, "col", axis=0, tiled=True)


def sum_tokens(term_fn, local_rows):
    return lax.psum_scatter(
        term_fn(jnp.int32(0), lax.axis_size("col") * local_rows),
        "col",
        scatter_dimension=0,
        tiled=True,
    )


def body(
    tokens,
    blocks,
    w_qkv,
    b_qv,
    w_out,
    b_out,
    w_up,
    b_up,
    w_down,
    b_down,
    gain1,
    shift1,
    gain2,
    shift2,
    grad_out,
):
    f32 = jnp.float32
    bf16 = jnp.bfloat16
    local_rows = tokens.shape[0]
    model_width = tokens.shape[1]
    col_count = lax.axis_size("col")
    group_rows = local_rows * col_count
    head_cols = w_qkv.shape[2]
    heads_here = head_cols // HD
    score_scale = HD ** (-0.5)
    query_rows = min(512, SEQ_LEN)
    block_count = group_rows // query_rows
    qkv_weight = lax.all_gather(w_qkv, "row", axis=0, tiled=True)
    qkv_flat = qkv_weight.reshape(model_width, 3 * head_cols)
    out_weight, down_weight, up_weight = (
        lax.all_gather(w_out, "row", axis=1, tiled=True),
        lax.all_gather(w_down, "row", axis=1, tiled=True),
        lax.all_gather(w_up, "row", axis=1, tiled=True),
    )
    tokens_f = tokens.astype(f32)
    normed_in, norm1_back = jax.vjp(norm, tokens_f, gain1.astype(f32), shift1.astype(f32))
    attn_input = normed_in.astype(bf16)
    attn_rows, block_ids = (
        lax.all_gather(attn_input, "col", axis=0, tiled=True),
        lax.all_gather(blocks, "col", axis=0, tiled=True),
    )
    bias_qv = b_qv.astype(f32)
    mixed = jnp.dot(attn_rows, qkv_flat, preferred_element_type=f32).reshape(
        group_rows, 3, head_cols
    )
    queries = (mixed[:, 0] + bias_qv[0]).astype(bf16).reshape(group_rows, heads_here, HD)
    keys = mixed[:, 1].astype(bf16).reshape(group_rows, heads_here, HD)
    values = (mixed[:, 2] + bias_qv[1]).astype(bf16).reshape(group_rows, heads_here, HD)

    def block_scores(row_start):
        seq_start = row_start // SEQ_LEN * SEQ_LEN
        query_part = lax.dynamic_slice_in_dim(queries, row_start, query_rows, 0)
        key_seq = lax.dynamic_slice_in_dim(keys, seq_start, SEQ_LEN, 0)
        query_blocks = lax.dynamic_slice_in_dim(block_ids, row_start, query_rows, 0)
        key_blocks = lax.dynamic_slice_in_dim(block_ids, seq_start, SEQ_LEN, 0)
        raw_scores = jnp.einsum("qhd,khd->hqk", query_part, key_seq, preferred_element_type=f32)
        allowed = query_blocks[:, None] >= key_blocks[None, :]
        scores = jnp.where(allowed[None], raw_scores * score_scale, -1e30)
        return (scores, query_part, key_seq, seq_start)

    def forward_block(block_index):
        row_start = block_index * query_rows
        scores, query_part, key_seq, seq_start = block_scores(row_start)
        value_seq = lax.dynamic_slice_in_dim(values, seq_start, SEQ_LEN, 0)
        row_max = jnp.max(scores, axis=-1, keepdims=True)
        row_total = jnp.sum(jnp.exp(scores - row_max), axis=-1, keepdims=True)
        log_total = row_max + jnp.log(row_total)
        probs_low = jnp.exp(scores - log_total).astype(bf16)
        block_out = jnp.einsum("hqk,khd->qhd", probs_low, value_seq, preferred_element_type=f32)
        return (block_out, log_total)

    block_outs, log_totals = lax.map(forward_block, jnp.arange(block_count, dtype=jnp.int32))
    heads_out = block_outs.reshape(group_rows, head_cols).astype(bf16)
    part = heads_out
    attn_branch = lax.psum_scatter(
        jnp.dot(part, out_weight, preferred_element_type=f32),
        "col",
        scatter_dimension=0,
        tiled=True,
    )
    resid = tokens_f + attn_branch + b_out.astype(f32)
    normed_mid, norm2_back = jax.vjp(norm, resid, gain2.astype(f32), shift2.astype(f32))
    ffn_input = normed_mid.astype(bf16)
    up_all, down_all, up_bias = (up_weight, down_weight, b_up)
    ffn_rows = gather_tokens(ffn_input)
    up_pre = jnp.einsum("td,fd->tf", ffn_rows, up_all, preferred_element_type=f32) + up_bias.astype(
        f32
    )
    hidden_f, gelu_back = jax.vjp(gelu_tanh, up_pre)
    hidden = hidden_f.astype(bf16)
    part = hidden
    ffn_branch = lax.psum_scatter(
        jnp.dot(part, down_all, preferred_element_type=f32).astype(jnp.bfloat16),
        "col",
        scatter_dimension=0,
        tiled=True,
    ).astype(jnp.float32)
    output = (resid + ffn_branch + b_down.astype(f32)).astype(bf16)
    grad_f = grad_out.astype(f32)
    grad_bdown = jnp.sum(grad_f, axis=0)
    grad_rows = gather_tokens(grad_out)
    grad_wdown = jnp.einsum("tf,td->fd", hidden, grad_rows, preferred_element_type=f32)
    d_hidden = jnp.einsum("td,fd->tf", grad_rows, down_all, preferred_element_type=f32)
    d_up = gelu_back(d_hidden)[0]
    grad_bup = jnp.sum(d_up, axis=0)
    d_up_low = d_up.astype(bf16)
    grad_wup = jnp.einsum("tf,td->fd", d_up_low, ffn_rows, preferred_element_type=f32)

    def up_term(row_start, count):
        return jnp.dot(d_up_low, up_all, preferred_element_type=f32)

    d_norm2 = sum_tokens(up_term, local_rows)
    d_resid_in, grad_gain2, grad_shift2 = norm2_back(d_norm2)
    d_resid = grad_f + d_resid_in
    grad_bout = jnp.sum(d_resid, axis=0)
    d_resid_low = d_resid.astype(bf16)
    resid_rows = gather_tokens(d_resid_low)
    grad_wout = jnp.einsum("tk,td->kd", heads_out, resid_rows, preferred_element_type=f32)
    d_heads = jnp.einsum("td,kd->tk", resid_rows, out_weight, preferred_element_type=f32).astype(
        bf16
    )
    d_heads = d_heads.reshape(group_rows, heads_here, HD)

    def backward_block(carry, block_index):
        grad_keys, grad_values = carry
        row_start = block_index * query_rows
        scores, query_part, key_seq, seq_start = block_scores(row_start)
        value_seq = lax.dynamic_slice_in_dim(values, seq_start, SEQ_LEN, 0)
        probs = jnp.exp(scores - log_totals[block_index])
        probs_low = probs.astype(bf16)
        dout_part = lax.dynamic_slice_in_dim(d_heads, row_start, query_rows, 0)
        value_part = jnp.einsum("hqk,qhd->khd", probs_low, dout_part, preferred_element_type=f32)
        d_probs = jnp.einsum("qhd,khd->hqk", dout_part, value_seq, preferred_element_type=f32)
        d_scores = probs * (d_probs - jnp.sum(probs * d_probs, axis=-1, keepdims=True))
        d_scores_low = d_scores.astype(bf16)
        query_grad = (
            jnp.einsum("hqk,khd->qhd", d_scores_low, key_seq, preferred_element_type=f32)
            * score_scale
        )
        key_part = (
            jnp.einsum("hqk,qhd->khd", d_scores_low, query_part, preferred_element_type=f32)
            * score_scale
        )
        old_keys = lax.dynamic_slice_in_dim(grad_keys, seq_start, SEQ_LEN, 0)
        grad_keys = lax.dynamic_update_slice_in_dim(grad_keys, old_keys + key_part, seq_start, 0)
        old_values = lax.dynamic_slice_in_dim(grad_values, seq_start, SEQ_LEN, 0)
        grad_values = lax.dynamic_update_slice_in_dim(
            grad_values, old_values + value_part, seq_start, 0
        )
        return ((grad_keys, grad_values), query_grad)

    empty = jnp.zeros((group_rows, heads_here, HD), f32)
    (grad_keys, grad_values), grad_queries = lax.scan(
        backward_block, (empty, empty), jnp.arange(block_count, dtype=jnp.int32)
    )
    grad_queries = grad_queries.reshape(group_rows, head_cols)
    grad_keys = grad_keys.reshape(group_rows, head_cols)
    grad_values = grad_values.reshape(group_rows, head_cols)
    grad_bqv = jnp.stack([jnp.sum(grad_queries, axis=0), jnp.sum(grad_values, axis=0)])
    d_mixed = jnp.stack([grad_queries, grad_keys, grad_values], axis=1).astype(bf16)
    d_mixed_flat = d_mixed.reshape(group_rows, 3 * head_cols)
    grad_wqkv = jnp.einsum(
        "td,tk->dk", attn_rows, d_mixed_flat, preferred_element_type=f32
    ).reshape(model_width, 3, head_cols)

    def qkv_term(row_start, count):
        return jnp.einsum("tk,dk->td", d_mixed_flat, qkv_flat, preferred_element_type=f32)

    d_norm1 = sum_tokens(qkv_term, local_rows)
    d_tokens_in, grad_gain1, grad_shift1 = norm1_back(d_norm1)
    grad_tokens = d_resid + d_tokens_in
    grad_wqkv = lax.psum_scatter(grad_wqkv, "row", scatter_dimension=0, tiled=True)
    grad_wout, grad_wdown, grad_wup = (
        lax.psum_scatter(grad_wout, "row", scatter_dimension=1, tiled=True),
        lax.psum_scatter(grad_wdown, "row", scatter_dimension=1, tiled=True),
        lax.psum_scatter(grad_wup, "row", scatter_dimension=1, tiled=True),
    )
    grad_bqv, grad_bup = lax.psum((grad_bqv, grad_bup), "row")
    grad_gain1, grad_shift1, grad_gain2, grad_shift2, grad_bout, grad_bdown = lax.psum(
        (grad_gain1, grad_shift1, grad_gain2, grad_shift2, grad_bout, grad_bdown), ("row", "col")
    )
    return (
        output,
        grad_tokens,
        grad_wqkv,
        grad_bqv,
        grad_wout,
        grad_bout,
        grad_wup,
        grad_bup,
        grad_wdown,
        grad_bdown,
        grad_gain1,
        grad_shift1,
        grad_gain2,
        grad_shift2,
    )


def solution(mesh):
    return jax.shard_map(
        body,
        mesh=mesh,
        in_specs=(
            P(("row", "col"), None),
            P(("row", "col")),
            P("row", None, "col"),
            P(None, "col"),
            P("col", "row"),
            P(),
            P("col", "row"),
            P("col"),
            P("col", "row"),
            P(),
            P(),
            P(),
            P(),
            P(),
            P(("row", "col"), None),
        ),
        out_specs=(
            P(("row", "col"), None),
            P(("row", "col"), None),
            P("row", None, "col"),
            P(None, "col"),
            P("col", "row"),
            P(),
            P("col", "row"),
            P("col"),
            P("col", "row"),
            P(),
            P(),
            P(),
            P(),
            P(),
        ),
        check_vma=False,
    )
```

profile of v0, /device:TPU:0, one launch (start us, length us, event | category | flops | bytes accessed | tf_op | source)
XLA Modules:
  0.0 1737.6 jit_solution(14940055284473691748)
XLA Ops:
  15.6 12.7 all_gather.29
  28.6 13.3 all-gather
  53.8 46.6 %all-gather.8.cloned.1.call-done = bf16[4096,1024]{1,0:T(8,128)(2,1)} async-done(((bf16[512,1024]{1,0:T(8,128)(2,1)}), bf16[4096,1024]{1,0:T(8,128)(2,1)}) %all-gather.8.cloned.1.call-update) | async-done | bytes 8388624 | tf_op jit(solution)/shard_map/all_gather | solution.py:76
  107.3 127.5 %while.29 = (s32[]{:T(128)}, bf16[8,512,2,64]{1,3,2,0:T(8,128)(2,1)}, f32[8,2,512,1]{2,1,3,0:T(2,128)S(1)}, s32[8]{0:T(128)S(1)}, s32[4096]{0:T(1024)S(1)}, /*in...) while((s32[]{:T(128)}, ...), condition=%wide.region_5.6_spmd.clone, body=%wide.region_2.5_spmd.sunk.clone | while | flops 1121975296 | bytes 61266096 | solution.py:109
  246.6 166.2 %reduce-scatter.9.cloned.1.call-done = f32[512,1024]{1,0:T(8,128)} async-done(((f32[4096,1024]{1,0:T(8,128)}), f32[512,1024]{1,0:T(8,128)}) %reduce-scatter.9.cloned.1.call-update) | async-done | bytes 2097168 | tf_op jit(solution)/shard_map/reduce_scatter | solution.py:112
  418.3 78.9 %all-gather.10.cloned.1.call-done = bf16[4096,1024]{1,0:T(8,128)(2,1)} async-done(((bf16[512,1024]{1,0:T(8,128)(2,1)}), bf16[4096,1024]{1,0:T(8,128)(2,1)}) %all-gather.10.cloned.1.call-update) | async-done | bytes 8388624 | tf_op jit(solution)/shard_map/all_gather | solution.py:25
  508.6 15.2 all-gather.14.cloned.1.call-done
  523.8 83.6 %all-gather.16.cloned.1.call-done = bf16[4096,1024]{1,0:T(8,128)(2,1)} async-done(((bf16[512,1024]{1,0:T(8,128)(2,1)}), bf16[4096,1024]{1,0:T(8,128)(2,1)}) %all-gather.16.cloned.1.call-update) | async-done | bytes 8388624 | tf_op jit(solution)/shard_map/all_gather | solution.py:25
  607.4 14.9 fusion.71
  646.0 153.0 %reduce-scatter.13.cloned.1.call-done = f32[512,1024]{1,0:T(8,128)} async-done(((f32[4096,1024]{1,0:T(8,128)}), f32[512,1024]{1,0:T(8,128)}) %reduce-scatter.13.cloned.1.call-update) | async-done | bytes 2097168 | tf_op jit(solution)/shard_map/reduce_scatter | solution.py:29
  801.9 87.3 %reduce-scatter.11.cloned.1.call-done = bf16[512,1024]{1,0:T(8,128)(2,1)} async-done(((bf16[4096,1024]{1,0:T(8,128)(2,1)}), bf16[512,1024]{1,0:T(8,128)(2,1)}) %reduce-scatter.11.cloned.1.call-update) | async-done | bytes 1048592 | tf_op jit(solution)/shard_map/reduce_scatter | solution.py:129
  895.7 80.6 %all-gather.18.cloned.1.call-done = bf16[4096,1024]{1,0:T(8,128)(2,1)} async-done(((bf16[512,1024]{1,0:T(8,128)(2,1)}), bf16[4096,1024]{1,0:T(8,128)(2,1)}) %all-gather.18.cloned.1.call-update) | async-done | bytes 8388624 | tf_op jit(solution)/shard_map/all_gather | solution.py:25
  983.5 418.0 %while.30 = (s32[]{:T(128)}, f32[4096,2,64]{0,2,1:T(8,128)S(1)}, f32[4096,2,64]{0,2,1:T(8,128)}, f32[8,512,2,64]{1,3,2,0:T(8,128)}, s32[8]{0:T(128)S(1)}, /*inde...) while((s32[]{:T(128)}, f32[4096,2,64]{0,2,1:T(8,128)S(1)}, ...), condition=%wide.region_15.16_spmd.clone.clone, body=%wide.region_13.15_spmd.clone.sunk.clone | while | flops 2752052224 | bytes 217893168 | solution.py:190
  1004.5 12.6 multiply_reduce_fusion.6
  1056.8 12.6 multiply_reduce_fusion.6
  1109.0 12.7 multiply_reduce_fusion.6
  1265.7 12.7 multiply_reduce_fusion.6
  1318.0 12.7 multiply_reduce_fusion.6
  1370.2 12.7 multiply_reduce_fusion.6
  1481.0 109.6 %reduce-scatter.15.cloned.1.call-done = f32[512,1024]{1,0:T(8,128)} async-done(((f32[4096,1024]{1,0:T(8,128)}), f32[512,1024]{1,0:T(8,128)}) %reduce-scatter.15.cloned.1.call-update) | async-done | bytes 2097168 | tf_op jit(solution)/shard_map/reduce_scatter | solution.py:29
  1596.3 38.8 %all-reduce = (f32[1024]{0:T(1024)}, f32[1024]{0:T(1024)}, f32[1024]{0:T(1024)}, f32[1024]{0:T(1024)}, f32[1024]{0:T(1024)}, /*index=5*/f32[1024]{0:T(1024)}) all-reduce(f32[1024]{0:T(1024)S(1)} %get-tuple-element.165, f32[1024]{0:T(1024)S(1)} %get-tuple-element.164, ...), channel_id=1, replica_groups=mesh['row'=4,'col'=8] {'row','col'}, use_global_device_ids=true, to_apply=%region_25.26 | all-reduce | flops 6144 | bytes 49152 | tf_op jit(solution)/shard_map/psum | solution.py:216
  1635.1 31.7 %reduce-scatter.23.cloned.1.call-done = f32[512,256]{1,0:T(8,128)} async-done(((f32[512,1024]{1,0:T(8,128)}), f32[512,256]{1,0:T(8,128)}) %reduce-scatter.23.cloned.1.call-update) | async-done | bytes 524304 | tf_op jit(solution)/shard_map/reduce_scatter | solution.py:212
  1666.9 28.2 %reduce-scatter.19.cloned.1.call-done = f32[128,256]{1,0:T(8,128)} async-done(((f32[128,1024]{1,0:T(8,128)}), f32[128,256]{1,0:T(8,128)}) %reduce-scatter.19.cloned.1.call-update) | async-done | bytes 131088 | tf_op jit(solution)/shard_map/reduce_scatter | solution.py:211
  1695.1 34.8 %reduce-scatter.17.cloned.1.call-done = f32[256,3,128]{2,0,1:T(8,128)} async-done(((f32[1024,3,128]{2,0,1:T(8,128)}), f32[256,3,128]{2,0,1:T(8,128)}) %reduce-scatter.17.cloned.1.call-update) | async-done | bytes 393232 | tf_op jit(solution)/shard_map/reduce_scatter | solution.py:209
  (336 shorter events, 622.8 us)
Async XLA Ops:
  8.0 33.8 %copy-start.19 = (bf16[128,256]{1,0:T(8,128)(2,1)S(1)}, bf16[128,256]{1,0:T(8,128)(2,1)}, u32[]{:S(2)}) copy-start(bf16[128,256]{1,0:T(8,128)(2,1)} %param.23) | copy-start | bytes 196612
  8.1 92.3 %all-gather.8.cloned.1.call-start = ((), (), s32[]{:S(2)}) async-start(), calls=%async_computation.8 | async-start | bytes 9437184 | tf_op jit(solution)/shard_map/all_gather | solution.py:76
  15.3 397.5 %reduce-scatter.9.cloned.1.call-start = ((), (), s32[]{:S(2)}) async-start(), calls=%async_computation.9 | async-start | bytes 18874368 | tf_op jit(solution)/shard_map/reduce_scatter | solution.py:112
  28.3 78.0 %copy-start.12 = (bf16[1024,3,128]{2,0,1:T(8,128)(2,1)}, bf16[1024,3,128]{2,0,1:T(8,128)(2,1)S(1)}, u32[]{:S(2)}) copy-start(bf16[1024,3,128]{2,0,1:T(8,128)(2,1)S(1)} %all_gather.29) | copy-start | bytes 2359300
  245.9 172.4 %all-gather.12.cloned.1.call-start = ((), (), s32[]{:S(2)}) async-start(), calls=%async_computation.11 | async-start | bytes 1310720 | tf_op jit(solution)/shard_map/all_gather | solution.py:70
  246.5 250.7 %all-gather.10.cloned.1.call-start = ((), (), s32[]{:S(2)}) async-start(), calls=%async_computation.10 | async-start | bytes 9437184 | tf_op jit(solution)/shard_map/all_gather | solution.py:25
  416.9 106.9 %all-gather.14.cloned.1.call-start = ((), (), s32[]{:S(2)}) async-start(), calls=%async_computation.12 | async-start | bytes 1310720 | tf_op jit(solution)/shard_map/all_gather | solution.py:69
  417.4 189.9 %all-gather.16.cloned.1.call-start = ((), (), s32[]{:S(2)}) async-start(), calls=%async_computation.14 | async-start | bytes 9437184 | tf_op jit(solution)/shard_map/all_gather | solution.py:25
  418.2 380.8 %reduce-scatter.13.cloned.1.call-start = ((), (), s32[]{:S(2)}) async-start(), calls=%async_computation.15 | async-start | bytes 18874368 | tf_op jit(solution)/shard_map/reduce_scatter | solution.py:29
  418.2 214.5 %copy-start.34 = (f32[512]{0:T(512)}, f32[512]{0:T(512)S(1)}, u32[]{:S(2)}) copy-start(f32[512]{0:T(512)S(1)} %convert_element_type.106) | copy-start | bytes 6148
  632.3 256.9 %reduce-scatter.11.cloned.1.call-start = ((), (), s32[]{:S(2)}) async-start(), calls=%async_computation.13 | async-start | bytes 9437184 | tf_op jit(solution)/shard_map/reduce_scatter | solution.py:129
  645.4 330.9 %all-gather.18.cloned.1.call-start = ((), (), s32[]{:S(2)}) async-start(), calls=%async_computation.16 | async-start | bytes 9437184 | tf_op jit(solution)/shard_map/all_gather | solution.py:25
  895.6 695.0 %reduce-scatter.15.cloned.1.call-start = ((), (), s32[]{:S(2)}) async-start(), calls=%async_computation.17 | async-start | bytes 18874368 | tf_op jit(solution)/shard_map/reduce_scatter | solution.py:29
  1423.7 211.4 %reduce-scatter.21.cloned.1.call-start = ((), (), s32[]{:S(2)}) async-start(), calls=%async_computation.20 | async-start | bytes 2621440 | tf_op jit(solution)/shard_map/reduce_scatter | solution.py:213
  1434.4 232.5 %reduce-scatter.23.cloned.1.call-start = ((), (), s32[]{:S(2)}) async-start(), calls=%async_computation.21 | async-start | bytes 2621440 | tf_op jit(solution)/shard_map/reduce_scatter | solution.py:212
  1446.7 248.4 %reduce-scatter.19.cloned.1.call-start = ((), (), s32[]{:S(2)}) async-start(), calls=%async_computation.19 | async-start | bytes 655360 | tf_op jit(solution)/shard_map/reduce_scatter | solution.py:211
  1459.1 270.8 %reduce-scatter.17.cloned.1.call-start = ((), (), s32[]{:S(2)}) async-start(), calls=%async_computation.18 | async-start | bytes 1966080 | tf_op jit(solution)/shard_map/reduce_scatter | solution.py:209
  1468.2 122.4 %copy-start.1 = (bf16[512,1024]{1,0:T(8,128)(2,1)S(1)}, bf16[512,1024]{1,0:T(8,128)(2,1)}, u32[]{:S(2)}) copy-start(bf16[512,1024]{1,0:T(8,128)(2,1)} %param.19) | copy-start | bytes 3145732
  1468.2 122.4 %copy-start.16 = (f32[1024]{0:T(1024)S(1)}, f32[1024]{0:T(1024)}, u32[]{:S(2)}) copy-start(f32[1024]{0:T(1024)} %copy-done.15) | copy-start | bytes 12292
  1468.2 122.4 %copy-start.18 = (f32[512]{0:T(512)S(1)}, f32[512]{0:T(512)}, u32[]{:S(2)}) copy-start(f32[512]{0:T(512)} %copy-done.17) | copy-start | bytes 6148
  1468.2 124.7 %copy-start.25 = (f32[512]{0:T(512)S(1)}, f32[512]{0:T(512)}, u32[]{:S(2)}) copy-start(f32[512]{0:T(512)} %copy-done.24) | copy-start | bytes 6148
  1468.2 124.7 %copy-start.21 = (f32[512]{0:T(512)S(1)}, f32[512]{0:T(512)}, u32[]{:S(2)}) copy-start(f32[512]{0:T(512)} %copy-done.20) | copy-start | bytes 6148
  1468.5 125.5 %copy-start.6 = (f32[512,1024]{1,0:T(8,128)S(1)}, f32[512,1024]{1,0:T(8,128)}, u32[]{:S(2)}) copy-start(f32[512,1024]{1,0:T(8,128)} %copy-done.5) | copy-start | bytes 6291460
  1468.5 125.5 %copy-start.23 = (f32[512]{0:T(512)S(1)}, f32[512]{0:T(512)}, u32[]{:S(2)}) copy-start(f32[512]{0:T(512)} %copy-done.22) | copy-start | bytes 6148
  (44 other events, 246.4 us)
Sparse Core Ops, SparseCore 0:
  15.5 84.8 all-gather.7
  246.0 166.7 reduce-scatter.8
  895.7 80.5 all-gather.17
  1423.8 166.7 reduce-scatter.14
  1594.0 33.9 reduce-scatter.20
  1631.6 35.1 reduce-scatter.22
  1670.3 24.7 reduce-scatter.18
  1698.9 30.9 reduce-scatter.16
Sparse Core Ops, SparseCore 1:
  248.2 24.8 all-gather.11
  416.9 80.2 all-gather.9
  498.9 24.8 all-gather.13
  525.4 81.9 all-gather.15
  632.4 166.6 reduce-scatter.12
  801.3 87.8 reduce-scatter.10
where the time goes:
time: 1740 us
  waiting for transfers between devices  918 us (53%)
  matrix products  421 us (24%)
  other arithmetic  186 us (11%)
  blocking collectives  85.9 us (5%)
  local copies, waits for them, and re-layouts  82.3 us (5%)
  loops' own time  26.9 us (2%)
    reduce_scatter x2, waiting for transfers between devices, sum_tokens(): lax.psum_scatter(term_fn(jnp.int32(0), lax.axis_size('col') * local_rows)...  263 us
    all_gather x3, waiting for transfers between devices, gather_tokens(): return lax.all_gather(rows_in, 'col', axis=0, tiled=True)  243 us
    reduce_scatter x1, waiting for transfers between devices, body(): lax.psum_scatter(jnp.dot(part, out_weight, preferred_element_type=f32), '...  166 us
    dot_general x8, matrix products, backward_block(): jnp.einsum('qhd,khd->hqk', dout_part, value_seq, preferred_element_type=f32)  101 us
    convert_element_type x8, other arithmetic, backward_block(): d_scores_low = d_scores.astype(bf16)  98.2 us
    reduce_scatter x1, waiting for transfers between devices, body(): lax.psum_scatter(jnp.dot(part, down_all, preferred_element_type=f32).asty...  87.3 us
    dot_general x8, matrix products, backward_block(): jnp.einsum('hqk,qhd->khd', probs_low, dout_part, preferred_element_type=f32)  60.6 us
    dot_general x16, matrix products, block_scores(): jnp.einsum('qhd,khd->hqk', query_part, key_seq, preferred_element_type=f32)  56.2 us
  transfers between devices with their start and end apart: 14, of which 12 were waited for; matrix products, arithmetic and copies ran while one was open for 5% of the time, Pallas kernels for 0%

commit v1 on v0

v1 whole, which is shorter than its diff:
```python
import functools

import jax
import jax.numpy as jnp
from jax import lax
from jax.experimental import pallas as pl
from jax.experimental.pallas import tpu as pltpu
from jax.sharding import PartitionSpec as P

HD = 64
SEQ_LEN = 4096
BLOCK = 256
EPS = 1e-05
SCALE = HD ** (-0.5)
SCALE2 = SCALE * 1.4426950408889634
MASKED = -1e30
ONES = 16
MESH = pl.DeviceIdType.MESH
VMEM_LIMIT = 60 << 20

f32 = jnp.float32
bf16 = jnp.bfloat16

NN = (((1,), (0,)), ((), ()))
NT = (((1,), (1,)), ((), ()))
TN = (((0,), (0,)), ((), ()))


def dot(a, b, dims=NN):
    return lax.dot_general(a, b, dims, preferred_element_type=f32)


def flip(x):
    return x.astype(f32).T.astype(bf16)


def params(**more):
    return pltpu.CompilerParams(vmem_limit_bytes=VMEM_LIMIT, **more)


def cost(flops, nbytes, transcendentals=0):
    return pl.CostEstimate(flops=flops, bytes_accessed=nbytes, transcendentals=transcendentals)


def whole(shape):
    return pl.BlockSpec(shape, lambda *_: (0,) * len(shape))


def moments(v):
    center = jnp.mean(v, axis=-1, keepdims=True)
    centered = v - center
    spread = jnp.mean(centered * centered, axis=-1, keepdims=True)
    inv = lax.rsqrt(spread + EPS)
    return centered * inv, inv


def norm_back(xhat, inv, e):
    return inv * (
        e - jnp.mean(e, axis=-1, keepdims=True) - xhat * jnp.mean(e * xhat, axis=-1, keepdims=True)
    )


def gather_kernel(
    rows, cols, x_ref, blk_ref, bup_ref, w_ref, xo_ref, blko_ref, bupo_ref, wo_ref,
    send_x, recv_x, send_s, recv_s, send_w, recv_w, local,
):
    row, me = lax.axis_index("row"), lax.axis_index("col")
    chips = cols // 2
    chip, lane = me // 2, lax.rem(me, 2)
    mate = chip * 2 + 1 - lane
    depth = w_ref.shape[0]

    barrier = pltpu.get_barrier_semaphore()
    for k in range(1, cols):
        pl.semaphore_signal(
            barrier, inc=1, device_id=(row, lax.rem(me + k, cols)), device_id_type=MESH
        )
    for k in range(1, rows):
        pl.semaphore_signal(
            barrier, inc=1, device_id=(lax.rem(row + k, rows), me), device_id_type=MESH
        )
    pl.semaphore_wait(barrier, rows + cols - 2)

    def chunk(src, owner, target, route, at):
        return pltpu.make_async_remote_copy(
            src_ref=src,
            dst_ref=xo_ref.at[owner],
            send_sem=send_x.at[route, at],
            recv_sem=recv_x.at[route, at],
            device_id=(row, target),
            device_id_type=MESH,
        )

    @pl.when(chip + 1 < chips)
    def _():
        chunk(x_ref, me, me + 2, 0, chip).start()

    @pl.when(chip > 0)
    def _():
        chunk(x_ref, me, me - 2, 1, chip).start()

    chunk(x_ref, me, mate, 2, chip).start()
    weights = []
    where = pl.ds(pl.multiple_of(row * depth, depth), depth)
    for k in range(1, rows):
        copy = pltpu.make_async_remote_copy(
            src_ref=w_ref,
            dst_ref=wo_ref.at[where],
            send_sem=send_w.at[k],
            recv_sem=recv_w.at[k],
            device_id=(lax.rem(row + k, rows), me),
            device_id_type=MESH,
        )
        copy.start()
        weights.append(copy)
    small = []
    for k in range(1, cols):
        for at, (src, dst) in enumerate(((blk_ref, blko_ref), (bup_ref, bupo_ref))):
            copy = pltpu.make_async_remote_copy(
                src_ref=src,
                dst_ref=dst.at[me],
                send_sem=send_s.at[at, k],
                recv_sem=recv_s.at[at, k],
                device_id=(row, lax.rem(me + k, cols)),
                device_id_type=MESH,
            )
            copy.start()
            small.append(copy)
    own = [
        pltpu.make_async_copy(x_ref, xo_ref.at[me], local.at[0]),
        pltpu.make_async_copy(blk_ref, blko_ref.at[me], local.at[1]),
        pltpu.make_async_copy(bup_ref, bupo_ref.at[me], local.at[2]),
        pltpu.make_async_copy(w_ref, wo_ref.at[where], local.at[3]),
    ]
    for copy in own:
        copy.start()

    for hop in range(1, chips):
        below, above = chip - hop, chip + hop

        @pl.when(below >= 0)
        def _():
            owner = below * 2 + lane
            chunk(xo_ref.at[owner], owner, me, 0, below).wait_recv()

            @pl.when(chip + 1 < chips)
            def _():
                chunk(xo_ref.at[owner], owner, me + 2, 0, below).start()

            chunk(xo_ref.at[owner], owner, mate, 2, below).start()

        @pl.when(above < chips)
        def _():
            owner = above * 2 + lane
            chunk(xo_ref.at[owner], owner, me, 1, above).wait_recv()

            @pl.when(chip > 0)
            def _():
                chunk(xo_ref.at[owner], owner, me - 2, 1, above).start()

            chunk(xo_ref.at[owner], owner, mate, 2, above).start()

    for at in range(chips):
        copy = chunk(x_ref, me, mate, 2, at)
        copy.wait_recv()
        copy.wait_send()

        @pl.when((at <= chip) & (chip + 1 < chips))
        def _():
            chunk(x_ref, me, me, 0, at).wait_send()

        @pl.when((at >= chip) & (chip > 0))
        def _():
            chunk(x_ref, me, me, 1, at).wait_send()

    for copy in weights + small + own:
        copy.wait()


def gather_inputs(x, blocks, b_up, w_qkv, rows, cols):
    any_space = pl.BlockSpec(memory_space=pl.ANY)
    vmem = pl.BlockSpec(memory_space=pltpu.VMEM)
    chips = cols // 2
    dma = pltpu.SemaphoreType.DMA
    return pl.pallas_call(
        functools.partial(gather_kernel, rows, cols),
        out_shape=[
            jax.ShapeDtypeStruct((cols,) + x.shape, x.dtype),
            jax.ShapeDtypeStruct((cols,) + blocks.shape, blocks.dtype),
            jax.ShapeDtypeStruct((cols,) + b_up.shape, b_up.dtype),
            jax.ShapeDtypeStruct((rows * w_qkv.shape[0], w_qkv.shape[1]), w_qkv.dtype),
        ],
        in_specs=[vmem] * 4,
        out_specs=[any_space] * 4,
        scratch_shapes=[
            dma((3, chips)), dma((3, chips)),
            dma((2, cols)), dma((2, cols)),
            dma((rows,)), dma((rows,)), dma((4,)),
        ],
        compiler_params=pltpu.CompilerParams(collective_id=0, has_side_effects=True),
        name="gather_inputs",
    )(x, blocks, b_up, w_qkv)


def qkv_kernel(x_ref, w_ref, b_ref, q_ref, k_ref, v_ref):
    mixed = dot(x_ref[...], w_ref[...])
    width = q_ref.shape[1]
    bias = b_ref[...].astype(f32)
    q_ref[...] = (mixed[:, :width] + bias[0:1]).astype(bf16)
    k_ref[...] = mixed[:, width : 2 * width].astype(bf16)
    v_ref[...] = (mixed[:, 2 * width :] + bias[1:2]).astype(bf16)


def project_qkv(x, w, bias):
    count, depth = x.shape
    width = w.shape[1] // 3
    tile = min(1024, count)
    out = pl.BlockSpec((tile, width), lambda i: (i, 0))
    return pl.pallas_call(
        qkv_kernel,
        grid=(count // tile,),
        in_specs=[pl.BlockSpec((tile, depth), lambda i: (i, 0)), whole(w.shape), whole(bias.shape)],
        out_specs=[out] * 3,
        out_shape=[jax.ShapeDtypeStruct((count, width), bf16)] * 3,
        compiler_params=params(),
        cost_estimate=cost(2 * count * depth * 3 * width, 2 * count * (depth + 3 * width)),
        name="project_qkv",
    )(x, w, bias)


def tile_mask(blk_ref, key_start, count, query_blocks):
    key_blocks = jnp.broadcast_to(blk_ref[0, :, pl.ds(key_start, count)], (128, count)).T[:, :1]
    return query_blocks >= key_blocks


def attend_kernel(head, step, blk_ref, q_ref, k_ref, v_ref, o_ref, lse_ref, values):
    i = pl.program_id(1)
    tile = q_ref.shape[0]
    chunks, _, chunk = o_ref.shape
    lanes = slice(head * HD, (head + 1) * HD)

    @pl.when(i == 0)
    def _():
        values[:HD, :] = flip(v_ref[:, lanes])
        values[HD:, :] = jnp.ones((ONES, values.shape[1]), bf16)

    start = pl.multiple_of(i * tile, tile)
    query = q_ref[:, lanes]
    query_blocks = blk_ref[0, :, pl.ds(start, tile)]

    def update(state, key_start, count, masked):
        total, top = state
        scores = dot(k_ref[pl.ds(key_start, count), lanes], query, NT)
        if masked:
            mask = tile_mask(blk_ref, key_start, count, query_blocks)
            scores = jnp.where(mask, scores, MASKED)
        higher = jnp.maximum(top, jnp.max(scores, axis=0, keepdims=True) * SCALE2)
        probs = jnp.exp2(scores * SCALE2 - higher)
        part = dot(values[:, pl.ds(key_start, count)], probs.astype(bf16))
        return total * jnp.exp2(top - higher) + part, higher

    state = (jnp.zeros((HD + ONES, tile), f32), jnp.full((1, tile), MASKED, f32))
    state = lax.fori_loop(
        0, start // step, lambda j, s: update(s, pl.multiple_of(j * step, step), step, False), state
    )
    state = update(state, start, tile, True)
    total, top = lax.fori_loop(
        0,
        jnp.where(i < pl.num_programs(1) - 1, 1, 0),
        lambda j, s: update(s, pl.multiple_of(start + tile, BLOCK), BLOCK, True),
        state,
    )
    mass = total[HD : HD + 1]
    out = (total[:HD] / mass).astype(bf16)
    for b in range(chunks):
        o_ref[b] = out[:, b * chunk : (b + 1) * chunk]
    lse_ref[0] = top + jnp.log2(mass)


def attend(q, k, v, blocks, head, chunk):
    count, width = q.shape
    seqs = count // SEQ_LEN
    tile = 1024
    tiles = SEQ_LEN // tile
    pairs = seqs * SEQ_LEN * SEQ_LEN * 5 // 8
    return pl.pallas_call(
        functools.partial(attend_kernel, head, tile),
        grid=(seqs, tiles),
        in_specs=[
            pl.BlockSpec((1, 1, SEQ_LEN), lambda s, i: (s, 0, 0)),
            pl.BlockSpec((tile, width), lambda s, i: (s * tiles + i, 0)),
            pl.BlockSpec((SEQ_LEN, width), lambda s, i: (s, 0)),
            pl.BlockSpec((SEQ_LEN, width), lambda s, i: (s, 0)),
        ],
        out_specs=[
            pl.BlockSpec((tile // chunk, HD, chunk), lambda s, i: (s * tiles + i, 0, 0)),
            pl.BlockSpec((1, 1, tile), lambda s, i: (s, 0, i)),
        ],
        out_shape=[
            jax.ShapeDtypeStruct((count // chunk, HD, chunk), bf16),
            jax.ShapeDtypeStruct((seqs, 1, SEQ_LEN), f32),
        ],
        scratch_shapes=[pltpu.VMEM((HD + ONES, SEQ_LEN), bf16)],
        compiler_params=params(),
        cost_estimate=cost(16 * pairs * HD, 4 * count * width * 2, pairs),
        name="attend",
    )(blocks, q, k, v)


def attend_back_kernel(
    head, step, sub, blk_ref, q_ref, k_ref, v_ref, do_ref, o_ref, lse_ref, dm_ref, sum_ref,
    key_grad, value_grad,
):
    turn = pl.program_id(1)
    tiles = pl.num_programs(1)
    i = tiles - 1 - turn
    tile = q_ref.shape[0]
    chunks, _, chunk = do_ref.shape
    parts = tile // sub
    lanes = slice(head * HD, (head + 1) * HD)
    start = pl.multiple_of(i * tile, tile)

    @pl.when(turn == 0)
    def _():
        key_grad[...] = jnp.zeros_like(key_grad)
        value_grad[...] = jnp.zeros_like(value_grad)
        sum_ref[...] = jnp.zeros_like(sum_ref)

    d_out = jnp.concatenate([do_ref[b] for b in range(chunks)], axis=1)
    out = jnp.concatenate([o_ref[b] for b in range(chunks)], axis=1)
    delta = jnp.sum(d_out.astype(f32) * out.astype(f32), axis=0, keepdims=True)
    lse = lse_ref[0]

    def cut(x, a):
        return x[:, a * sub : (a + 1) * sub]

    queries = [q_ref[a * sub : (a + 1) * sub, lanes] for a in range(parts)]
    query_blocks = [
        blk_ref[0, :, pl.ds(pl.multiple_of(start + a * sub, sub), sub)] for a in range(parts)
    ]

    def update(a, query_grad, key_start, count, masked):
        keys = k_ref[pl.ds(key_start, count), lanes]
        values = v_ref[pl.ds(key_start, count), lanes]
        scores = dot(keys, queries[a], NT) * SCALE2 - cut(lse, a)
        if masked:
            mask = tile_mask(blk_ref, key_start, count, query_blocks[a])
            scores = jnp.where(mask, scores, MASKED)
        probs = jnp.exp2(scores)
        d_values = dot(probs.astype(bf16), cut(d_out, a), NT)
        d_scores = (probs * (dot(values, cut(d_out, a)) - cut(delta, a))).astype(bf16)
        d_keys = dot(d_scores, queries[a])
        return query_grad + dot(keys, d_scores, TN), d_keys, d_values

    def add(key_start, count, d_keys, d_values):
        key_grad[pl.ds(key_start, count), :] += d_keys
        value_grad[pl.ds(key_start, count), :] += d_values

    def body(j, grads):
        key_start = pl.multiple_of(j * step, step)
        found = [update(a, grads[a], key_start, step, False) for a in range(parts)]
        add(key_start, step, sum(f[1] for f in found), sum(f[2] for f in found))
        return tuple(f[0] for f in found)

    grads = list(
        lax.fori_loop(0, start // step, body, (jnp.zeros((HD, sub), f32),) * parts)
    )
    for a in range(parts):
        todo = [(pl.multiple_of(start + a * sub, sub), sub, True)]
        if a > 0:
            todo.append((start, a * sub, False))
        if a < parts - 1:
            todo.append((pl.multiple_of(start + (a + 1) * sub, BLOCK), BLOCK, True))
        for key_start, count, masked in todo:
            grads[a], d_keys, d_values = update(a, grads[a], key_start, count, masked)
            add(key_start, count, d_keys, d_values)

    def beyond(j, grad):
        key_start = pl.multiple_of(start + tile, BLOCK)
        grad, d_keys, d_values = update(parts - 1, grad, key_start, BLOCK, True)
        add(key_start, BLOCK, d_keys, d_values)
        return grad

    grads[-1] = lax.fori_loop(0, jnp.where(i < tiles - 1, 1, 0), beyond, grads[-1])
    query_grad = jnp.concatenate(grads, axis=1) * SCALE
    sum_ref[0, :, :1] += jnp.sum(query_grad, axis=1, keepdims=True)
    query_grad = query_grad.astype(bf16)
    for b in range(chunks):
        dm_ref[i * chunks + b, :HD] = query_grad[:, b * chunk : (b + 1) * chunk]

    @pl.when(turn == tiles - 1)
    def _():
        value_sum = jnp.zeros((HD, 1), f32)
        for c in range(dm_ref.shape[0]):
            rows = slice(c * chunk, (c + 1) * chunk)
            dm_ref[c, HD : 2 * HD] = (key_grad[rows, :].T * SCALE).astype(bf16)
            d_values = value_grad[rows, :].T
            dm_ref[c, 2 * HD :] = d_values.astype(bf16)
            value_sum += jnp.sum(d_values, axis=1, keepdims=True)
        sum_ref[0, :, 1:2] = value_sum


def attend_back(q, k, v, d_out, out, lse, blocks, head, chunk):
    count, width = q.shape
    seqs = count // SEQ_LEN
    tile, sub = 1024, 512
    tiles = SEQ_LEN // tile
    pairs = seqs * SEQ_LEN * SEQ_LEN * 5 // 8
    heads_spec = pl.BlockSpec(
        (tile // chunk, HD, chunk), lambda s, i: (s * tiles + tiles - 1 - i, 0, 0)
    )
    return pl.pallas_call(
        functools.partial(attend_back_kernel, head, tile, sub),
        grid=(seqs, tiles),
        in_specs=[
            pl.BlockSpec((1, 1, SEQ_LEN), lambda s, i: (s, 0, 0)),
            pl.BlockSpec((tile, width), lambda s, i: (s * tiles + tiles - 1 - i, 0)),
            pl.BlockSpec((SEQ_LEN, width), lambda s, i: (s, 0)),
            pl.BlockSpec((SEQ_LEN, width), lambda s, i: (s, 0)),
            heads_spec,
            heads_spec,
            pl.BlockSpec((1, 1, tile), lambda s, i: (s, 0, tiles - 1 - i)),
        ],
        out_specs=[
            pl.BlockSpec((SEQ_LEN // chunk, 3 * HD, chunk), lambda s, i: (s, 0, 0)),
            pl.BlockSpec((1, HD, 128), lambda s, i: (s, 0, 0)),
        ],
        out_shape=[
            jax.ShapeDtypeStruct((count // chunk, 3 * HD, chunk), bf16),
            jax.ShapeDtypeStruct((seqs, HD, 128), f32),
        ],
        scratch_shapes=[pltpu.VMEM((SEQ_LEN, HD), f32)] * 2,
        compiler_params=params(),
        cost_estimate=cost(40 * pairs * HD, 8 * count * width * 2, pairs),
        name="attend_back",
    )(blocks, q, k, v, d_out, out, lse)


def stack_heads(refs):
    return jnp.concatenate([ref[s] for s in range(refs[0].shape[0]) for ref in refs], axis=0)


def project_out_kernel(heads_here, *refs):
    heads, (tok_ref, w_ref, b_ref, g_ref, s_ref, resid_ref, ffn_ref) = (
        refs[:heads_here],
        refs[heads_here:],
    )
    rows, cols, depth, width = w_ref.shape
    heads_all = flip(stack_heads(heads))
    for r in range(rows):
        here = slice(r * width, (r + 1) * width)
        branch = dot(heads_all, w_ref[r].reshape(cols * depth, width))
        resid_ref[:, here] = (
            tok_ref[:, here].astype(f32) + branch + b_ref[:, here].astype(f32)
        )
    xhat, _ = moments(resid_ref[...])
    ffn_ref[...] = (xhat * g_ref[...].astype(f32) + s_ref[...].astype(f32)).astype(bf16)


def project_out(heads, tokens, w, b_out, gain, shift):
    count, depth = tokens.shape
    tile = 256
    block = pl.BlockSpec((tile, depth), lambda i: (i, 0))
    vec = whole((1, depth))
    return pl.pallas_call(
        functools.partial(project_out_kernel, len(heads)),
        grid=(count // tile,),
        in_specs=[pl.BlockSpec((h.shape[0], HD, tile), lambda i: (0, 0, i)) for h in heads]
        + [block, whole(w.shape), vec, vec, vec],
        out_specs=[block, block],
        out_shape=[
            jax.ShapeDtypeStruct((count, depth), f32),
            jax.ShapeDtypeStruct((count, depth), bf16),
        ],
        compiler_params=params(),
        cost_estimate=cost(2 * count * depth * depth, 2 * depth * depth + 8 * count * depth),
        name="project_out",
    )(*heads, tokens, w, b_out, gain, shift)


GELU_A = 0.7978845608028654
GELU_B = 0.044715


def feed_kernel(
    heads_here, x_ref, g_ref, resid_ref, up_ref, down_ref, bup_ref, bdown_ref, gain_ref, out_w_ref,
    gup_ref, gdown_ref, gbup_ref, output_ref, dres_ref, drl_ref, sums_ref, *rest,
):
    d_heads, (out_acc, norm_acc) = rest[:heads_here], rest[heads_here:]
    step = pl.program_id(0)
    rows, width = up_ref.shape[0], up_ref.shape[3]

    @pl.when(step == 0)
    def _():
        out_acc[...] = jnp.zeros_like(out_acc)
        norm_acc[...] = jnp.zeros_like(norm_acc)

    def part(r):
        return slice(r * width, (r + 1) * width)

    up = bup_ref[0].astype(f32)
    d_hidden = 0.0
    for r in range(rows):
        up = up + dot(x_ref[:, part(r)], up_ref[r, 0], NT)
        d_hidden = d_hidden + dot(g_ref[:, part(r)], down_ref[r, 0], NT)
    square = up * up
    bent = jnp.tanh(GELU_A * up * (1.0 + GELU_B * square))
    half = 0.5 + 0.5 * bent
    hidden = (up * half).astype(bf16)
    slope = half + (0.5 * GELU_A) * up * (1.0 - bent * bent) * (1.0 + (3.0 * GELU_B) * square)
    d_up = d_hidden * slope
    gbup_ref[0] = jnp.sum(d_up, axis=0, keepdims=True)
    d_up = d_up.astype(bf16)
    for r in range(rows):
        out_acc[:, part(r)] += dot(hidden, down_ref[r, 0])
        norm_acc[:, part(r)] += dot(d_up, up_ref[r, 0])
    grad_down = dot(hidden, g_ref[...], TN)
    grad_up = dot(d_up, x_ref[...], TN)
    for r in range(rows):
        gdown_ref[0, r, 0] = grad_down[:, part(r)].astype(bf16)
        gup_ref[0, r, 0] = grad_up[:, part(r)].astype(bf16)

    @pl.when(step == pl.num_programs(0) - 1)
    def _():
        resid = resid_ref[...]
        output_ref[...] = (resid + out_acc[...] + bdown_ref[...].astype(f32)).astype(bf16)
        xhat, inv = moments(resid)
        d_norm = norm_acc[...]
        grad = g_ref[...].astype(f32)
        d_resid = grad + norm_back(xhat, inv, d_norm * gain_ref[...].astype(f32))
        dres_ref[...] = d_resid
        low = d_resid.astype(bf16)
        drl_ref[...] = low
        sums_ref[0:1] = jnp.sum(grad, axis=0, keepdims=True)
        sums_ref[1:2] = jnp.sum(d_norm * xhat, axis=0, keepdims=True)
        sums_ref[2:3] = jnp.sum(d_norm, axis=0, keepdims=True)
        sums_ref[3:4] = jnp.sum(d_resid, axis=0, keepdims=True)
        sums_ref[4:] = jnp.zeros((4, sums_ref.shape[1]), f32)
        cols, depth = out_w_ref.shape[1], out_w_ref.shape[2]
        found = 0.0
        for r in range(rows):
            found = found + dot(out_w_ref[r].reshape(cols * depth, width), low[:, part(r)], NT)
        found = found.astype(bf16)
        for c in range(cols):
            for h, ref in enumerate(d_heads):
                ref[c] = found[c * depth + h * HD : c * depth + (h + 1) * HD]


def feed_forward(x, grad, resid, w_up, w_down, b_up, b_down, gain, w_out):
    count, depth = x.shape
    rows, cols, units, width = w_up.shape
    heads_here = w_out.shape[2] // HD
    weight = pl.BlockSpec((rows, 1, units, width), lambda c: (0, c, 0, 0))
    grad_spec = pl.BlockSpec(
        (1, rows, 1, units, width), lambda c: (lax.rem(c, 2), 0, c // 2, 0, 0)
    )
    grad_shape = jax.ShapeDtypeStruct((2, rows, cols // 2, units, width), bf16)
    low, high = whole((count, depth)), whole((count, depth))
    vec = whole((1, depth))
    heads_shape = (cols, HD, count)
    return pl.pallas_call(
        functools.partial(feed_kernel, heads_here),
        grid=(cols,),
        in_specs=[
            low, low, high, weight, weight,
            pl.BlockSpec((1, 1, units), lambda c: (c, 0, 0)), vec, vec, whole(w_out.shape),
        ],
        out_specs=[
            grad_spec, grad_spec, pl.BlockSpec((1, 1, units), lambda c: (c, 0, 0)),
            low, high, low, whole((8, depth)),
        ] + [whole(heads_shape)] * heads_here,
        out_shape=[
            grad_shape, grad_shape, jax.ShapeDtypeStruct((cols, 1, units), f32),
            jax.ShapeDtypeStruct((count, depth), bf16),
            jax.ShapeDtypeStruct((count, depth), f32),
            jax.ShapeDtypeStruct((count, depth), bf16),
            jax.ShapeDtypeStruct((8, depth), f32),
        ] + [jax.ShapeDtypeStruct(heads_shape, bf16)] * heads_here,
        scratch_shapes=[pltpu.VMEM((count, depth), f32)] * 2,
        compiler_params=params(),
        cost_estimate=cost(
            12 * count * depth * cols * units, 8 * depth * cols * units + 16 * count * depth
        ),
        name="feed_forward",
    )(x, grad, resid, w_up, w_down, b_up, b_down, gain, w_out)


def grad_out_kernel(heads_here, *refs):
    heads, (d_ref, out_ref) = refs[:heads_here], refs[heads_here:]
    cores, rows, chips, depth, width = out_ref.shape
    found = dot(stack_heads(heads), d_ref[...]).astype(bf16)
    for r in range(rows):
        for c in range(cores * chips):
            out_ref[c % 2, r, c // 2] = found[
                c * depth : (c + 1) * depth, r * width : (r + 1) * width
            ]


def grad_w_out(heads, d_resid, rows):
    count, depth = d_resid.shape
    cols = heads[0].shape[0]
    shape = (2, rows, cols // 2, depth // cols, depth // rows)
    return pl.pallas_call(
        functools.partial(grad_out_kernel, len(heads)),
        in_specs=[pl.BlockSpec(memory_space=pltpu.VMEM)] * (len(heads) + 1),
        out_specs=pl.BlockSpec(memory_space=pltpu.VMEM),
        out_shape=jax.ShapeDtypeStruct(shape, bf16),
        compiler_params=params(),
        cost_estimate=cost(2 * count * depth * depth, 2 * depth * depth + 4 * count * depth),
        name="grad_w_out",
    )(*heads, d_resid)


def grad_qkv_kernel(dm_ref, x_ref, out_ref, acc):
    step = pl.program_id(0)

    @pl.when(step == 0)
    def _():
        acc[...] = jnp.zeros_like(acc)

    acc[...] += dot(dm_ref[0], x_ref[0])

    @pl.when(step == pl.num_programs(0) - 1)
    def _():
        width = out_ref.shape[2]
        for r in range(out_ref.shape[0]):
            out_ref[r] = acc[:, r * width : (r + 1) * width].astype(bf16)


def grad_w_qkv(dm, x, rows):
    chunks, parts, count = dm.shape
    depth = x.shape[2]
    shape = (rows, parts, depth // rows)
    return pl.pallas_call(
        grad_qkv_kernel,
        grid=(chunks,),
        in_specs=[
            pl.BlockSpec((1, parts, count), lambda c: (c, 0, 0)),
            pl.BlockSpec((1, count, depth), lambda c: (c, 0, 0)),
        ],
        out_specs=whole(shape),
        out_shape=jax.ShapeDtypeStruct(shape, bf16),
        scratch_shapes=[pltpu.VMEM((parts, depth), f32)],
        compiler_params=params(),
        cost_estimate=cost(2 * chunks * count * parts * depth, 2 * chunks * count * depth),
        name="grad_w_qkv",
    )(dm, x)


def finish_kernel(heads_here, *refs):
    dms, (w_ref, tok_ref, dres_ref, gain_ref, out_ref, sums_ref, acc) = (
        refs[:heads_here],
        refs[heads_here:],
    )
    step = pl.program_id(0)
    rows, width = w_ref.shape[0], w_ref.shape[2]

    @pl.when(step == 0)
    def _():
        acc[...] = jnp.zeros_like(acc)

    d_mixed = flip(
        jnp.concatenate([dm[0, j * HD : (j + 1) * HD] for j in range(3) for dm in dms], axis=0)
    )
    for r in range(rows):
        acc[:, r * width : (r + 1) * width] += dot(d_mixed, w_ref[r, 0], NT)

    @pl.when(step == pl.num_programs(0) - 1)
    def _():
        xhat, inv = moments(tok_ref[...].astype(f32))
        d_norm = acc[...]
        out_ref[...] = dres_ref[...] + norm_back(xhat, inv, d_norm * gain_ref[...].astype(f32))
        sums_ref[0:1] = jnp.sum(d_norm * xhat, axis=0, keepdims=True)
        sums_ref[1:2] = jnp.sum(d_norm, axis=0, keepdims=True)


def finish(dms, w, tokens, d_resid, gain):
    count, depth = tokens.shape
    rows, cols, width, parts = w.shape
    block = whole((count, depth))
    return pl.pallas_call(
        functools.partial(finish_kernel, len(dms)),
        grid=(cols,),
        in_specs=[pl.BlockSpec((1, 3 * HD, count), lambda c: (c, 0, 0)) for _ in dms]
        + [
            pl.BlockSpec((rows, 1, width, parts), lambda c: (0, c, 0, 0)),
            block, block, whole((1, depth)),
        ],
        out_specs=[block, whole((2, depth))],
        out_shape=[
            jax.ShapeDtypeStruct((count, depth), f32),
            jax.ShapeDtypeStruct((2, depth), f32),
        ],
        scratch_shapes=[pltpu.VMEM((count, depth), f32)],
        compiler_params=params(),
        cost_estimate=cost(2 * count * depth * cols * parts, 2 * depth * cols * parts),
        name="finish",
    )(*dms, w, tokens, d_resid, gain)


def swap(x, axis, groups=None):
    return lax.all_to_all(x, axis, 0, 0, tiled=True, axis_index_groups=groups)


def total_of(x):
    return jnp.sum(x.astype(f32), axis=0)


def body(
    tokens, blocks, w_qkv, b_qv, w_out, b_out, w_up, b_up, w_down, b_down,
    gain1, shift1, gain2, shift2, grad_out,
):
    rows, cols = lax.axis_size("row"), lax.axis_size("col")
    chips = cols // 2
    pairs = [[2 * c, 2 * c + 1] for c in range(chips)]
    lines = [[2 * c + core for c in range(chips)] for core in range(2)]
    local_rows, depth = tokens.shape
    group_rows = local_rows * cols
    head_cols = w_qkv.shape[2]
    heads = range(head_cols // HD)
    units = w_up.shape[0]

    def vec(v):
        return v.reshape(1, -1)

    xhat, _ = moments(tokens.astype(f32))
    attn_input = (xhat * gain1.astype(f32) + shift1.astype(f32)).astype(bf16)
    w_qkv_flat = w_qkv.reshape(w_qkv.shape[0], 3 * head_cols)

    def gather_all(w):
        return lax.all_gather(w, ("row", "col"), axis=0, tiled=False).reshape(
            (rows, cols) + w.shape
        )

    out_weight, up_weight, down_weight, qkv_weight = (
        gather_all(w_out), gather_all(w_up), gather_all(w_down), gather_all(w_qkv_flat)
    )

    attn_rows, block_ids, up_bias, qkv_here = gather_inputs(
        attn_input, vec(blocks), vec(b_up), w_qkv_flat, rows, cols
    )
    block_ids = block_ids.reshape(group_rows // SEQ_LEN, 1, SEQ_LEN)
    q, k, v = project_qkv(attn_rows.reshape(group_rows, depth), qkv_here, b_qv)
    found = [attend(q, k, v, block_ids, h, local_rows) for h in heads]
    arrived = [swap(out, "col") for out, _ in found]
    resid, ffn_input = project_out(
        arrived, tokens, out_weight, vec(b_out), vec(gain2), vec(shift2)
    )
    grad_up, grad_down, grad_bup, output, d_resid, d_low, sums, *d_heads = feed_forward(
        ffn_input, grad_out, resid, up_weight, down_weight, up_bias, vec(b_down), vec(gain2),
        out_weight,
    )
    d_heads = [swap(d, "col") for d in d_heads]
    grad_wout = grad_w_out(arrived, d_low, rows)

    def reduce_weight(g):
        g = total_of(swap(g, "col", pairs)).astype(bf16)
        g = total_of(swap(g, "row")).astype(bf16)
        return total_of(swap(g, "col", lines))

    grad_wdown, grad_wup, grad_wout = (
        reduce_weight(grad_down), reduce_weight(grad_up), reduce_weight(grad_wout)
    )

    d_mixed, bias_sums = [], []
    for h in heads:
        dm, bias_sum = attend_back(
            q, k, v, d_heads[h], found[h][0], found[h][1], block_ids, h, local_rows
        )
        d_mixed.append(dm)
        bias_sums.append(jnp.sum(bias_sum[:, :, :2], axis=0))
    returned = [swap(dm, "col") for dm in d_mixed]
    grad_qkv = [total_of(swap(grad_w_qkv(dm, attn_rows, rows), "row")) for dm in d_mixed]
    grad_wqkv = jnp.stack(
        [g.reshape(3, HD, depth // rows) for g in grad_qkv], axis=1
    ).reshape(3 * head_cols, depth // rows)
    grad_wqkv = grad_wqkv.T.reshape(depth // rows, 3, head_cols)
    grad_tokens, norm_sums = finish(returned, qkv_weight, tokens, d_resid, vec(gain1))

    world = rows * cols
    early = jnp.concatenate([grad_bup.reshape(-1), sums[:4].reshape(-1)]).reshape(world, -1)
    early = total_of(swap(early, ("row", "col")))
    early = swap(jnp.broadcast_to(early, (world,) + early.shape), ("row", "col")).reshape(-1)
    hidden_units = units * cols
    grad_bup = lax.dynamic_slice_in_dim(early, lax.axis_index("col") * units, units)
    grad_bdown, grad_gain2, grad_shift2, grad_bout = early[hidden_units:].reshape(4, depth)
    late = jnp.broadcast_to(norm_sums, (world,) + norm_sums.shape)
    grad_gain1, grad_shift1 = total_of(swap(late, ("row", "col")))
    bias = jnp.concatenate(bias_sums, axis=0).T
    grad_bqv = total_of(swap(jnp.broadcast_to(bias, (rows,) + bias.shape), "row"))
    return (
        output, grad_tokens, grad_wqkv, grad_bqv, grad_wout, grad_bout, grad_wup, grad_bup,
        grad_wdown, grad_bdown, grad_gain1, grad_shift1, grad_gain2, grad_shift2,
    )


def solution(mesh):
    tokens, weight, whole_vec = P(("row", "col"), None), P("col", "row"), P()
    qkv, bias_qv = P("row", None, "col"), P(None, "col")
    return jax.shard_map(
        body,
        mesh=mesh,
        in_specs=(
            tokens, P(("row", "col")), qkv, bias_qv, weight, whole_vec, weight, P("col"), weight,
            whole_vec, whole_vec, whole_vec, whole_vec, whole_vec, tokens,
        ),
        out_specs=(
            tokens, tokens, qkv, bias_qv, weight, whole_vec, weight, P("col"), weight,
            whole_vec, whole_vec, whole_vec, whole_vec, whole_vec,
        ),
        check_vma=False,
    )
```

time: 1740 us -> 794 us (0.46)
  waiting for transfers between devices: 918 us -> 175 us
  matrix products: 421 us -> 0 us
  Pallas kernels: 0 us -> 315 us
  other arithmetic: 186 us -> 35.1 us
  starting transfers between devices: 1.24 us -> 72.7 us
  local copies, waits for them, and re-layouts: 82.3 us -> 16.2 us
  blocking collectives: 85.9 us -> 152 us
  loops' own time: 26.9 us -> 0 us
    reduce_scatter x8 -> x0, waiting for transfers between devices: 611 us -> none  [the longest x2 263 us: sum_tokens(): lax.psum_scatter(term_fn(jnp.int32(0), lax.axis_size('col') * local_rows)...]
    dot_general x68 -> x0, matrix products: 421 us -> none  [the longest x8 101 us: backward_block(): jnp.einsum('qhd,khd->hqk', dout_part, value_seq, preferred_element_type=f32)]
    pallas_call x0 -> x12, Pallas kernels: none -> 315 us  [the longest x1 107 us: gather_inputs(): pl.pallas_call(functools.partial(gather_kernel, rows, cols), out_shape=[j...]
    all_gather x6 -> x4, waiting for transfers between devices: 305 us -> 21.6 us  [gather_all(): lax.all_gather(w, ('row', 'col'), axis=0, tiled=False)]
    all_to_all x0 -> x5, blocking collectives: none -> 152 us  [swap(): return lax.all_to_all(x, axis, 0, 0, tiled=True, axis_index_groups=groups)]
    all_to_all x0 -> x16, waiting for transfers between devices: none -> 151 us  [swap(): return lax.all_to_all(x, axis, 0, 0, tiled=True, axis_index_groups=groups)]
    convert_element_type x21 -> x3, other arithmetic: 107 us -> 2.8 us  [body(): attn_input = (xhat * gain1.astype(f32) + shift1.astype(f32)).astype(bf16)]
    all_to_all x0 -> x16, starting transfers between devices: none -> 72.6 us  [swap(): return lax.all_to_all(x, axis, 0, 0, tiled=True, axis_index_groups=groups)]
  transfers between devices with their start and end apart: 14 -> 20, of which waited for: 12 -> 11; matrix products, arithmetic and copies ran while one was open for 5% -> 6% of each run, Pallas kernels for 0% -> 35%
where the time goes in v1:
time: 794 us; the launch traced here: 780 us
  Pallas kernels  315 us (40%)
  waiting for transfers between devices  175 us (22%)
  blocking collectives  152 us (19%)
  starting transfers between devices  72.7 us (9%)
  other arithmetic  35.1 us (4%)
  local copies, waits for them, and re-layouts  16.2 us (2%)
  between operations  14.2 us (2%)
    all_to_all x5, blocking collectives, swap(): return lax.all_to_all(x, axis, 0, 0, tiled=True, axis_index_groups=groups)  152 us
    all_to_all x16, waiting for transfers between devices, swap(): return lax.all_to_all(x, axis, 0, 0, tiled=True, axis_index_groups=groups)  151 us
    pallas_call x1, Pallas kernels, gather_inputs(): pl.pallas_call(functools.partial(gather_kernel, rows, cols), out_shape=[j...  107 us
    all_to_all x16, starting transfers between devices, swap(): return lax.all_to_all(x, axis, 0, 0, tiled=True, axis_index_groups=groups)  72.6 us
    pallas_call x2, Pallas kernels, attend_back(): pl.pallas_call(functools.partial(attend_back_kernel, head, tile, sub), gr...  71.2 us
    pallas_call x2, Pallas kernels, attend(): pl.pallas_call(functools.partial(attend_kernel, head, tile), grid=(seqs,...  46.5 us
    pallas_call x1, Pallas kernels, feed_forward(): pl.pallas_call(functools.partial(feed_kernel, heads_here), grid=(cols,),...  42.3 us
    reduce_sum x14, other arithmetic, total_of(): return jnp.sum(x.astype(f32), axis=0)  30.8 us
  transfers between devices with their start and end apart: 20, of which 11 were waited for; matrix products, arithmetic and copies ran while one was open for 6% of the time, Pallas kernels for 35%

profile of v1, /device:TPU:0, one launch (start us, length us, event | category | flops | bytes accessed | tf_op | source)
XLA Modules:
  0.0 780.3 jit_solution(10516934406989981109)
XLA Ops:
  16.0 107.2 %gather_inputs.1 = (bf16[8,512,1024]{2,1,0:T(8,128)(2,1)}, s32[8,1,512]{2,1,0:T(1,128)}, bf16[8,1,512]{2,1,0:T(2,128)(2,1)}, bf16[1024,384]{1,0:T(8,128)(2,1)}) custom-call(bf16[512,1024]{1,0:T(8,128)(2,1)} %fusion.5.x_ref, s32[1,512]{1,0:T(1,128)} %bitcast.49, bf16[1,512]{1,0:T(2,128)(2,1)} %reshape.131.bup_ref, bf16[256,384]{1,0:T(8,128)(2,1)} %copy.54.w_ref), custom_call_target="tpu_custom_call" | custom-call | tf_op jit(solution)/shard_map/gather_inputs/pallas_call | solution.py:185
  123.2 8.7 %project_qkv.1 = (bf16[4096,128]{1,0:T(8,128)(2,1)}, bf16[4096,128]{1,0:T(8,128)(2,1)}, bf16[4096,128]{1,0:T(8,128)(2,1)}) custom-call(bf16[4096,1024]{1,0:T(8,128)(2,1)} %bitcast.29, bf16[1024,384]{1,0:T(8,128)(2,1)} %get-tuple-element.44.w_ref, bf16[2,128]{1,0:T(2,128)(2,1)} %b_ref.1), custom_call_target="tpu_custom_call" | custom-call | flops 3221225472 | bytes 11534336 | tf_op jit(solution)/shard_map/project_qkv/pallas_call | solution.py:219
  131.9 23.4 %attend.3 = (bf16[8,64,512]{2,1,0:T(8,128)(2,1)}, f32[1,1,4096]{2,1,0:T(1,128)}) custom-call(s32[1,1,4096]{2,1,0:T(1,128)} %bitcast.52, bf16[4096,128]{1,0:T(8,128)(2,1)} %get-tuple-element.45.q_ref, bf16[4096,128]{1,0:T(8,128)(2,1)} %get-tuple-element.46.k_ref, bf16[4096,128]{1,0:T(8,128)(2,1)} %get-tuple-element.47.v_ref), custom_call_target="tpu_custom_call" | custom-call | flops 10737418240 | bytes 4194304 | tf_op jit(solution)/shard_map/attend/pallas_call | solution.py:286
  159.1 23.1 %attend.2 = (bf16[8,64,512]{2,1,0:T(8,128)(2,1)}, f32[1,1,4096]{2,1,0:T(1,128)}) custom-call(s32[1,1,4096]{2,1,0:T(1,128)} %bitcast.53, bf16[4096,128]{1,0:T(8,128)(2,1)} %get-tuple-element.45.q_ref, bf16[4096,128]{1,0:T(8,128)(2,1)} %get-tuple-element.46.k_ref, bf16[4096,128]{1,0:T(8,128)(2,1)} %get-tuple-element.47.v_ref), custom_call_target="tpu_custom_call" | custom-call | flops 10737418240 | bytes 4194304 | tf_op jit(solution)/shard_map/attend/pallas_call | solution.py:286
  182.2 15.7 %all-to-all-start = ((bf16[8,64,512]{2,1,0:T(8,128)(2,1)}), bf16[8,64,512]{2,1,0:T(8,128)(2,1)S(1)}, u32[]{:S(2)}, u32[]{:S(2)}) async-start(bf16[8,64,512]{2,1,0:T(8,128)(2,1)} %get-tuple-element.48.o_ref), calls=%async_computation | async-start | bytes 1048576 | tf_op jit(solution)/shard_map/all_to_all | solution.py:702
  200.3 15.7 %all-to-all-done.refs_0_ = bf16[8,64,512]{2,1,0:T(8,128)(2,1)S(1)} async-done(((bf16[8,64,512]{2,1,0:T(8,128)(2,1)}), bf16[8,64,512]{2,1,0:T(8,128)(2,1)S(1)}, u32[]{:S(2)}, u32[]{:S(2)}) %all-to-all-start) | async-done | bytes 524320 | tf_op jit(solution)/shard_map/all_to_all | solution.py:702
  221.8 21.6 %all-gather.14.cloned.1.call-done = bf16[16384,256]{1,0:T(8,128)(2,1)} async-done(((bf16[512,256]{1,0:T(8,128)(2,1)}), bf16[16384,256]{1,0:T(8,128)(2,1)}) %all-gather.14.cloned.1.call-update) | async-done | bytes 8388624 | tf_op jit(solution)/shard_map/all_gather | solution.py:731
  243.4 42.3 %feed_forward.1 = (bf16[2,4,4,512,256]{4,3,2,1,0:T(8,128)(2,1)}, bf16[2,4,4,512,256]{4,3,2,1,0:T(8,128)(2,1)}, f32[8,1,512]{2,1,0:T(1,128)}, bf16[512,1024]{1,0:...) custom-call(bf16[512,1024]{1,0:T(8,128)(2,1)} %get-tuple-element.50., ...), custom_call_target="tpu_custom_call" | custom-call | flops 25769803776 | bytes 41943040 | tf_op jit(solution)/shard_map/feed_forward/pallas_call | solution.py:561
  304.9 18.5 %all_to_all.110 = bf16[2,4,4,512,256]{4,3,2,1,0:T(8,128)(2,1)} all-to-all(bf16[2,4,4,512,256]{4,3,2,1,0:T(8,128)(2,1)} %get-tuple-element.68), channel_id=1, replica_groups={{0,1},{2,3},{4,5},{6,7},{8,9},{10,11},{12,13},{14,15},{16,17},{18,19},{..., dimensions={0} | all-to-all | bytes 16777216 | tf_op jit(solution)/shard_map/all_to_all | solution.py:702
  323.4 18.5 %all_to_all.111 = bf16[2,4,4,512,256]{4,3,2,1,0:T(8,128)(2,1)} all-to-all(bf16[2,4,4,512,256]{4,3,2,1,0:T(8,128)(2,1)} %get-tuple-element.67), channel_id=1, replica_groups={{0,1},{2,3},{4,5},{6,7},{8,9},{10,11},{12,13},{14,15},{16,17},{18,19},{..., dimensions={0} | all-to-all | bytes 16777216 | tf_op jit(solution)/shard_map/all_to_all | solution.py:702
  341.9 9.8 %all_to_all.112 = f32[32,1,256]{2,1,0:T(1,128)S(1)} all-to-all(f32[32,1,256]{2,1,0:T(1,128)S(1)} %broadcast_in_dim.14), channel_id=1, replica_groups=mesh['row'=4,'col'=8] {'row','col'}, dimensions={0} | all-to-all | bytes 65536 | tf_op jit(solution)/shard_map/all_to_all | solution.py:702
  356.8 13.6 %all-to-all-done.4.do_ref = bf16[8,64,512]{2,1,0:T(8,128)(2,1)S(1)} async-done(((bf16[8,64,512]{2,1,0:T(8,128)(2,1)}), bf16[8,64,512]{2,1,0:T(8,128)(2,1)S(1)}, u32[]{:S(2)}, u32[]{:S(2)}) %all-to-all-start.4) | async-done | bytes 524320 | tf_op jit(solution)/shard_map/all_to_all | solution.py:702
  374.0 36.1 %attend_back.3 = (bf16[8,192,512]{2,1,0:T(8,128)(2,1)}, f32[1,64,128]{2,1,0:T(8,128)}) custom-call(s32[1,1,4096]{2,1,0:T(1,128)} %bitcast.54, bf16[4096,128]{1,0:T(8,128)(2,1)} %get-tuple-element.45.q_ref, bf16[4096,128]{1,0:T(8,128)(2,1)} %get-tuple-element.46.k_ref, bf16[4096,128]{1,0:T(8,128)(2,1)} %get-tuple-element.47.v_ref, ...), custom_call_target="tpu_custom_call" | custom-call | flops 26843545600 | bytes 8388608 | tf_op jit(solution)/shard_map/attend_back/pallas_call | solution.py:412
  414.1 35.0 %attend_back.2 = (bf16[8,192,512]{2,1,0:T(8,128)(2,1)}, f32[1,64,128]{2,1,0:T(8,128)}) custom-call(s32[1,1,4096]{2,1,0:T(1,128)} %bitcast.55, bf16[4096,128]{1,0:T(8,128)(2,1)} %get-tuple-element.45.q_ref, bf16[4096,128]{1,0:T(8,128)(2,1)} %get-tuple-element.46.k_ref, bf16[4096,128]{1,0:T(8,128)(2,1)} %get-tuple-element.47.v_ref, ...), custom_call_target="tpu_custom_call" | custom-call | flops 26843545600 | bytes 8388608 | tf_op jit(solution)/shard_map/attend_back/pallas_call | solution.py:412
  477.2 8.3 %grad_w_qkv.3 = bf16[4,192,256]{2,1,0:T(8,128)(2,1)} custom-call(bf16[8,192,512]{2,1,0:T(8,128)(2,1)} %get-tuple-element.59.dm_ref, bf16[8,512,1024]{2,1,0:T(8,128)(2,1)} %get-tuple-element.43.x_ref), custom_call_target="tpu_custom_call" | custom-call | flops 1610612736 | bytes 8388608 | tf_op jit(solution)/shard_map/grad_w_qkv/pallas_call | solution.py:634
  489.7 8.3 %reduce_sum.188 = bf16[4,4,512,256]{3,2,1,0:T(8,128)(2,1)} reduce(bf16[2,4,4,512,256]{4,3,2,1,0:T(8,128)(2,1)} %all_to_all.110, bf16[]{:T(256)} %constant.20.clone.1), dimensions={0}, to_apply=%region_12.0 | reduce | flops 2097152 | bytes 12582914 | tf_op jit(solution)/shard_map/reduce_sum | solution.py:706
  498.0 63.0 %all_to_all.113 = bf16[4,4,512,256]{3,2,1,0:T(8,128)(2,1)} all-to-all(bf16[4,4,512,256]{3,2,1,0:T(8,128)(2,1)} %reduce_sum.188), channel_id=1, replica_groups=mesh['row'=4,'col'=8] {'row'}, dimensions={0} | all-to-all | bytes 8388608 | tf_op jit(solution)/shard_map/all_to_all | solution.py:702
  561.0 42.5 %all_to_all.114.refs_1_ = bf16[8,192,512]{2,1,0:T(8,128)(2,1)} all-to-all(bf16[8,192,512]{2,1,0:T(8,128)(2,1)S(1)} %copy-done.1), channel_id=1, replica_groups=mesh['row'=4,'col'=8] {'col'}, dimensions={0} | all-to-all | bytes 3145728 | tf_op jit(solution)/shard_map/all_to_all | solution.py:702
  607.3 8.3 %reduce_sum.185 = bf16[4,4,512,256]{3,2,1,0:T(8,128)(2,1)} reduce(bf16[2,4,4,512,256]{4,3,2,1,0:T(8,128)(2,1)} %all_to_all.111, bf16[]{:T(256)} %constant.20.clone.1), dimensions={0}, to_apply=%region_9.0 | reduce | flops 2097152 | bytes 12582914 | tf_op jit(solution)/shard_map/reduce_sum | solution.py:706
  615.6 29.4 %all-to-all-done.3.refs_0_ = bf16[8,192,512]{2,1,0:T(8,128)(2,1)S(1)} async-done(((bf16[8,192,512]{2,1,0:T(8,128)(2,1)}), bf16[8,192,512]{2,1,0:T(8,128)(2,1)S(1)}, u32[]{:S(2)}, u32[]{:S(2)}) %all-to-all-start.3) | async-done | bytes 1572896 | tf_op jit(solution)/shard_map/all_to_all | solution.py:702
  651.7 13.3 %finish.1 = (f32[512,1024]{1,0:T(8,128)}, f32[2,1024]{1,0:T(2,128)}) custom-call(bf16[8,192,512]{2,1,0:T(8,128)(2,1)} %copy-done.2, bf16[8,192,512]{2,1,0:T(8,128)(2,1)} %all_to_all.114.refs_1_, bf16[4,8,256,384]{3,2,1,0:T(8,128)(2,1)} %bitcast.30, bf16[512,1024]{1,0:T(8,128)(2,1)} %refs_3_.1, f32[512,1024]{1,0:T(8,128)} %get-tuple-element.60.refs_4_, ...), custom_call_target="tpu_custom_call" | custom-call | flops 3221225472 | bytes 6291456 | tf_op jit(solution)/shard_map/finish/pallas_call | solution.py:681
  665.0 33.6 %all-to-all-done.15 = bf16[4,4,512,256]{3,2,1,0:T(8,128)(2,1)} async-done(((bf16[4,4,512,256]{3,2,1,0:T(8,128)(2,1)}), bf16[4,4,512,256]{3,2,1,0:T(8,128)(2,1)}, u32[]{:S(2)}, u32[]{:S(2)}) %all-to-all-start.15) | async-done | bytes 4194336 | tf_op jit(solution)/shard_map/all_to_all | solution.py:702
  721.0 22.4 %all-to-all-done.19 = bf16[4,512,256]{2,1,0:T(8,128)(2,1)S(1)} async-done(((bf16[4,512,256]{2,1,0:T(8,128)(2,1)}), bf16[4,512,256]{2,1,0:T(8,128)(2,1)S(1)}, u32[]{:S(2)}, u32[]{:S(2)}) %all-to-all-start.19) | async-done | bytes 1048608 | tf_op jit(solution)/shard_map/all_to_all | solution.py:702
  752.2 20.5 %all-to-all-done.16 = bf16[4,512,256]{2,1,0:T(8,128)(2,1)S(1)} async-done(((bf16[4,512,256]{2,1,0:T(8,128)(2,1)}), bf16[4,512,256]{2,1,0:T(8,128)(2,1)S(1)}, u32[]{:S(2)}, u32[]{:S(2)}) %all-to-all-start.16) | async-done | bytes 1048608 | tf_op jit(solution)/shard_map/all_to_all | solution.py:702
  (110 shorter events, 127.2 us)
Async XLA Ops:
  7.2 208.8 %all-gather.10.cloned.1.call-start = ((), (), s32[]{:S(2)}) async-start(), calls=%async_computation.22 | async-start | bytes 2162688 | tf_op jit(solution)/shard_map/all_gather | solution.py:731
  7.9 213.9 %all-gather.12.cloned.1.call-start = ((), (), s32[]{:S(2)}) async-start(), calls=%async_computation.23 | async-start | bytes 8650752 | tf_op jit(solution)/shard_map/all_gather | solution.py:731
  8.7 234.7 %all-gather.14.cloned.1.call-start = ((), (), s32[]{:S(2)}) async-start(), calls=%async_computation.24 | async-start | bytes 8650752 | tf_op jit(solution)/shard_map/all_gather | solution.py:731
  155.3 26.9 %all-to-all-start.1 = ((bf16[8,64,512]{2,1,0:T(8,128)(2,1)}), bf16[8,64,512]{2,1,0:T(8,128)(2,1)S(1)}, u32[]{:S(2)}, u32[]{:S(2)}) async-start(bf16[8,64,512]{2,1,0:T(8,128)(2,1)} %get-tuple-element.49.o_ref), calls=%async_computation.1 | async-start | bytes 1048576 | tf_op jit(solution)/shard_map/all_to_all | solution.py:702
  159.0 39.4 %copy-start.10 = (bf16[1024]{0:T(1024)(128)(2,1)S(1)}, bf16[1024]{0:T(1024)(128)(2,1)}, u32[]{:S(2)}) copy-start(bf16[1024]{0:T(1024)(128)(2,1)} %param.20) | copy-start | bytes 6148
  159.1 40.0 %copy-start.11 = (bf16[1024]{0:T(1024)(128)(2,1)S(1)}, bf16[1024]{0:T(1024)(128)(2,1)}, u32[]{:S(2)}) copy-start(bf16[1024]{0:T(1024)(128)(2,1)} %param.28) | copy-start | bytes 6148
  159.1 40.6 %copy-start.12 = (bf16[1024]{0:T(1024)(128)(2,1)S(1)}, bf16[1024]{0:T(1024)(128)(2,1)}, u32[]{:S(2)}) copy-start(bf16[1024]{0:T(1024)(128)(2,1)} %param.24) | copy-start | bytes 6148
  182.2 33.8 %all-to-all-start = ((bf16[8,64,512]{2,1,0:T(8,128)(2,1)}), bf16[8,64,512]{2,1,0:T(8,128)(2,1)S(1)}, u32[]{:S(2)}, u32[]{:S(2)}) async-start(bf16[8,64,512]{2,1,0:T(8,128)(2,1)} %get-tuple-element.48.o_ref), calls=%async_computation | async-start | bytes 1048576 | tf_op jit(solution)/shard_map/all_to_all | solution.py:702
  287.9 10.4 %all-to-all-start.12 = ((f32[32,1,256]{2,1,0:T(1,128)}), f32[32,1,256]{2,1,0:T(1,128)S(1)}, u32[]{:S(2)}, u32[]{:S(2)}) async-start(f32[32,1,256]{2,1,0:T(1,128)} %all_to_all.79), calls=%async_computation.12 | async-start | bytes 65536 | tf_op jit(solution)/shard_map/all_to_all | solution.py:702
  298.3 6.6 all-to-all-start.9
  351.7 18.8 %all-to-all-start.4 = ((bf16[8,64,512]{2,1,0:T(8,128)(2,1)}), bf16[8,64,512]{2,1,0:T(8,128)(2,1)S(1)}, u32[]{:S(2)}, u32[]{:S(2)}) async-start(bf16[8,64,512]{2,1,0:T(8,128)(2,1)} %get-tuple-element.57), calls=%async_computation.4 | async-start | bytes 1048576 | tf_op jit(solution)/shard_map/all_to_all | solution.py:702
  370.5 39.7 %all-to-all-start.2 = ((bf16[8,64,512]{2,1,0:T(8,128)(2,1)}), bf16[8,64,512]{2,1,0:T(8,128)(2,1)S(1)}, u32[]{:S(2)}, u32[]{:S(2)}) async-start(bf16[8,64,512]{2,1,0:T(8,128)(2,1)} %get-tuple-element.54), calls=%async_computation.2 | async-start | bytes 1048576 | tf_op jit(solution)/shard_map/all_to_all | solution.py:702
  410.2 40.0 %all-to-all-start.10 = ((bf16[4,4,128,256]{3,2,1,0:T(8,128)(2,1)}), bf16[4,4,128,256]{3,2,1,0:T(8,128)(2,1)S(1)}, u32[]{:S(2)}, u32[]{:S(2)}) async-start(bf16[4,4,128,256]{3,2,1,0:T(8,128)(2,1)} %reduce_sum.181), calls=%async_computation.10 | async-start | bytes 2097152 | tf_op jit(solution)/shard_map/all_to_all | solution.py:702
  450.8 8.9 %all-to-all-start.8 = ((f32[4,2,128]{2,1,0:T(2,128)}), f32[4,2,128]{2,1,0:T(2,128)S(1)}, u32[]{:S(2)}, u32[]{:S(2)}) async-start(f32[4,2,128]{2,1,0:T(2,128)} %broadcast_in_dim.6), calls=%async_computation.8 | async-start | bytes 8192 | tf_op jit(solution)/shard_map/all_to_all | solution.py:702
  459.6 14.1 %all-to-all-start.11 = ((bf16[4,128,256]{2,1,0:T(8,128)(2,1)}), bf16[4,128,256]{2,1,0:T(8,128)(2,1)S(1)}, u32[]{:S(2)}, u32[]{:S(2)}) async-start(bf16[4,128,256]{2,1,0:T(8,128)(2,1)} %reduce_sum.182), calls=%async_computation.11 | async-start | bytes 524288 | tf_op jit(solution)/shard_map/all_to_all | solution.py:702
  464.6 187.1 %all-gather.8.cloned.1.call-start = ((), (), s32[]{:S(2)}) async-start(), calls=%async_computation.21 | async-start | bytes 6488064 | tf_op jit(solution)/shard_map/all_gather | solution.py:731
  473.7 11.8 %all-to-all-start.6 = ((bf16[4,192,256]{2,1,0:T(8,128)(2,1)}), bf16[4,192,256]{2,1,0:T(8,128)(2,1)S(1)}, u32[]{:S(2)}, u32[]{:S(2)}) async-start(bf16[4,192,256]{2,1,0:T(8,128)(2,1)} %grad_w_qkv.2), calls=%async_computation.6 | async-start | bytes 786432 | tf_op jit(solution)/shard_map/all_to_all | solution.py:702
  485.5 12.5 %all-to-all-start.7 = ((bf16[4,192,256]{2,1,0:T(8,128)(2,1)}), bf16[4,192,256]{2,1,0:T(8,128)(2,1)S(1)}, u32[]{:S(2)}, u32[]{:S(2)}) async-start(bf16[4,192,256]{2,1,0:T(8,128)(2,1)} %grad_w_qkv.3), calls=%async_computation.7 | async-start | bytes 786432 | tf_op jit(solution)/shard_map/all_to_all | solution.py:702
  498.0 63.0 %copy-start.1 = (bf16[8,192,512]{2,1,0:T(8,128)(2,1)S(1)}, bf16[8,192,512]{2,1,0:T(8,128)(2,1)}, u32[]{:S(2)}) copy-start(bf16[8,192,512]{2,1,0:T(8,128)(2,1)} %get-tuple-element.59.dm_ref) | copy-start | bytes 4718596
  603.5 41.5 %all-to-all-start.3 = ((bf16[8,192,512]{2,1,0:T(8,128)(2,1)}), bf16[8,192,512]{2,1,0:T(8,128)(2,1)S(1)}, u32[]{:S(2)}, u32[]{:S(2)}) async-start(bf16[8,192,512]{2,1,0:T(8,128)(2,1)} %get-tuple-element.56.dm_ref), calls=%async_computation.3 | async-start | bytes 3145728 | tf_op jit(solution)/shard_map/all_to_all | solution.py:702
  646.2 52.3 %all-to-all-start.15 = ((bf16[4,4,512,256]{3,2,1,0:T(8,128)(2,1)}), bf16[4,4,512,256]{3,2,1,0:T(8,128)(2,1)}, u32[]{:S(2)}, u32[]{:S(2)}) async-start(bf16[4,4,512,256]{3,2,1,0:T(8,128)(2,1)} %reduce_sum.185), calls=%async_computation.15 | async-start | bytes 8388608 | tf_op jit(solution)/shard_map/all_to_all | solution.py:702
  700.0 13.3 %all-to-all-start.20 = ((f32[32,2,1024]{2,1,0:T(2,128)}), f32[32,2,1024]{2,1,0:T(2,128)S(1)}, u32[]{:S(2)}, u32[]{:S(2)}) async-start(f32[32,2,1024]{2,1,0:T(2,128)} %broadcast_in_dim.15), calls=%async_computation.20 | async-start | bytes 524288 | tf_op jit(solution)/shard_map/all_to_all | solution.py:702
  713.4 30.0 %all-to-all-start.19 = ((bf16[4,512,256]{2,1,0:T(8,128)(2,1)}), bf16[4,512,256]{2,1,0:T(8,128)(2,1)S(1)}, u32[]{:S(2)}, u32[]{:S(2)}) async-start(bf16[4,512,256]{2,1,0:T(8,128)(2,1)} %reduce_sum.189), calls=%async_computation.19 | async-start | bytes 2097152 | tf_op jit(solution)/shard_map/all_to_all | solution.py:702
  743.4 29.2 %all-to-all-start.16 = ((bf16[4,512,256]{2,1,0:T(8,128)(2,1)}), bf16[4,512,256]{2,1,0:T(8,128)(2,1)S(1)}, u32[]{:S(2)}, u32[]{:S(2)}) async-start(bf16[4,512,256]{2,1,0:T(8,128)(2,1)} %reduce_sum.186), calls=%async_computation.16 | async-start | bytes 2097152 | tf_op jit(solution)/shard_map/all_to_all | solution.py:702
  (9 other events, 159.3 us)
Sparse Core Ops, SparseCore 0:
  11.0 61.3 all-gather.9
  75.4 79.1 all-gather.11
  157.6 85.8 all-gather.13
  468.7 92.5 all-gather.7

commit v2 on v1

v2 whole, which is shorter than its diff:
```python
import functools

import jax
import jax.numpy as jnp
from jax import lax
from jax.experimental import pallas as pl
from jax.experimental.pallas import tpu as pltpu
from jax.sharding import PartitionSpec as P

HD = 64
SEQ_LEN = 4096
BLOCK = 256
EPS = 1e-05
SCALE = HD ** (-0.5)
SCALE2 = SCALE * 1.4426950408889634
MASKED = -1e30
ONES = 16
MESH = pl.DeviceIdType.MESH
VMEM_LIMIT = 60 << 20

f32 = jnp.float32
bf16 = jnp.bfloat16

NN = (((1,), (0,)), ((), ()))
NT = (((1,), (1,)), ((), ()))
TN = (((0,), (0,)), ((), ()))


def dot(a, b, dims=NN):
    return lax.dot_general(a, b, dims, preferred_element_type=f32)


def flip(x):
    return x.astype(f32).T.astype(bf16)


def params(**more):
    return pltpu.CompilerParams(vmem_limit_bytes=VMEM_LIMIT, **more)


def cost(flops, nbytes, transcendentals=0):
    return pl.CostEstimate(flops=flops, bytes_accessed=nbytes, transcendentals=transcendentals)


def whole(shape):
    return pl.BlockSpec(shape, lambda *_: (0,) * len(shape))


def moments(v):
    center = jnp.mean(v, axis=-1, keepdims=True)
    centered = v - center
    spread = jnp.mean(centered * centered, axis=-1, keepdims=True)
    inv = lax.rsqrt(spread + EPS)
    return centered * inv, inv


def norm_back(xhat, inv, e):
    return inv * (
        e - jnp.mean(e, axis=-1, keepdims=True) - xhat * jnp.mean(e * xhat, axis=-1, keepdims=True)
    )


def gather_kernel(
    rows, cols, x_ref, blk_ref, bup_ref, w_ref, xo_ref, blko_ref, bupo_ref, wo_ref,
    send_x, recv_x, send_s, recv_s, send_w, recv_w, local,
):
    row, me = lax.axis_index("row"), lax.axis_index("col")
    chips = cols // 2
    chip, lane = me // 2, lax.rem(me, 2)
    mate = chip * 2 + 1 - lane
    depth = w_ref.shape[0]

    barrier = pltpu.get_barrier_semaphore()
    for k in range(1, cols):
        pl.semaphore_signal(
            barrier, inc=1, device_id=(row, lax.rem(me + k, cols)), device_id_type=MESH
        )
    for k in range(1, rows):
        pl.semaphore_signal(
            barrier, inc=1, device_id=(lax.rem(row + k, rows), me), device_id_type=MESH
        )
    pl.semaphore_wait(barrier, rows + cols - 2)

    def chunk(src, owner, target, route, at):
        return pltpu.make_async_remote_copy(
            src_ref=src,
            dst_ref=xo_ref.at[owner],
            send_sem=send_x.at[route, at],
            recv_sem=recv_x.at[route, at],
            device_id=(row, target),
            device_id_type=MESH,
        )

    @pl.when(chip + 1 < chips)
    def _():
        chunk(x_ref, me, me + 2, 0, chip).start()

    @pl.when(chip > 0)
    def _():
        chunk(x_ref, me, me - 2, 1, chip).start()

    chunk(x_ref, me, mate, 2, chip).start()
    weights = []
    where = pl.ds(pl.multiple_of(row * depth, depth), depth)
    for k in range(1, rows):
        copy = pltpu.make_async_remote_copy(
            src_ref=w_ref,
            dst_ref=wo_ref.at[where],
            send_sem=send_w.at[k],
            recv_sem=recv_w.at[k],
            device_id=(lax.rem(row + k, rows), me),
            device_id_type=MESH,
        )
        copy.start()
        weights.append(copy)
    small = []
    for k in range(1, cols):
        for at, (src, dst) in enumerate(((blk_ref, blko_ref), (bup_ref, bupo_ref))):
            copy = pltpu.make_async_remote_copy(
                src_ref=src,
                dst_ref=dst.at[me],
                send_sem=send_s.at[at, k],
                recv_sem=recv_s.at[at, k],
                device_id=(row, lax.rem(me + k, cols)),
                device_id_type=MESH,
            )
            copy.start()
            small.append(copy)
    own = [
        pltpu.make_async_copy(x_ref, xo_ref.at[me], local.at[0]),
        pltpu.make_async_copy(blk_ref, blko_ref.at[me], local.at[1]),
        pltpu.make_async_copy(bup_ref, bupo_ref.at[me], local.at[2]),
        pltpu.make_async_copy(w_ref, wo_ref.at[where], local.at[3]),
    ]
    for copy in own:
        copy.start()

    for hop in range(1, chips):
        below, above = chip - hop, chip + hop

        @pl.when(below >= 0)
        def _():
            owner = below * 2 + lane
            chunk(xo_ref.at[owner], owner, me, 0, below).wait_recv()

            @pl.when(chip + 1 < chips)
            def _():
                chunk(xo_ref.at[owner], owner, me + 2, 0, below).start()

            chunk(xo_ref.at[owner], owner, mate, 2, below).start()

        @pl.when(above < chips)
        def _():
            owner = above * 2 + lane
            chunk(xo_ref.at[owner], owner, me, 1, above).wait_recv()

            @pl.when(chip > 0)
            def _():
                chunk(xo_ref.at[owner], owner, me - 2, 1, above).start()

            chunk(xo_ref.at[owner], owner, mate, 2, above).start()

    for at in range(chips):
        copy = chunk(x_ref, me, mate, 2, at)
        copy.wait_recv()
        copy.wait_send()

        @pl.when((at <= chip) & (chip + 1 < chips))
        def _():
            chunk(x_ref, me, me, 0, at).wait_send()

        @pl.when((at >= chip) & (chip > 0))
        def _():
            chunk(x_ref, me, me, 1, at).wait_send()

    for copy in weights + small + own:
        copy.wait()


def gather_inputs(x, blocks, b_up, w_qkv, rows, cols):
    any_space = pl.BlockSpec(memory_space=pl.ANY)
    vmem = pl.BlockSpec(memory_space=pltpu.VMEM)
    chips = cols // 2
    dma = pltpu.SemaphoreType.DMA
    return pl.pallas_call(
        functools.partial(gather_kernel, rows, cols),
        out_shape=[
            jax.ShapeDtypeStruct((cols,) + x.shape, x.dtype),
            jax.ShapeDtypeStruct((cols,) + blocks.shape, blocks.dtype),
            jax.ShapeDtypeStruct((cols,) + b_up.shape, b_up.dtype),
            jax.ShapeDtypeStruct((rows * w_qkv.shape[0], w_qkv.shape[1]), w_qkv.dtype),
        ],
        in_specs=[vmem] * 4,
        out_specs=[any_space] * 4,
        scratch_shapes=[
            dma((3, chips)), dma((3, chips)),
            dma((2, cols)), dma((2, cols)),
            dma((rows,)), dma((rows,)), dma((4,)),
        ],
        compiler_params=pltpu.CompilerParams(collective_id=0, has_side_effects=True),
        name="gather_inputs",
    )(x, blocks, b_up, w_qkv)


def qkv_kernel(x_ref, w_ref, b_ref, q_ref, k_ref, v_ref):
    mixed = dot(x_ref[...], w_ref[...])
    heads = q_ref.shape[0]
    width = heads * HD
    bias = b_ref[...].astype(f32)
    for h in range(heads):
        lanes = slice(h * HD, (h + 1) * HD)
        q_ref[h] = (mixed[:, :width][:, lanes] + bias[0:1, lanes]).astype(bf16)
        k_ref[h] = mixed[:, width : 2 * width][:, lanes].astype(bf16)
        v_ref[h] = (mixed[:, 2 * width :][:, lanes] + bias[1:2, lanes]).astype(bf16)


def project_qkv(x, w, bias):
    count, depth = x.shape
    width = w.shape[1] // 3
    heads = width // HD
    tile = min(1024, count)
    out = pl.BlockSpec((heads, tile, HD), lambda i: (0, i, 0))
    return pl.pallas_call(
        qkv_kernel,
        grid=(count // tile,),
        in_specs=[pl.BlockSpec((tile, depth), lambda i: (i, 0)), whole(w.shape), whole(bias.shape)],
        out_specs=[out] * 3,
        out_shape=[jax.ShapeDtypeStruct((heads, count, HD), bf16)] * 3,
        compiler_params=params(),
        cost_estimate=cost(2 * count * depth * 3 * width, 2 * count * (depth + 3 * width)),
        name="project_qkv",
    )(x, w, bias)


def tile_mask(blk_ref, key_start, count, query_blocks):
    key_blocks = jnp.broadcast_to(blk_ref[0, :, pl.ds(key_start, count)], (128, count)).T[:, :1]
    return query_blocks >= key_blocks


def attend_kernel(step, blk_ref, q_ref, k_ref, v_ref, o_ref, lse_ref, values):
    i = pl.program_id(2)
    tile = q_ref.shape[1]
    chunks, _, chunk = o_ref.shape

    @pl.when(i == 0)
    def _():
        values[:HD, :] = flip(v_ref[0])
        values[HD:, :] = jnp.ones((ONES, values.shape[1]), bf16)

    start = pl.multiple_of(i * tile, tile)
    query = q_ref[0]
    query_blocks = blk_ref[0, :, pl.ds(start, tile)]

    def update(state, key_start, count, masked):
        total, top = state
        scores = dot(k_ref[0, pl.ds(key_start, count), :], query, NT)
        if masked:
            mask = tile_mask(blk_ref, key_start, count, query_blocks)
            scores = jnp.where(mask, scores, MASKED)
        higher = jnp.maximum(top, jnp.max(scores, axis=0, keepdims=True) * SCALE2)
        probs = jnp.exp2(scores * SCALE2 - higher)
        part = dot(values[:, pl.ds(key_start, count)], probs.astype(bf16))
        return total * jnp.exp2(top - higher) + part, higher

    state = (jnp.zeros((HD + ONES, tile), f32), jnp.full((1, tile), MASKED, f32))
    state = lax.fori_loop(
        0, start // step, lambda j, s: update(s, pl.multiple_of(j * step, step), step, False), state
    )
    state = update(state, start, tile, True)
    total, top = lax.fori_loop(
        0,
        jnp.where(i < pl.num_programs(2) - 1, 1, 0),
        lambda j, s: update(s, pl.multiple_of(start + tile, BLOCK), BLOCK, True),
        state,
    )
    mass = total[HD : HD + 1]
    out = (total[:HD] / mass).astype(bf16)
    for b in range(chunks):
        o_ref[b] = out[:, b * chunk : (b + 1) * chunk]
    lse_ref[0, 0] = top + jnp.log2(mass)


def attend(q, k, v, blocks, chunk):
    heads, count, _ = q.shape
    seqs = count // SEQ_LEN
    tile = 1024
    tiles = SEQ_LEN // tile
    pairs = heads * seqs * SEQ_LEN * SEQ_LEN * 5 // 8
    keys = pl.BlockSpec((1, SEQ_LEN, HD), lambda h, s, i: (h, s, 0))
    return pl.pallas_call(
        functools.partial(attend_kernel, tile),
        grid=(heads, seqs, tiles),
        in_specs=[
            pl.BlockSpec((1, 1, SEQ_LEN), lambda h, s, i: (s, 0, 0)),
            pl.BlockSpec((1, tile, HD), lambda h, s, i: (h, s * tiles + i, 0)),
            keys,
            keys,
        ],
        out_specs=[
            pl.BlockSpec((tile // chunk, HD, chunk), lambda h, s, i: (s * tiles + i, h, 0)),
            pl.BlockSpec((1, 1, 1, tile), lambda h, s, i: (h, s, 0, i)),
        ],
        out_shape=[
            jax.ShapeDtypeStruct((count // chunk, heads * HD, chunk), bf16),
            jax.ShapeDtypeStruct((heads, seqs, 1, SEQ_LEN), f32),
        ],
        scratch_shapes=[pltpu.VMEM((HD + ONES, SEQ_LEN), bf16)],
        compiler_params=params(),
        cost_estimate=cost(16 * pairs * HD, 8 * heads * count * HD, pairs),
        name="attend",
    )(blocks, q, k, v)


def place():
    return lax.axis_index("row"), lax.axis_index("col")


def greet(rows, cols):
    row, col = place()
    barrier = pltpu.get_barrier_semaphore()

    def to_col(k, carry):
        pl.semaphore_signal(
            barrier, inc=1, device_id=(row, lax.rem(col + k, cols)), device_id_type=MESH
        )
        return carry

    def to_row(k, carry):
        pl.semaphore_signal(
            barrier, inc=1, device_id=(lax.rem(row + k, rows), col), device_id_type=MESH
        )
        return carry

    lax.fori_loop(1, cols, to_col, 0)
    lax.fori_loop(1, rows, to_row, 0)
    pl.semaphore_wait(barrier, rows + cols - 2)


def remote(src, dst, send, recv, device):
    return pltpu.make_async_remote_copy(
        src_ref=src, dst_ref=dst, send_sem=send, recv_sem=recv, device_id=device, device_id_type=MESH
    )


def each(count, act):
    def turn(k, carry):
        act(k)
        return carry

    lax.fori_loop(1, count, turn, 0)


class Exchange:
    def __init__(self, count, here, slot, to, out, into, send, recv):
        self.count, self.here, self.slot, self.to = count, here, slot, to
        self.out, self.into, self.send, self.recv = out, into, send, recv

    def copy(self, k):
        at = self.slot(k)
        return remote(
            self.out(at), self.into(self.here), self.send.at[k], self.recv.at[self.here], self.to(k)
        )

    def arrival(self, k):
        at = self.slot(k)
        return remote(self.out(at), self.into(at), self.send.at[k], self.recv.at[at], self.to(k))

    def start(self):
        each(self.count, lambda k: self.copy(k).start())

    def wait_recv(self):
        each(self.count, lambda k: self.arrival(k).wait_recv())

    def wait_send(self):
        each(self.count, lambda k: self.copy(k).wait_send())


def over_row(rows, out, into, send, recv):
    row, col = place()
    slot = lambda k: lax.rem(row + k, rows)
    return Exchange(rows, row, slot, lambda k: (slot(k), col), out, into, send, recv)


def over_col(cols, out, into, send, recv):
    row, col = place()
    slot = lambda k: lax.rem(col + k, cols)
    return Exchange(cols, col, slot, lambda k: (row, slot(k)), out, into, send, recv)


def over_line(chips, out, into, send, recv):
    row, col = place()
    chip, lane = col // 2, lax.rem(col, 2)
    slot = lambda k: lax.rem(chip + k, chips)
    return Exchange(chips, chip, slot, lambda k: (row, slot(k) * 2 + lane), out, into, send, recv)


def mate():
    row, col = place()
    return (row, col // 2 * 2 + 1 - lax.rem(col, 2))


GELU_A = 0.7978845608028654
GELU_B = 0.044715


def middle_kernel(
    rows, cols,
    heads_ref, tok_ref, g_ref, up_ref, down_ref, bup_ref, bout_ref, gain_ref, shift_ref, bdown_ref,
    wout_ref, wq_ref,
    gup_ref, gdown_ref, gout_ref, gbup_ref, output_ref, dres_ref, sums_ref, dheads_ref, wqo_ref,
    x, heads_all, resid, out_acc, norm_acc, hiddens, d_ups, low, d_send,
    mine, other, out_mine, out_other,
    send_d, recv_d, send_p, recv_p, send_o, recv_o, send_z, recv_z, send_r, recv_r, send_m, recv_m,
    local,
):
    step = pl.program_id(0)
    chips = cols // 2
    row, col = place()
    chip, lane = col // 2, lax.rem(col, 2)
    width = up_ref.shape[3]
    depth = wout_ref.shape[2]

    def part(r):
        return slice(r * width, (r + 1) * width)

    z_stage = over_line(
        chips, lambda at: wq_ref, lambda at: wqo_ref.at[lane, row, at], send_z, recv_z
    )

    def r_stage(c):
        return over_row(
            rows,
            lambda at: wqo_ref.at[lane, row, c],
            lambda at: wqo_ref.at[lane, at, c],
            send_r.at[c],
            recv_r.at[c],
        )

    m_stage = remote(wqo_ref.at[lane], wqo_ref.at[lane], send_m, recv_m, mate())
    m_arrival = remote(wqo_ref.at[1 - lane], wqo_ref.at[1 - lane], send_m, recv_m, mate())
    own_wq = pltpu.make_async_copy(wq_ref, wqo_ref.at[lane, row, chip], local.at[0])
    d_stage = over_col(
        cols, lambda at: d_send.at[at], lambda at: dheads_ref.at[at], send_d, recv_d
    )
    own_d = pltpu.make_async_copy(d_send.at[col], dheads_ref.at[col], local.at[1])

    def pair(at, which):
        return remote(
            mine.at[which, at], other.at[which, at], send_p.at[which, at], recv_p.at[which, at],
            mate(),
        )

    pair_out = remote(out_mine, out_other, send_o, recv_o, mate())

    @pl.when(step == 0)
    def _():
        greet(rows, cols)
        own_wq.start()
        z_stage.start()
        for s in range(cols):
            heads_all[s * depth : (s + 1) * depth] = heads_ref[s]
        stacked = flip(heads_all[...])
        for r in range(rows):
            branch = dot(stacked, wout_ref[r].reshape(cols * depth, width))
            resid[:, part(r)] = (
                tok_ref[:, part(r)].astype(f32) + branch + bout_ref[:, part(r)].astype(f32)
            )
        xhat, _ = moments(resid[...])
        x[...] = (xhat * gain_ref[...].astype(f32) + shift_ref[...].astype(f32)).astype(bf16)
        out_acc[...] = jnp.zeros_like(out_acc)
        norm_acc[...] = jnp.zeros_like(norm_acc)

    @pl.when(step == 1)
    def _():
        own_wq.wait()
        z_stage.wait_recv()
        for c in range(chips):
            r_stage(c).start()

    @pl.when(step < cols)
    def _():
        up = bup_ref[0].astype(f32)
        d_hidden = 0.0
        for r in range(rows):
            up = up + dot(x[:, part(r)], up_ref[r, 0], NT)
            d_hidden = d_hidden + dot(g_ref[:, part(r)], down_ref[r, 0], NT)
        square = up * up
        bent = jnp.tanh(GELU_A * up * (1.0 + GELU_B * square))
        half = 0.5 + 0.5 * bent
        hidden = (up * half).astype(bf16)
        slope = half + (0.5 * GELU_A) * up * (1.0 - bent * bent) * (1.0 + (3.0 * GELU_B) * square)
        d_up = d_hidden * slope
        gbup_ref[0] = jnp.sum(d_up, axis=0, keepdims=True)
        d_up = d_up.astype(bf16)
        hiddens[step] = hidden
        d_ups[step] = d_up
        for r in range(rows):
            out_acc[:, part(r)] += dot(hidden, down_ref[r, 0])
            norm_acc[:, part(r)] += dot(d_up, up_ref[r, 0])

    @pl.when(step == cols - 1)
    def _():
        output_ref[...] = (resid[...] + out_acc[...] + bdown_ref[...].astype(f32)).astype(bf16)
        xhat, inv = moments(resid[...])
        d_norm = norm_acc[...]
        grad = g_ref[...].astype(f32)
        d_resid = grad + norm_back(xhat, inv, d_norm * gain_ref[...].astype(f32))
        dres_ref[...] = d_resid
        low[...] = d_resid.astype(bf16)
        sums_ref[0:1] = jnp.sum(grad, axis=0, keepdims=True)
        sums_ref[1:2] = jnp.sum(d_norm * xhat, axis=0, keepdims=True)
        sums_ref[2:3] = jnp.sum(d_norm, axis=0, keepdims=True)
        sums_ref[3:4] = jnp.sum(d_resid, axis=0, keepdims=True)
        sums_ref[4:] = jnp.zeros((4, sums_ref.shape[1]), f32)
        for c in range(cols):
            found = 0.0
            for r in range(rows):
                found = found + dot(wout_ref[r, c], low[:, part(r)], NT)
            d_send[c] = found.astype(bf16)
        own_d.start()
        d_stage.start()
        found = dot(heads_all[...], low[...])
        for c in range(chips):
            first = found[2 * c * depth : (2 * c + 1) * depth]
            second = found[(2 * c + 1) * depth : (2 * c + 2) * depth]
            out_mine[c] = jnp.where(lane == 0, second, first).astype(bf16)
            kept = jnp.where(lane == 0, first, second)
            for r in range(rows):
                out_acc[c * depth : (c + 1) * depth, part(r)] = kept[:, part(r)]
        pair_out.start()

    at = step - cols

    @pl.when((at >= 0) & (at < chips))
    def _():
        c = at * 2 + 1 - lane
        mine[0, at] = dot(hiddens[c], g_ref[...], TN).astype(bf16)
        pair(at, 0).start()
        mine[1, at] = dot(d_ups[c], x[...], TN).astype(bf16)
        pair(at, 1).start()

    @pl.when(at == 0)
    def _():
        for c in range(chips):
            r_stage(c).wait_recv()
        m_stage.start()

    @pl.when(at >= chips)
    def _():
        k = at - chips
        c = k * 2 + lane
        grad_down = dot(hiddens[c], g_ref[...], TN)
        pair(k, 0).wait_recv()
        grad_down = (grad_down + other[0, k].astype(f32)).astype(bf16)
        grad_up = dot(d_ups[c], x[...], TN)
        pair(k, 1).wait_recv()
        grad_up = (grad_up + other[1, k].astype(f32)).astype(bf16)
        for r in range(rows):
            gdown_ref[r, 0] = grad_down[:, part(r)]
            gup_ref[r, 0] = grad_up[:, part(r)]

    @pl.when(step == 2 * cols - 1)
    def _():
        pair_out.wait_recv()
        for c in range(chips):
            for r in range(rows):
                kept = out_acc[c * depth : (c + 1) * depth, part(r)]
                gout_ref[r, c] = (kept + out_other[c, :, part(r)].astype(f32)).astype(bf16)
        d_stage.wait_recv()
        m_arrival.wait_recv()
        pair_out.wait_send()
        for k in range(chips):
            pair(k, 0).wait_send()
            pair(k, 1).wait_send()
            r_stage(k).wait_send()
        z_stage.wait_send()
        d_stage.wait_send()
        m_stage.wait_send()
        own_d.wait()


def middle(heads, tokens, grad, w_up, w_down, b_up, b_out, gain, shift, b_down, w_out, w_qkv):
    count, depth = tokens.shape
    rows, cols, units, width = w_up.shape
    chips = cols // 2
    head_cols = w_out.shape[2]
    any_space = pl.BlockSpec(memory_space=pl.ANY)
    weight = pl.BlockSpec(
        (rows, 1, units, width), lambda s: (0, jnp.minimum(s, cols - 1), 0, 0)
    )
    grad_spec = pl.BlockSpec(
        (rows, 1, units, width), lambda s: (0, jnp.maximum(s - cols - chips, 0), 0, 0)
    )
    grad_shape = jax.ShapeDtypeStruct((rows, chips, units, width), bf16)
    bias = pl.BlockSpec((1, 1, units), lambda s: (jnp.minimum(s, cols - 1), 0, 0))
    block, vec = whole((count, depth)), whole((1, depth))
    dma = pltpu.SemaphoreType.DMA
    vmem = pltpu.VMEM
    return pl.pallas_call(
        functools.partial(middle_kernel, rows, cols),
        grid=(2 * cols,),
        in_specs=[
            whole(heads.shape), block, block, weight, weight, bias, vec, vec, vec, vec,
            whole(w_out.shape), any_space,
        ],
        out_specs=[
            grad_spec, grad_spec, whole((rows, chips, head_cols, width)), bias, block, block,
            whole((8, depth)), any_space, any_space,
        ],
        out_shape=[
            grad_shape, grad_shape,
            jax.ShapeDtypeStruct((rows, chips, head_cols, width), bf16),
            jax.ShapeDtypeStruct((cols, 1, units), f32),
            jax.ShapeDtypeStruct((count, depth), bf16),
            jax.ShapeDtypeStruct((count, depth), f32),
            jax.ShapeDtypeStruct((8, depth), f32),
            jax.ShapeDtypeStruct((cols, head_cols, count), bf16),
            jax.ShapeDtypeStruct((2, rows, chips) + w_qkv.shape, bf16),
        ],
        scratch_shapes=[
            vmem((count, depth), bf16), vmem((depth, count), bf16),
            vmem((count, depth), f32), vmem((count, depth), f32), vmem((count, depth), f32),
            vmem((cols, count, units), bf16), vmem((cols, count, units), bf16),
            vmem((count, depth), bf16), vmem((cols, head_cols, count), bf16),
            vmem((2, chips, units, depth), bf16), vmem((2, chips, units, depth), bf16),
            vmem((chips, head_cols, depth), bf16), vmem((chips, head_cols, depth), bf16),
            dma((cols,)), dma((cols,)), dma((2, chips)), dma((2, chips)), dma, dma,
            dma((chips,)), dma((chips,)), dma((chips, rows)), dma((chips, rows)), dma, dma,
            dma((2,)),
        ],
        compiler_params=pltpu.CompilerParams(
            vmem_limit_bytes=63 << 20, collective_id=1, has_side_effects=True
        ),
        cost_estimate=cost(
            12 * count * depth * cols * units, 8 * depth * cols * units + 16 * count * depth
        ),
        name="middle",
    )(heads, tokens, grad, w_up, w_down, b_up, b_out, gain, shift, b_down, w_out, w_qkv)


def back_kernel(
    rows, cols, heads, seqs, tiles, sub,
    blk_ref, q_ref, k_ref, v_ref, do_ref, o_ref, lse_ref, x_ref, w_ref, tok_ref, dres_ref, gain_ref,
    gup_ref, gdown_ref, gout_ref, early_ref,
    dtok_ref, wup_ref, wdown_ref, wout_ref, wqkv_ref, all_ref, bias_ref,
    d_mixed, d_arrived, key_grad, value_grad, bias_sum, qkv_acc, qkv_send, qkv_recv, norm_acc,
    up_recv, down_recv, out_recv, up_send, down_send, out_send, up_line, down_line, out_line,
    small, small_core, small_row, small_line, bias_send, bias_recv,
    send_r, recv_r, send_z, recv_z, send_d, recv_d, send_q, recv_q, send_b, recv_b,
    send_s0, recv_s0, send_s1, recv_s1, send_s2, recv_s2, local,
):
    step = pl.program_id(0)
    chips = cols // 2
    row, col = place()
    chip, lane = col // 2, lax.rem(col, 2)
    work = heads * seqs * tiles
    last = work + 2 * cols - 1
    head = step // (seqs * tiles)
    seq = lax.rem(step // tiles, seqs)
    turn = lax.rem(step, tiles)
    i = tiles - 1 - turn
    tile = q_ref.shape[1]
    chunks, _, chunk = do_ref.shape
    chunks_seq = SEQ_LEN // chunk
    parts = tile // sub
    steps = tile
    start = pl.multiple_of(i * tile, tile)

    given = (gdown_ref, gup_ref, gout_ref)
    by_row = (down_recv, up_recv, out_recv)
    to_line = (down_send, up_send, out_send)
    by_line = (down_line, up_line, out_line)
    results = (wdown_ref, wup_ref, wout_ref)

    def row_stage(n):
        return over_row(
            rows, lambda at: given[n].at[at], lambda at: by_row[n].at[at], send_r.at[n],
            recv_r.at[n],
        )

    def own_row(n):
        return pltpu.make_async_copy(given[n].at[row], by_row[n].at[row], local.at[n])

    def line_stage(n):
        return over_line(
            chips, lambda at: to_line[n].at[at], lambda at: by_line[n].at[at], send_z.at[n],
            recv_z.at[n],
        )

    def add_rows(n):
        own_row(n).wait()
        row_stage(n).wait_recv()

        def one(c, carry):
            total = by_row[n][0, c].astype(f32)
            for r in range(1, rows):
                total = total + by_row[n][r, c].astype(f32)
            to_line[n][c] = total.astype(bf16)
            return carry

        lax.fori_loop(0, chips, one, 0)
        by_line[n][chip] = to_line[n][chip]
        line_stage(n).start()

    def d_stage(h):
        return over_col(
            cols, lambda at: d_mixed.at[h, at], lambda at: d_arrived.at[h, at], send_d.at[h],
            recv_d.at[h],
        )

    def own_d(h):
        return pltpu.make_async_copy(d_mixed.at[h, col], d_arrived.at[h, col], local.at[3 + h])

    q_stage = over_row(
        rows, lambda at: qkv_send.at[at], lambda at: qkv_recv.at[at], send_q, recv_q
    )
    b_stage = over_row(rows, lambda at: bias_send, lambda at: bias_recv.at[at], send_b, recv_b)
    s_core = remote(small.at[0], small_core, send_s0, recv_s0, mate())
    s_row = over_row(
        rows, lambda at: small.at[1], lambda at: small_row.at[at], send_s1, recv_s1
    )
    s_line = over_line(
        chips, lambda at: small.at[2], lambda at: small_line.at[at], send_s2, recv_s2
    )

    @pl.when(step == 0)
    def _():
        greet(rows, cols)
        for n in range(3):
            own_row(n).start()
            row_stage(n).start()

    @pl.when(step == work // 2 + 1)
    def _():
        add_rows(0)

    @pl.when((step < work) & (turn == 0))
    def _():
        key_grad[...] = jnp.zeros_like(key_grad)
        value_grad[...] = jnp.zeros_like(value_grad)

    @pl.when((step < work) & (turn == 0) & (seq == 0))
    def _():
        bias_sum[head] = jnp.zeros((HD, 128), f32)

    @pl.when(step < work)
    def _():
        d_out = jnp.concatenate([do_ref[b] for b in range(chunks)], axis=1)
        out = jnp.concatenate([o_ref[b] for b in range(chunks)], axis=1)
        delta = jnp.sum(d_out.astype(f32) * out.astype(f32), axis=0, keepdims=True)
        lse = lse_ref[0, 0]

        def cut(x, a):
            return x[:, a * sub : (a + 1) * sub]

        queries = [q_ref[0, a * sub : (a + 1) * sub, :] for a in range(parts)]
        query_blocks = [
            blk_ref[0, :, pl.ds(pl.multiple_of(start + a * sub, sub), sub)] for a in range(parts)
        ]

        def update(a, query_grad, key_start, count, masked):
            keys = k_ref[0, pl.ds(key_start, count), :]
            values = v_ref[0, pl.ds(key_start, count), :]
            scores = dot(keys, queries[a], NT) * SCALE2 - cut(lse, a)
            if masked:
                mask = tile_mask(blk_ref, key_start, count, query_blocks[a])
                scores = jnp.where(mask, scores, MASKED)
            probs = jnp.exp2(scores)
            d_values = dot(probs.astype(bf16), cut(d_out, a), NT)
            d_scores = (probs * (dot(values, cut(d_out, a)) - cut(delta, a))).astype(bf16)
            d_keys = dot(d_scores, queries[a])
            return query_grad + dot(keys, d_scores, TN), d_keys, d_values

        def add(key_start, count, d_keys, d_values):
            key_grad[pl.ds(key_start, count), :] += d_keys
            value_grad[pl.ds(key_start, count), :] += d_values

        def sweep(j, grads):
            key_start = pl.multiple_of(j * steps, steps)
            found = [update(a, grads[a], key_start, steps, False) for a in range(parts)]
            add(key_start, steps, sum(f[1] for f in found), sum(f[2] for f in found))
            return tuple(f[0] for f in found)

        grads = list(
            lax.fori_loop(0, start // steps, sweep, (jnp.zeros((HD, sub), f32),) * parts)
        )
        for a in range(parts):
            todo = [(pl.multiple_of(start + a * sub, sub), sub, True)]
            if a > 0:
                todo.append((start, a * sub, False))
            if a < parts - 1:
                todo.append((pl.multiple_of(start + (a + 1) * sub, BLOCK), BLOCK, True))
            for key_start, count, masked in todo:
                grads[a], d_keys, d_values = update(a, grads[a], key_start, count, masked)
                add(key_start, count, d_keys, d_values)

        def beyond(j, grad):
            key_start = pl.multiple_of(start + tile, BLOCK)
            grad, d_keys, d_values = update(parts - 1, grad, key_start, BLOCK, True)
            add(key_start, BLOCK, d_keys, d_values)
            return grad

        grads[-1] = lax.fori_loop(0, jnp.where(i < tiles - 1, 1, 0), beyond, grads[-1])
        query_grad = jnp.concatenate(grads, axis=1) * SCALE
        bias_sum[head, :, :1] += jnp.sum(query_grad, axis=1, keepdims=True)
        query_grad = query_grad.astype(bf16)
        for b in range(chunks):
            d_mixed[head, seq * chunks_seq + i * chunks + b, :HD] = query_grad[
                :, b * chunk : (b + 1) * chunk
            ]

    @pl.when((step < work) & (turn == tiles - 1))
    def _():
        def one(c, value_sum):
            where = pl.ds(pl.multiple_of(c * chunk, chunk), chunk)
            at = seq * chunks_seq + c
            d_mixed[head, at, HD : 2 * HD] = (key_grad[where, :].T * SCALE).astype(bf16)
            d_values = value_grad[where, :].T
            d_mixed[head, at, 2 * HD :] = d_values.astype(bf16)
            return value_sum + jnp.sum(d_values, axis=1, keepdims=True)

        value_sum = lax.fori_loop(0, chunks_seq, one, jnp.zeros((HD, 1), f32))
        bias_sum[head, :, 1:2] += value_sum

    for h in range(heads):

        @pl.when(step == (h + 1) * seqs * tiles - 1)
        def _():
            own_d(h).start()
            d_stage(h).start()

    at = step - work

    @pl.when(at == 0)
    def _():
        qkv_acc[...] = jnp.zeros_like(qkv_acc)
        bias_send[...] = bias_sum[...]
        bias_recv[row] = bias_sum[...]
        b_stage.start()

    @pl.when((at >= 0) & (at < cols))
    def _():
        grads = jnp.concatenate([d_mixed[h, at] for h in range(heads)], axis=0)
        qkv_acc[...] += dot(grads, x_ref[0])

    @pl.when(at == cols - 1)
    def _():
        width = qkv_send.shape[2]
        for r in range(rows):
            qkv_send[r] = qkv_acc[:, r * width : (r + 1) * width].astype(bf16)
        qkv_recv[row] = qkv_send[row]
        q_stage.start()
        add_rows(1)
        add_rows(2)
        norm_acc[...] = jnp.zeros_like(norm_acc)
        for h in range(heads):
            own_d(h).wait()
            d_stage(h).wait_recv()

    @pl.when(at >= cols)
    def _():
        c = at - cols
        width = w_ref.shape[3]
        found = flip(
            jnp.concatenate(
                [
                    d_arrived[h, c, j * HD : (j + 1) * HD, :]
                    for j in range(3)
                    for h in range(heads)
                ],
                axis=0,
            )
        )
        for r in range(rows):
            norm_acc[:, r * width : (r + 1) * width] += dot(found, w_ref[0, r, 0], NT)

    @pl.when(step == last)
    def _():
        xhat, inv = moments(tok_ref[...].astype(f32))
        d_norm = norm_acc[...]
        late = early_ref.shape[0] - 2
        small[0] = early_ref[...]
        small[0, late : late + 1] = jnp.sum(d_norm * xhat, axis=0, keepdims=True)
        small[0, late + 1 : late + 2] = jnp.sum(d_norm, axis=0, keepdims=True)
        s_core.start()
        dtok_ref[...] = dres_ref[...] + norm_back(xhat, inv, d_norm * gain_ref[...].astype(f32))
        s_core.wait_recv()
        small[1] = small[0] + small_core[...]
        small_row[row] = small[1]
        s_row.start()
        b_stage.wait_recv()
        bias_ref[...] = sum(bias_recv[r] for r in range(1, rows)) + bias_recv[0]
        q_stage.wait_recv()
        total = qkv_recv[0].astype(f32)
        for r in range(1, rows):
            total = total + qkv_recv[r].astype(f32)
        wqkv_ref[...] = total
        s_row.wait_recv()
        small[2] = sum(small_row[r] for r in range(1, rows)) + small_row[0]
        small_line[chip] = small[2]
        s_line.start()
        for n in range(3):
            line_stage(n).wait_recv()
            total = by_line[n][0].astype(f32)
            for c in range(1, chips):
                total = total + by_line[n][c].astype(f32)
            results[n][...] = total
        s_line.wait_recv()
        all_ref[...] = sum(small_line[c] for c in range(1, chips)) + small_line[0]
        for n in range(3):
            row_stage(n).wait_send()
            line_stage(n).wait_send()
        for h in range(heads):
            d_stage(h).wait_send()
        q_stage.wait_send()
        b_stage.wait_send()
        s_core.wait_send()
        s_row.wait_send()
        s_line.wait_send()


def backward(
    blocks, q, k, v, d_heads, out, lse, x, w_qkv, tokens, d_resid, gain, grad_up, grad_down,
    grad_out, early,
):
    heads, total, _ = q.shape
    count, depth = tokens.shape
    rows, chips, units, width = grad_up.shape
    cols = 2 * chips
    head_cols = grad_out.shape[2]
    seqs = total // SEQ_LEN
    tile, sub = 1024, 512
    tiles = SEQ_LEN // tile
    work = heads * seqs * tiles
    pairs = heads * seqs * SEQ_LEN * SEQ_LEN * 5 // 8

    def unpack(s):
        s = jnp.minimum(s, work - 1)
        return s // (seqs * tiles), lax.rem(s // tiles, seqs), tiles - 1 - lax.rem(s, tiles)

    def queries_map(s):
        h, b, i = unpack(s)
        return (h, b * tiles + i, 0)

    def keys_map(s):
        h, b, _ = unpack(s)
        return (h, b, 0)

    def heads_map(s):
        h, b, i = unpack(s)
        return (b * tiles + i, h, 0)

    def lse_map(s):
        h, b, i = unpack(s)
        return (h, b, 0, i)

    def w_map(s):
        c = jnp.maximum(s - work - cols, 0)
        return (lax.rem(c, 2), 0, c // 2, 0, 0)

    keys = pl.BlockSpec((1, SEQ_LEN, HD), keys_map)
    heads_spec = pl.BlockSpec((tile // chunk_of(tokens), HD, count), heads_map)
    any_space = pl.BlockSpec(memory_space=pl.ANY)
    block = whole((count, depth))
    dma, vmem = pltpu.SemaphoreType.DMA, pltpu.VMEM
    parts = heads * 3 * HD
    shape = jax.ShapeDtypeStruct
    small = early.shape
    return pl.pallas_call(
        functools.partial(back_kernel, rows, cols, heads, seqs, tiles, sub),
        grid=(work + 2 * cols,),
        in_specs=[
            pl.BlockSpec((1, 1, SEQ_LEN), lambda s: (unpack(s)[1], 0, 0)),
            pl.BlockSpec((1, tile, HD), queries_map), keys, keys, heads_spec, heads_spec,
            pl.BlockSpec((1, 1, 1, tile), lse_map),
            pl.BlockSpec((1, count, depth), lambda s: (jnp.clip(s - work, 0, cols - 1), 0, 0)),
            pl.BlockSpec((1, rows, 1) + w_qkv.shape[3:], w_map),
            block, block, whole((1, depth)), any_space, any_space, any_space, whole(small),
        ],
        out_specs=[
            block, whole((units, width)), whole((units, width)), whole((head_cols, width)),
            whole((parts, width)), whole(small), whole((heads, HD, 128)),
        ],
        out_shape=[
            shape((count, depth), f32), shape((units, width), f32), shape((units, width), f32),
            shape((head_cols, width), f32), shape((parts, width), f32), shape(small, f32),
            shape((heads, HD, 128), f32),
        ],
        scratch_shapes=[
            vmem((heads, cols, 3 * HD, count), bf16), vmem((heads, cols, 3 * HD, count), bf16),
            vmem((SEQ_LEN, HD), f32), vmem((SEQ_LEN, HD), f32), vmem((heads, HD, 128), f32),
            vmem((parts, depth), f32), vmem((rows, parts, width), bf16),
            vmem((rows, parts, width), bf16), vmem((count, depth), f32),
            vmem((rows, chips, units, width), bf16), vmem((rows, chips, units, width), bf16),
            vmem((rows, chips, head_cols, width), bf16),
            vmem((chips, units, width), bf16), vmem((chips, units, width), bf16),
            vmem((chips, head_cols, width), bf16),
            vmem((chips, units, width), bf16), vmem((chips, units, width), bf16),
            vmem((chips, head_cols, width), bf16),
            vmem((3,) + small, f32), vmem(small, f32), vmem((rows,) + small, f32),
            vmem((chips,) + small, f32),
            vmem((heads, HD, 128), f32), vmem((rows, heads, HD, 128), f32),
            dma((3, rows)), dma((3, rows)), dma((3, chips)), dma((3, chips)),
            dma((heads, cols)), dma((heads, cols)), dma((rows,)), dma((rows,)),
            dma((rows,)), dma((rows,)), dma, dma, dma((rows,)), dma((rows,)),
            dma((chips,)), dma((chips,)), dma((3 + heads,)),
        ],
        compiler_params=pltpu.CompilerParams(
            vmem_limit_bytes=63 << 20, collective_id=2, has_side_effects=True
        ),
        cost_estimate=cost(40 * pairs * HD, 16 * heads * total * HD, pairs),
        name="backward",
    )(
        blocks, q, k, v, d_heads, out, lse, x, w_qkv, tokens, d_resid, gain, grad_up, grad_down,
        grad_out, early,
    )


def chunk_of(tokens):
    return tokens.shape[0]


def swap(x, axis, groups=None):
    return lax.all_to_all(x, axis, 0, 0, tiled=True, axis_index_groups=groups)


def body(
    tokens, blocks, w_qkv, b_qv, w_out, b_out, w_up, b_up, w_down, b_down,
    gain1, shift1, gain2, shift2, grad_out,
):
    rows, cols = lax.axis_size("row"), lax.axis_size("col")
    local_rows, depth = tokens.shape
    group_rows = local_rows * cols
    head_cols = w_qkv.shape[2]
    heads = head_cols // HD
    units = w_up.shape[0]

    def vec(v):
        return v.reshape(1, -1)

    xhat, _ = moments(tokens.astype(f32))
    attn_input = (xhat * gain1.astype(f32) + shift1.astype(f32)).astype(bf16)
    w_qkv_flat = w_qkv.reshape(w_qkv.shape[0], 3 * head_cols)

    def gather_all(w):
        return lax.all_gather(w, ("row", "col"), axis=0, tiled=False).reshape(
            (rows, cols) + w.shape
        )

    out_weight, up_weight, down_weight = gather_all(w_out), gather_all(w_up), gather_all(w_down)

    attn_rows, block_ids, up_bias, qkv_here = gather_inputs(
        attn_input, vec(blocks), vec(b_up), w_qkv_flat, rows, cols
    )
    block_ids = block_ids.reshape(group_rows // SEQ_LEN, 1, SEQ_LEN)
    q, k, v = project_qkv(attn_rows.reshape(group_rows, depth), qkv_here, b_qv)
    found, lse = attend(q, k, v, block_ids, local_rows)
    arrived = swap(found, "col")
    grad_up, grad_down, grad_wout, grad_bup, output, d_resid, sums, d_heads, qkv_all = middle(
        arrived, tokens, grad_out, up_weight, down_weight, up_bias, vec(b_out), vec(gain2),
        vec(shift2), vec(b_down), out_weight, w_qkv_flat,
    )
    hidden_units = units * cols
    used = 4 + hidden_units // depth
    spare = (used + 9) // 8 * 8 - used
    early = jnp.concatenate(
        [sums[:4], grad_bup.reshape(-1, depth), jnp.zeros((spare, depth), f32)]
    )
    grad_tokens, grad_wup, grad_wdown, grad_wout, grad_wqkv, small, bias = backward(
        block_ids, q, k, v, d_heads, found, lse, attn_rows, qkv_all, tokens, d_resid, vec(gain1),
        grad_up, grad_down, grad_wout, early,
    )
    grad_wqkv = (
        grad_wqkv.reshape(heads, 3, HD, depth // rows)
        .transpose(3, 1, 0, 2)
        .reshape(depth // rows, 3, head_cols)
    )
    grad_bqv = bias[:, :, :2].reshape(head_cols, 2).T
    grad_bdown, grad_gain2, grad_shift2, grad_bout = small[:4]
    grad_bup = lax.dynamic_slice_in_dim(
        small[4:used].reshape(-1), lax.axis_index("col") * units, units
    )
    grad_gain1, grad_shift1 = small[-2:]
    return (
        output, grad_tokens, grad_wqkv, grad_bqv, grad_wout, grad_bout, grad_wup, grad_bup,
        grad_wdown, grad_bdown, grad_gain1, grad_shift1, grad_gain2, grad_shift2,
    )


def solution(mesh):
    tokens, weight, whole_vec = P(("row", "col"), None), P("col", "row"), P()
    qkv, bias_qv = P("row", None, "col"), P(None, "col")
    return jax.shard_map(
        body,
        mesh=mesh,
        in_specs=(
            tokens, P(("row", "col")), qkv, bias_qv, weight, whole_vec, weight, P("col"), weight,
            whole_vec, whole_vec, whole_vec, whole_vec, whole_vec, tokens,
        ),
        out_specs=(
            tokens, tokens, qkv, bias_qv, weight, whole_vec, weight, P("col"), weight,
            whole_vec, whole_vec, whole_vec, whole_vec, whole_vec,
        ),
        check_vma=False,
    )
```

time: 794 us -> 516 us (0.65); the launches traced: 780 us -> 515 us
  blocking collectives: 152 us -> 0 us
  waiting for transfers between devices: 175 us -> 63.1 us
  Pallas kernels: 315 us -> 409 us
  starting transfers between devices: 72.7 us -> 4.51 us
  other arithmetic: 35.1 us -> 4.9 us
    all_to_all x5 -> x0, blocking collectives: 152 us -> none  [swap(): return lax.all_to_all(x, axis, 0, 0, tiled=True, axis_index_groups=groups)]
    all_to_all x16 -> x1, waiting for transfers between devices: 151 us -> 35.3 us  [swap(): return lax.all_to_all(x, axis, 0, 0, tiled=True, axis_index_groups=groups)]
    pallas_call x10 -> x3, Pallas kernels: 199 us -> 292 us  [the longest x1 173 us: backward(): pl.pallas_call(functools.partial(back_kernel, rows, cols, heads, seqs, ti...]
    all_to_all x16 -> x1, starting transfers between devices: 72.6 us -> 4.4 us  [swap(): return lax.all_to_all(x, axis, 0, 0, tiled=True, axis_index_groups=groups)]
    reduce_sum x14 -> x0, other arithmetic: 30.8 us -> none  [total_of(): return jnp.sum(x.astype(f32), axis=0)]
    all_gather x4 -> x3, waiting for transfers between devices: 21.6 us -> 25.7 us  [gather_all(): lax.all_gather(w, ('row', 'col'), axis=0, tiled=False)]
  transfers between devices with their start and end apart: 20 -> 4, of which waited for: 11 -> 2; matrix products, arithmetic and copies ran while one was open for 6% -> 2% of each run, Pallas kernels for 35% -> 31%
where the time goes in v2:
time: 516 us; the launch traced here: 515 us
  Pallas kernels  409 us (79%)
  waiting for transfers between devices  63.1 us (12%)
  local copies, waits for them, and re-layouts  19.4 us (4%)
  between operations  13.9 us (3%)
    pallas_call x1, Pallas kernels, backward(): pl.pallas_call(functools.partial(back_kernel, rows, cols, heads, seqs, ti...  173 us
    pallas_call x1, Pallas kernels, gather_inputs(): pl.pallas_call(functools.partial(gather_kernel, rows, cols), out_shape=[j...  107 us
    pallas_call x1, Pallas kernels, middle(): pl.pallas_call(functools.partial(middle_kernel, rows, cols), grid=(2 * co...  75.2 us
    pallas_call x1, Pallas kernels, attend(): pl.pallas_call(functools.partial(attend_kernel, tile), grid=(heads, seqs,...  44.1 us
    all_to_all x1, waiting for transfers between devices, swap(): return lax.all_to_all(x, axis, 0, 0, tiled=True, axis_index_groups=groups)  35.3 us
    all_gather x3, waiting for transfers between devices, gather_all(): lax.all_gather(w, ('row', 'col'), axis=0, tiled=False)  25.7 us
  transfers between devices with their start and end apart: 4, of which 2 were waited for; matrix products, arithmetic and copies ran while one was open for 2% of the time, Pallas kernels for 31%

profile of v2, /device:TPU:0, one launch (start us, length us, event | category | flops | bytes accessed | tf_op | source)
XLA Modules:
  0.0 514.9 jit_solution(6473104138886271490)
XLA Ops:
  10.8 1.1 copy.32
  11.8 0.8 copy.33.w_ref.wq_ref
  12.7 1.3 reshape.97.bup_ref
  14.6 1.4 fusion.5.x_ref
  16.0 107.2 %gather_inputs.1 = (bf16[8,512,1024]{2,1,0:T(8,128)(2,1)}, s32[8,1,512]{2,1,0:T(1,128)}, bf16[8,1,512]{2,1,0:T(2,128)(2,1)}, bf16[1024,384]{1,0:T(8,128)(2,1)}) custom-call(bf16[512,1024]{1,0:T(8,128)(2,1)} %fusion.5.x_ref, s32[1,512]{1,0:T(1,128)} %bitcast.36, bf16[1,512]{1,0:T(2,128)(2,1)} %reshape.97.bup_ref, bf16[256,384]{1,0:T(8,128)(2,1)} %copy.33.w_ref.wq_ref), custom_call_target="tpu_custom_call" | custom-call | tf_op jit(solution)/shard_map/gather_inputs/pallas_call | solution.py:185
  123.2 9.8 %project_qkv.1 = (bf16[2,4096,64]{2,1,0:T(8,128)(2,1)}, bf16[2,4096,64]{2,1,0:T(8,128)(2,1)}, bf16[2,4096,64]{2,1,0:T(8,128)(2,1)}) custom-call(bf16[4096,1024]{1,0:T(8,128)(2,1)} %bitcast.39, bf16[1024,384]{1,0:T(8,128)(2,1)} %get-tuple-element.41.w_ref, bf16[2,128]{1,0:T(2,128)(2,1)} %b_ref.1), custom_call_target="tpu_custom_call" | custom-call | flops 3221225472 | bytes 11534336 | tf_op jit(solution)/shard_map/project_qkv/pallas_call | solution.py:223
  133.0 44.1 %attend.1 = (bf16[8,128,512]{2,1,0:T(8,128)(2,1)}, f32[2,1,1,4096]{3,2,1,0:T(1,128)}) custom-call(s32[1,1,4096]{2,1,0:T(1,128)} %bitcast.42, bf16[2,4096,64]{2,1,0:T(8,128)(2,1)} %get-tuple-element.42.q_ref, bf16[2,4096,64]{2,1,0:T(8,128)(2,1)} %get-tuple-element.43.k_ref, bf16[2,4096,64]{2,1,0:T(8,128)(2,1)} %get-tuple-element.44.v_ref), custom_call_target="tpu_custom_call" | custom-call | flops 21474836480 | bytes 4194304 | tf_op jit(solution)/shard_map/attend/pallas_call | solution.py:290
  177.2 4.4 all-to-all-start
  184.7 35.3 %all-to-all-done.heads_ref = bf16[8,128,512]{2,1,0:T(8,128)(2,1)} async-done(((bf16[8,128,512]{2,1,0:T(8,128)(2,1)}), bf16[8,128,512]{2,1,0:T(8,128)(2,1)}, u32[]{:S(2)}, u32[]{:S(2)}) %all-to-all-start) | async-done | bytes 1048608 | tf_op jit(solution)/shard_map/all_to_all | solution.py:1024
  219.9 25.7 %all-gather.9.cloned.1.call-done = bf16[16384,256]{1,0:T(8,128)(2,1)} async-done(((bf16[512,256]{1,0:T(8,128)(2,1)}), bf16[16384,256]{1,0:T(8,128)(2,1)}) %all-gather.9.cloned.1.call-update) | async-done | bytes 8388624 | tf_op jit(solution)/shard_map/all_gather | solution.py:1046
  245.7 75.2 %middle.1 = (bf16[4,4,512,256]{3,2,1,0:T(8,128)(2,1)}, bf16[4,4,512,256]{3,2,1,0:T(8,128)(2,1)}, bf16[4,4,128,256]{3,2,1,0:T(8,128)(2,1)}, f32[8,1,512]{2,1,0:T(...) custom-call(bf16[8,128,512]{2,1,0:T(8,128)(2,1)} %all-to-all-done.he, ...), custom_call_target="tpu_custom_call" | custom-call | flops 25769803776 | bytes 41943040 | tf_op jit(solution)/shard_map/middle/pallas_call | solution.py:599
  320.9 0.8 reduce
  321.6 0.8 slice.17
  322.4 0.7 maximum_maximum_fusion.early_ref
  323.1 172.8 %backward.1 = (f32[512,1024]{1,0:T(8,128)}, f32[512,256]{1,0:T(8,128)}, f32[512,256]{1,0:T(8,128)}, f32[128,256]{1,0:T(8,128)}, f32[384,256]{1,0:T(8,128)}, /*index=5*/f32[16,1024]{1,0:T(8,128)}, f32[2,64,128]{2,1,0:T(8,128)}) custom-call(s32[1,1,4096]{2,1,0:T(1,128)} %bitcast.43, bf16[2,4096,64]{2,1,0:T(8,128)(2,1)} %get-tuple-element.42.q_ref, ...), custom_call_target="tpu_custom_call" | custom-call | flops 53687091200 | bytes 8388608 | tf_op jit(solution)/shard_map/backward/pallas_call | solution.py:969
  495.9 0.9 slice_bitcast_fusion
  496.8 1.6 fusion.6
  498.5 1.0 copy.35
  499.5 0.9 copy.37
  500.4 1.5 copy.36
  502.5 2.3 copy.46
  504.8 1.3 copy.47
  506.8 0.8 copy.49
  507.6 0.8 copy.50
  (45 shorter events, 8.6 us)
Async XLA Ops:
  7.2 6.7 %copy-start = (bf16[512,1024]{1,0:T(8,128)(2,1)S(1)}, bf16[512,1024]{1,0:T(8,128)(2,1)}, u32[]{:S(2)}) copy-start(bf16[512,1024]{1,0:T(8,128)(2,1)} %tok_ref.3) | copy-start | bytes 3145732
  7.2 212.7 %all-gather.11.cloned.1.call-start = ((), (), s32[]{:S(2)}) async-start(), calls=%async_computation.3 | async-start | bytes 2162688 | tf_op jit(solution)/shard_map/all_gather | solution.py:1046
  7.9 212.0 %all-gather.7.cloned.1.call-start = ((), (), s32[]{:S(2)}) async-start(), calls=%async_computation.1 | async-start | bytes 8650752 | tf_op jit(solution)/shard_map/all_gather | solution.py:1046
  8.7 237.0 %all-gather.9.cloned.1.call-start = ((), (), s32[]{:S(2)}) async-start(), calls=%async_computation.2 | async-start | bytes 8650752 | tf_op jit(solution)/shard_map/all_gather | solution.py:1046
  177.1 4.5 copy-start.5
  177.1 5.1 copy-start.6
  177.1 5.7 %copy-start.7 = (bf16[1024]{0:T(1024)(128)(2,1)S(1)}, bf16[1024]{0:T(1024)(128)(2,1)}, u32[]{:S(2)}) copy-start(bf16[1024]{0:T(1024)(128)(2,1)} %param.27) | copy-start | bytes 6148
  177.1 6.2 %copy-start.8 = (bf16[1024]{0:T(1024)(128)(2,1)S(1)}, bf16[1024]{0:T(1024)(128)(2,1)}, u32[]{:S(2)}) copy-start(bf16[1024]{0:T(1024)(128)(2,1)} %param.28) | copy-start | bytes 6148
  177.2 6.8 %copy-start.9 = (bf16[1024]{0:T(1024)(128)(2,1)S(1)}, bf16[1024]{0:T(1024)(128)(2,1)}, u32[]{:S(2)}) copy-start(bf16[1024]{0:T(1024)(128)(2,1)} %param.24) | copy-start | bytes 6148
  177.2 42.8 %all-to-all-start = ((bf16[8,128,512]{2,1,0:T(8,128)(2,1)}), bf16[8,128,512]{2,1,0:T(8,128)(2,1)}, u32[]{:S(2)}, u32[]{:S(2)}) async-start(bf16[8,128,512]{2,1,0:T(8,128)(2,1)} %get-tuple-element.45.o_ref), calls=%async_computation | async-start | bytes 2097152 | tf_op jit(solution)/shard_map/all_to_all | solution.py:1024
  495.9 8.9 %copy-start.1 = (f32[512,1024]{1,0:T(8,128)S(1)}, f32[512,1024]{1,0:T(8,128)}, u32[]{:S(2)}) copy-start(f32[512,1024]{1,0:T(8,128)} %get-tuple-element.99) | copy-start | bytes 6291460
  504.8 1.3 copy-start.4
  504.8 2.0 copy-start.3
  504.8 2.8 copy-start.2
Sparse Core Ops, SparseCore 0:
  11.0 61.4 all-gather.10
  75.4 79.0 all-gather.6
  157.6 88.0 all-gather.8

commit v3 on v2

--- a/solution.py
+++ b/solution.py
@@ -60,257 +60,6 @@
     )
 
 
-def gather_kernel(
-    rows, cols, x_ref, blk_ref, bup_ref, w_ref, xo_ref, blko_ref, bupo_ref, wo_ref,
-    send_x, recv_x, send_s, recv_s, send_w, recv_w, local,
-):
-    row, me = lax.axis_index("row"), lax.axis_index("col")
-    chips = cols // 2
-    chip, lane = me // 2, lax.rem(me, 2)
-    mate = chip * 2 + 1 - lane
-    depth = w_ref.shape[0]
-
-    barrier = pltpu.get_barrier_semaphore()
-    for k in range(1, cols):
-        pl.semaphore_signal(
-            barrier, inc=1, device_id=(row, lax.rem(me + k, cols)), device_id_type=MESH
-        )
-    for k in range(1, rows):
-        pl.semaphore_signal(
-            barrier, inc=1, device_id=(lax.rem(row + k, rows), me), device_id_type=MESH
-        )
-    pl.semaphore_wait(barrier, rows + cols - 2)
-
-    def chunk(src, owner, target, route, at):
-        return pltpu.make_async_remote_copy(
-            src_ref=src,
-            dst_ref=xo_ref.at[owner],
-            send_sem=send_x.at[route, at],
-            recv_sem=recv_x.at[route, at],
-            device_id=(row, target),
-            device_id_type=MESH,
-        )
-
-    @pl.when(chip + 1 < chips)
-    def _():
-        chunk(x_ref, me, me + 2, 0, chip).start()
-
-    @pl.when(chip > 0)
-    def _():
-        chunk(x_ref, me, me - 2, 1, chip).start()
-
-    chunk(x_ref, me, mate, 2, chip).start()
-    weights = []
-    where = pl.ds(pl.multiple_of(row * depth, depth), depth)
-    for k in range(1, rows):
-        copy = pltpu.make_async_remote_copy(
-            src_ref=w_ref,
-            dst_ref=wo_ref.at[where],
-            send_sem=send_w.at[k],
-            recv_sem=recv_w.at[k],
-            device_id=(lax.rem(row + k, rows), me),
-            device_id_type=MESH,
-        )
-        copy.start()
-        weights.append(copy)
-    small = []
-    for k in range(1, cols):
-        for at, (src, dst) in enumerate(((blk_ref, blko_ref), (bup_ref, bupo_ref))):
-            copy = pltpu.make_async_remote_copy(
-                src_ref=src,
-                dst_ref=dst.at[me],
-                send_sem=send_s.at[at, k],
-                recv_sem=recv_s.at[at, k],
-                device_id=(row, lax.rem(me + k, cols)),
-                device_id_type=MESH,
-            )
-            copy.start()
-            small.append(copy)
-    own = [
-        pltpu.make_async_copy(x_ref, xo_ref.at[me], local.at[0]),
-        pltpu.make_async_copy(blk_ref, blko_ref.at[me], local.at[1]),
-        pltpu.make_async_copy(bup_ref, bupo_ref.at[me], local.at[2]),
-        pltpu.make_async_copy(w_ref, wo_ref.at[where], local.at[3]),
-    ]
-    for copy in own:
-        copy.start()
-
-    for hop in range(1, chips):
-        below, above = chip - hop, chip + hop
-
-        @pl.when(below >= 0)
-        def _():
-            owner = below * 2 + lane
-            chunk(xo_ref.at[owner], owner, me, 0, below).wait_recv()
-
-            @pl.when(chip + 1 < chips)
-            def _():
-                chunk(xo_ref.at[owner], owner, me + 2, 0, below).start()
-
-            chunk(xo_ref.at[owner], owner, mate, 2, below).start()
-
-        @pl.when(above < chips)
-        def _():
-            owner = above * 2 + lane
-            chunk(xo_ref.at[owner], owner, me, 1, above).wait_recv()
-
-            @pl.when(chip > 0)
-            def _():
-                chunk(xo_ref.at[owner], owner, me - 2, 1, above).start()
-
-            chunk(xo_ref.at[owner], owner, mate, 2, above).start()
-
-    for at in range(chips):
-        copy = chunk(x_ref, me, mate, 2, at)
-        copy.wait_recv()
-        copy.wait_send()
-
-        @pl.when((at <= chip) & (chip + 1 < chips))
-        def _():
-            chunk(x_ref, me, me, 0, at).wait_send()
-
-        @pl.when((at >= chip) & (chip > 0))
-        def _():
-            chunk(x_ref, me, me, 1, at).wait_send()
-
-    for copy in weights + small + own:
-        copy.wait()
-
-
-def gather_inputs(x, blocks, b_up, w_qkv, rows, cols):
-    any_space = pl.BlockSpec(memory_space=pl.ANY)
-    vmem = pl.BlockSpec(memory_space=pltpu.VMEM)
-    chips = cols // 2
-    dma = pltpu.SemaphoreType.DMA
-    return pl.pallas_call(
-        functools.partial(gather_kernel, rows, cols),
-        out_shape=[
-            jax.ShapeDtypeStruct((cols,) + x.shape, x.dtype),
-            jax.ShapeDtypeStruct((cols,) + blocks.shape, blocks.dtype),
-            jax.ShapeDtypeStruct((cols,) + b_up.shape, b_up.dtype),
-            jax.ShapeDtypeStruct((rows * w_qkv.shape[0], w_qkv.shape[1]), w_qkv.dtype),
-        ],
-        in_specs=[vmem] * 4,
-        out_specs=[any_space] * 4,
-        scratch_shapes=[
-            dma((3, chips)), dma((3, chips)),
-            dma((2, cols)), dma((2, cols)),
-            dma((rows,)), dma((rows,)), dma((4,)),
-        ],
-        compiler_params=pltpu.CompilerParams(collective_id=0, has_side_effects=True),
-        name="gather_inputs",
-    )(x, blocks, b_up, w_qkv)
-
-
-def qkv_kernel(x_ref, w_ref, b_ref, q_ref, k_ref, v_ref):
-    mixed = dot(x_ref[...], w_ref[...])
-    heads = q_ref.shape[0]
-    width = heads * HD
-    bias = b_ref[...].astype(f32)
-    for h in range(heads):
-        lanes = slice(h * HD, (h + 1) * HD)
-        q_ref[h] = (mixed[:, :width][:, lanes] + bias[0:1, lanes]).astype(bf16)
-        k_ref[h] = mixed[:, width : 2 * width][:, lanes].astype(bf16)
-        v_ref[h] = (mixed[:, 2 * width :][:, lanes] + bias[1:2, lanes]).astype(bf16)
-
-
-def project_qkv(x, w, bias):
-    count, depth = x.shape
-    width = w.shape[1] // 3
-    heads = width // HD
-    tile = min(1024, count)
-    out = pl.BlockSpec((heads, tile, HD), lambda i: (0, i, 0))
-    return pl.pallas_call(
-        qkv_kernel,
-        grid=(count // tile,),
-        in_specs=[pl.BlockSpec((tile, depth), lambda i: (i, 0)), whole(w.shape), whole(bias.shape)],
-        out_specs=[out] * 3,
-        out_shape=[jax.ShapeDtypeStruct((heads, count, HD), bf16)] * 3,
-        compiler_params=params(),
-        cost_estimate=cost(2 * count * depth * 3 * width, 2 * count * (depth + 3 * width)),
-        name="project_qkv",
-    )(x, w, bias)
-
-
-def tile_mask(blk_ref, key_start, count, query_blocks):
-    key_blocks = jnp.broadcast_to(blk_ref[0, :, pl.ds(key_start, count)], (128, count)).T[:, :1]
-    return query_blocks >= key_blocks
-
-
-def attend_kernel(step, blk_ref, q_ref, k_ref, v_ref, o_ref, lse_ref, values):
-    i = pl.program_id(2)
-    tile = q_ref.shape[1]
-    chunks, _, chunk = o_ref.shape
-
-    @pl.when(i == 0)
-    def _():
-        values[:HD, :] = flip(v_ref[0])
-        values[HD:, :] = jnp.ones((ONES, values.shape[1]), bf16)
-
-    start = pl.multiple_of(i * tile, tile)
-    query = q_ref[0]
-    query_blocks = blk_ref[0, :, pl.ds(start, tile)]
-
-    def update(state, key_start, count, masked):
-        total, top = state
-        scores = dot(k_ref[0, pl.ds(key_start, count), :], query, NT)
-        if masked:
-            mask = tile_mask(blk_ref, key_start, count, query_blocks)
-            scores = jnp.where(mask, scores, MASKED)
-        higher = jnp.maximum(top, jnp.max(scores, axis=0, keepdims=True) * SCALE2)
-        probs = jnp.exp2(scores * SCALE2 - higher)
-        part = dot(values[:, pl.ds(key_start, count)], probs.astype(bf16))
-        return total * jnp.exp2(top - higher) + part, higher
-
-    state = (jnp.zeros((HD + ONES, tile), f32), jnp.full((1, tile), MASKED, f32))
-    state = lax.fori_loop(
-        0, start // step, lambda j, s: update(s, pl.multiple_of(j * step, step), step, False), state
-    )
-    state = update(state, start, tile, True)
-    total, top = lax.fori_loop(
-        0,
-        jnp.where(i < pl.num_programs(2) - 1, 1, 0),
-        lambda j, s: update(s, pl.multiple_of(start + tile, BLOCK), BLOCK, True),
-        state,
-    )
-    mass = total[HD : HD + 1]
-    out = (total[:HD] / mass).astype(bf16)
-    for b in range(chunks):
-        o_ref[b] = out[:, b * chunk : (b + 1) * chunk]
-    lse_ref[0, 0] = top + jnp.log2(mass)
-
-
-def attend(q, k, v, blocks, chunk):
-    heads, count, _ = q.shape
-    seqs = count // SEQ_LEN
-    tile = 1024
-    tiles = SEQ_LEN // tile
-    pairs = heads * seqs * SEQ_LEN * SEQ_LEN * 5 // 8
-    keys = pl.BlockSpec((1, SEQ_LEN, HD), lambda h, s, i: (h, s, 0))
-    return pl.pallas_call(
-        functools.partial(attend_kernel, tile),
-        grid=(heads, seqs, tiles),
-        in_specs=[
-            pl.BlockSpec((1, 1, SEQ_LEN), lambda h, s, i: (s, 0, 0)),
-            pl.BlockSpec((1, tile, HD), lambda h, s, i: (h, s * tiles + i, 0)),
-            keys,
-            keys,
-        ],
-        out_specs=[
-            pl.BlockSpec((tile // chunk, HD, chunk), lambda h, s, i: (s * tiles + i, h, 0)),
-            pl.BlockSpec((1, 1, 1, tile), lambda h, s, i: (h, s, 0, i)),
-        ],
-        out_shape=[
-            jax.ShapeDtypeStruct((count // chunk, heads * HD, chunk), bf16),
-            jax.ShapeDtypeStruct((heads, seqs, 1, SEQ_LEN), f32),
-        ],
-        scratch_shapes=[pltpu.VMEM((HD + ONES, SEQ_LEN), bf16)],
-        compiler_params=params(),
-        cost_estimate=cost(16 * pairs * HD, 8 * heads * count * HD, pairs),
-        name="attend",
-    )(blocks, q, k, v)
-
-
 def place():
     return lax.axis_index("row"), lax.axis_index("col")
 
@@ -397,6 +146,375 @@
 def mate():
     row, col = place()
     return (row, col // 2 * 2 + 1 - lax.rem(col, 2))
+
+
+def front_kernel(
+    rows, cols, heads,
+    tok_ref, gain_ref, shift_ref, blk_ref, bup_ref, wq_ref, bias_ref, wout_ref, wup_ref, wdown_ref,
+    xo_ref, q_ref, k_ref, v_ref, found_ref, arrived_ref, lse_ref, blko_ref, bupo_ref,
+    wouto_ref, wupo_ref, wdowno_ref,
+    xs, wqs, qs, ks, vs, vt, totals, tops, founds, blks, bups,
+    send_x, recv_x, send_q, recv_q, send_s, recv_s, send_f, recv_f,
+    send_wz, recv_wz, send_wr, recv_wr, send_wm, recv_wm, local_x, local_q, local_f, local_w,
+):
+    chips = cols // 2
+    row, me = place()
+    chip, lane = me // 2, lax.rem(me, 2)
+    count = tok_ref.shape[0]
+    tile = 2 * count
+    seq_chips = SEQ_LEN // tile
+    depth = wq_ref.shape[0]
+    width = heads * HD
+
+    xhat, _ = moments(tok_ref[...].astype(f32))
+    xs[me] = (xhat * gain_ref[...].astype(f32) + shift_ref[...].astype(f32)).astype(bf16)
+    blks[me] = blk_ref[...]
+    bups[me] = bup_ref[...]
+    own_rows = pl.ds(pl.multiple_of(row * depth, depth), depth)
+    wqs[own_rows] = wq_ref[...]
+    vt[:, HD:, :] = jnp.ones((heads, ONES, vt.shape[2]), bf16)
+    greet(rows, cols)
+
+    def chunk(owner, target, route, at):
+        return remote(
+            xs.at[owner], xs.at[owner], send_x.at[route, at], recv_x.at[route, at], (row, target)
+        )
+
+    def to_mate(owner, at):
+        return remote(xs.at[owner], xs.at[owner], send_x.at[2, at], recv_x.at[2, at], mate())
+
+    given = (wout_ref, wup_ref, wdown_ref)
+    gathered = (wouto_ref, wupo_ref, wdowno_ref)
+
+    q_stage = over_row(
+        rows,
+        lambda at: wq_ref,
+        lambda at: wqs.at[pl.ds(pl.multiple_of(at * depth, depth), depth)],
+        send_q,
+        recv_q,
+    )
+    small = [
+        over_col(cols, lambda at: blk_ref, lambda at: blks.at[at], send_s.at[0], recv_s.at[0]),
+        over_col(cols, lambda at: bup_ref, lambda at: bups.at[at], send_s.at[1], recv_s.at[1]),
+    ]
+    f_stage_out = lambda at: founds.at[at]
+    f_stage = over_col(cols, f_stage_out, lambda at: arrived_ref.at[at], send_f, recv_f)
+
+    def w_line(n):
+        return over_line(
+            chips, lambda at: given[n], lambda at: gathered[n].at[lane, at, row], send_wz.at[n],
+            recv_wz.at[n],
+        )
+
+    def w_row(n, c, out):
+        return over_row(
+            rows, lambda at: out, lambda at: gathered[n].at[lane, c, at], send_wr.at[n, c],
+            recv_wr.at[n, c],
+        )
+
+    def w_own(n):
+        return pltpu.make_async_copy(given[n], gathered[n].at[lane, chip, row], local_w.at[n])
+
+    def w_mate(n, c, side):
+        block = gathered[n].at[side, c]
+        return remote(block, block, send_wm.at[n, c], recv_wm.at[n, c], mate())
+
+    q_stage.start()
+    for exchange in small:
+        exchange.start()
+
+    @pl.when(chip + 1 < chips)
+    def _():
+        chunk(me, me + 2, 0, chip).start()
+
+    @pl.when(chip > 0)
+    def _():
+        chunk(me, me - 2, 1, chip).start()
+
+    to_mate(me, chip).start()
+    for n in range(3):
+        w_own(n).start()
+        w_row(n, chip, given[n]).start()
+        w_line(n).start()
+    q_stage.wait_recv()
+    for exchange in small:
+        exchange.wait_recv()
+
+    def update(h, q_tile, q_low, q_count, key_start, key_count, mask):
+        lanes = pl.ds(q_low, q_count)
+        query = qs[h, pl.ds(pl.multiple_of(q_tile * tile + q_low, BLOCK), q_count), :]
+        keys = pl.ds(pl.multiple_of(key_start, BLOCK), key_count)
+        scores = dot(ks[h, keys, :], query, NT)
+        if mask is not None:
+            scores = jnp.where(mask, scores, MASKED)
+        top = tops[h, q_tile, :, lanes]
+        higher = jnp.maximum(top, jnp.max(scores, axis=0, keepdims=True) * SCALE2)
+        probs = jnp.exp2(scores * SCALE2 - higher)
+        part = dot(vt[h, :, keys], probs.astype(bf16))
+        totals[h, q_tile, :, lanes] = totals[h, q_tile, :, lanes] * jnp.exp2(top - higher) + part
+        tops[h, q_tile, :, lanes] = higher
+
+    def column(blocks, amount):
+        return jnp.broadcast_to(blocks, (128, amount)).T[:, :1]
+
+    def diagonal(p):
+        low, high = blks[2 * p], blks[2 * p + 1]
+        first = column(jnp.concatenate([low, high[:, :BLOCK]], axis=1), count + BLOCK)
+        second = column(jnp.concatenate([low, high], axis=1), tile)
+        for h in range(heads):
+            update(h, p, 0, count, p * tile, count + BLOCK, low >= first)
+            update(h, p, count, count, p * tile, tile, high >= second)
+
+    def boundary(p):
+        mask = blks[2 * p + 1][:, count - BLOCK :] >= column(blks[2 * p + 2][:, :BLOCK], BLOCK)
+        for h in range(heads):
+            update(h, p, tile - BLOCK, BLOCK, (p + 1) * tile, BLOCK, mask)
+
+    def project(p):
+        both = jnp.concatenate([xs[2 * p], xs[2 * p + 1]], axis=0)
+        mixed = dot(both, wqs[...])
+        bias = bias_ref[...].astype(f32)
+        where = pl.ds(pl.multiple_of(p * tile, tile), tile)
+        for h in range(heads):
+            at = [slice(j * width + h * HD, j * width + (h + 1) * HD) for j in range(3)]
+            here = slice(h * HD, (h + 1) * HD)
+            qs[h, where, :] = (mixed[:, at[0]] + bias[0:1, here]).astype(bf16)
+            ks[h, where, :] = mixed[:, at[1]].astype(bf16)
+            values = (mixed[:, at[2]] + bias[1:2, here]).astype(bf16)
+            vs[h, where, :] = values
+            vt[h, :HD, where] = flip(values)
+            totals[h, p] = jnp.zeros(totals.shape[2:], f32)
+            tops[h, p] = jnp.full(tops.shape[2:], MASKED, f32)
+
+    def keep(p):
+        where = pl.ds(pl.multiple_of(p * tile, tile), tile)
+        pairs = [
+            pltpu.make_async_copy(held.at[:, where, :], out.at[:, where, :], local_q.at[n, p])
+            for n, (held, out) in enumerate(((qs, q_ref), (ks, k_ref), (vs, v_ref)))
+        ]
+        return pairs + [
+            pltpu.make_async_copy(xs.at[2 * p + c], xo_ref.at[2 * p + c], local_x.at[2 * p + c])
+            for c in range(2)
+        ]
+
+    def kept(c):
+        return pltpu.make_async_copy(founds.at[c], found_ref.at[c], local_f.at[0, c])
+
+    def own(c):
+        return pltpu.make_async_copy(founds.at[c], arrived_ref.at[c], local_f.at[1, 0])
+
+    def conclude(p):
+        for h in range(heads):
+            mass = totals[h, p, HD : HD + 1, :]
+            out = (totals[h, p, :HD, :] / mass).astype(bf16)
+            for c in range(2):
+                founds[2 * p + c, h * HD : (h + 1) * HD, :] = out[:, c * count : (c + 1) * count]
+            lse_ref[
+                h, p // seq_chips, :, pl.ds(pl.multiple_of(lax.rem(p, seq_chips) * tile, tile), tile)
+            ] = tops[h, p] + jnp.log2(mass)
+        for c in range(2):
+            owner = 2 * p + c
+            kept(owner).start()
+
+            @pl.when(owner == me)
+            def _():
+                own(owner).start()
+
+            @pl.when(owner != me)
+            def _():
+                f_stage.copy(lax.rem(owner - me + cols, cols)).start()
+
+    def event(e, carry):
+        hop = (e + 1) // 2
+        lower = lax.rem(e, 2) == 1
+        p = jnp.where(lower, chip - hop, chip + hop)
+
+        @pl.when(lower)
+        def _():
+            below, above = chip - hop, chip + hop
+
+            @pl.when(below >= 0)
+            def _():
+                owner = below * 2 + lane
+                chunk(owner, me, 0, below).wait_recv()
+
+                @pl.when(chip + 1 < chips)
+                def _():
+                    chunk(owner, me + 2, 0, below).start()
+
+                to_mate(owner, below).start()
+
+            @pl.when(above < chips)
+            def _():
+                owner = above * 2 + lane
+                chunk(owner, me, 1, above).wait_recv()
+
+                @pl.when(chip > 0)
+                def _():
+                    chunk(owner, me - 2, 1, above).start()
+
+                to_mate(owner, above).start()
+
+        @pl.when(e == min(3, 2 * chips - 3))
+        def _():
+            for n in range(3):
+                w_line(n).wait_recv()
+
+                def onward(k, carry):
+                    c = lax.rem(chip + k, chips)
+                    w_row(n, c, gathered[n].at[lane, c, row]).start()
+                    return carry
+
+                lax.fori_loop(1, chips, onward, 0)
+
+        @pl.when(e == 2 * chips - 3)
+        def _():
+            for n in range(3):
+                w_own(n).wait()
+                w_row(n, chip, given[n]).wait_recv()
+                w_mate(n, chip, lane).start()
+
+        @pl.when((p >= 0) & (p < chips))
+        def _():
+            to_mate(2 * p + 1 - lane, p).wait_recv()
+            project(p)
+            for copy in keep(p):
+                copy.start()
+            first = p // seq_chips * seq_chips
+            final = first + seq_chips - 1
+            high = jnp.minimum(chip + hop - 1, final)
+            low = jnp.maximum(jnp.maximum(chip - hop, 0), first)
+            diagonal(p)
+
+            @pl.when(lower & (p < final))
+            def _():
+                boundary(p)
+
+            @pl.when(lower & (p == first))
+            def _():
+                conclude(p)
+
+            amount = jnp.where(lower, high - p, p - low)
+
+            def pair(j, carry):
+                q_tile = jnp.where(lower, p + 1 + j, p)
+                key_tile = jnp.where(lower, p, low + j)
+                for h in range(heads):
+                    update(h, q_tile, 0, tile, key_tile * tile, tile, None)
+
+                @pl.when(lower & (p == first) & ((q_tile == final) | (q_tile < high)))
+                def _():
+                    conclude(q_tile)
+
+                return carry
+
+            lax.fori_loop(0, amount, pair, 0)
+
+            @pl.when(jnp.logical_not(lower) & (p > first) & (hop > 0))
+            def _():
+                boundary(p - 1)
+
+                @pl.when(low == first)
+                def _():
+                    conclude(p - 1)
+
+            @pl.when(jnp.logical_not(lower) & (p == final) & (low == first))
+            def _():
+                conclude(p)
+
+        return carry
+
+    lax.fori_loop(0, 2 * chips - 1, event, 0)
+
+    for n in range(3):
+
+        def across(k, carry):
+            c = lax.rem(chip + k, chips)
+            w_row(n, c, given[n]).wait_recv()
+            w_mate(n, c, lane).start()
+            return carry
+
+        lax.fori_loop(1, chips, across, 0)
+    for c in range(cols):
+        bupo_ref[c] = bups[c]
+        at = c * count
+        blko_ref[at // SEQ_LEN, :, at % SEQ_LEN : at % SEQ_LEN + count] = blks[c]
+    f_stage.wait_recv()
+    for c in range(chips):
+        for n in range(3):
+            w_mate(n, c, 1 - lane).wait_recv()
+            w_mate(n, c, lane).wait_send()
+            w_row(n, c, given[n]).wait_send()
+        for copy in keep(c):
+            copy.wait()
+        kept(2 * c).wait()
+        kept(2 * c + 1).wait()
+        to_mate(me, c).wait_send()
+
+        @pl.when((c <= chip) & (chip + 1 < chips))
+        def _():
+            chunk(me, me, 0, c).wait_send()
+
+        @pl.when((c >= chip) & (chip > 0))
+        def _():
+            chunk(me, me, 1, c).wait_send()
+
+    own(me).wait()
+    for n in range(3):
+        w_line(n).wait_send()
+    f_stage.wait_send()
+    q_stage.wait_send()
+    for exchange in small:
+        exchange.wait_send()
+
+
+def front(tokens, gain, shift, blocks, b_up, w_qkv, b_qv, w_out, w_up, w_down, rows, cols):
+    count, depth = tokens.shape
+    head_cols = w_qkv.shape[1] // 3
+    heads = head_cols // HD
+    chips = cols // 2
+    total = count * cols
+    tile = 2 * count
+    any_space = pl.BlockSpec(memory_space=pl.ANY)
+    in_vmem = pl.BlockSpec(memory_space=pltpu.VMEM)
+    dma, vmem, shape = pltpu.SemaphoreType.DMA, pltpu.VMEM, jax.ShapeDtypeStruct
+    pairs = heads * total * SEQ_LEN * 5 // 8
+    held = (heads, total, HD)
+    return pl.pallas_call(
+        functools.partial(front_kernel, rows, cols, heads),
+        in_specs=[in_vmem] * 10,
+        out_specs=[any_space] * 6 + [in_vmem] * 3 + [any_space] * 3,
+        out_shape=[
+            shape((cols, count, depth), bf16), shape(held, bf16), shape(held, bf16),
+            shape(held, bf16), shape((cols, head_cols, count), bf16),
+            shape((cols, head_cols, count), bf16),
+            shape((heads, total // SEQ_LEN, 1, SEQ_LEN), f32),
+            shape((total // SEQ_LEN, 1, SEQ_LEN), jnp.int32), shape((cols,) + b_up.shape, bf16),
+        ] + [shape((2, chips, rows) + w.shape, bf16) for w in (w_out, w_up, w_down)],
+        scratch_shapes=[
+            vmem((cols, count, depth), bf16), vmem((depth, 3 * head_cols), bf16),
+            vmem(held, bf16), vmem(held, bf16), vmem(held, bf16),
+            vmem((heads, HD + ONES, total), bf16),
+            vmem((heads, chips, HD + ONES, tile), f32), vmem((heads, chips, 1, tile), f32),
+            vmem((cols, head_cols, count), bf16), vmem((cols,) + blocks.shape, jnp.int32),
+            vmem((cols,) + b_up.shape, bf16),
+            dma((3, chips)), dma((3, chips)), dma((rows,)), dma((rows,)),
+            dma((2, cols)), dma((2, cols)), dma((cols,)), dma((cols,)),
+            dma((3, chips)), dma((3, chips)), dma((3, chips, rows)), dma((3, chips, rows)),
+            dma((3, chips)), dma((3, chips)),
+            dma((cols,)), dma((3, chips)), dma((2, cols)), dma((3,)),
+        ],
+        compiler_params=pltpu.CompilerParams(
+            vmem_limit_bytes=63 << 20, collective_id=0, has_side_effects=True
+        ),
+        cost_estimate=cost(16 * pairs * HD, 16 * heads * total * HD, pairs),
+        name="front",
+    )(tokens, gain, shift, blocks, b_up, w_qkv, b_qv, w_out, w_up, w_down)
+
+
+def tile_mask(blk_ref, key_start, count, query_blocks):
+    key_blocks = jnp.broadcast_to(blk_ref[0, :, pl.ds(key_start, count)], (128, count)).T[:, :1]
+    return query_blocks >= key_blocks
 
 
 GELU_A = 0.7978845608028654
@@ -417,8 +535,8 @@
     chips = cols // 2
     row, col = place()
     chip, lane = col // 2, lax.rem(col, 2)
-    width = up_ref.shape[3]
-    depth = wout_ref.shape[2]
+    width = up_ref.shape[4]
+    depth = wout_ref.shape[3]
 
     def part(r):
         return slice(r * width, (r + 1) * width)
@@ -461,7 +579,13 @@
             heads_all[s * depth : (s + 1) * depth] = heads_ref[s]
         stacked = flip(heads_all[...])
         for r in range(rows):
-            branch = dot(stacked, wout_ref[r].reshape(cols * depth, width))
+            branch = sum(
+                dot(
+                    stacked[:, c * depth : (c + 1) * depth],
+                    wout_ref[c % 2, c // 2, r],
+                )
+                for c in range(cols)
+            )
             resid[:, part(r)] = (
                 tok_ref[:, part(r)].astype(f32) + branch + bout_ref[:, part(r)].astype(f32)
             )
@@ -482,8 +606,8 @@
         up = bup_ref[0].astype(f32)
         d_hidden = 0.0
         for r in range(rows):
-            up = up + dot(x[:, part(r)], up_ref[r, 0], NT)
-            d_hidden = d_hidden + dot(g_ref[:, part(r)], down_ref[r, 0], NT)
+            up = up + dot(x[:, part(r)], up_ref[0, 0, r], NT)
+            d_hidden = d_hidden + dot(g_ref[:, part(r)], down_ref[0, 0, r], NT)
         square = up * up
         bent = jnp.tanh(GELU_A * up * (1.0 + GELU_B * square))
         half = 0.5 + 0.5 * bent
@@ -495,8 +619,8 @@
         hiddens[step] = hidden
         d_ups[step] = d_up
         for r in range(rows):
-            out_acc[:, part(r)] += dot(hidden, down_ref[r, 0])
-            norm_acc[:, part(r)] += dot(d_up, up_ref[r, 0])
+            out_acc[:, part(r)] += dot(hidden, down_ref[0, 0, r])
+            norm_acc[:, part(r)] += dot(d_up, up_ref[0, 0, r])
 
     @pl.when(step == cols - 1)
     def _():
@@ -515,7 +639,7 @@
         for c in range(cols):
             found = 0.0
             for r in range(rows):
-                found = found + dot(wout_ref[r, c], low[:, part(r)], NT)
+                found = found + dot(wout_ref[c % 2, c // 2, r], low[:, part(r)], NT)
             d_send[c] = found.astype(bf16)
         own_d.start()
         d_stage.start()
@@ -581,13 +705,16 @@
 
 def middle(heads, tokens, grad, w_up, w_down, b_up, b_out, gain, shift, b_down, w_out, w_qkv):
     count, depth = tokens.shape
-    rows, cols, units, width = w_up.shape
-    chips = cols // 2
-    head_cols = w_out.shape[2]
+    _, chips, rows, units, width = w_up.shape
+    cols = 2 * chips
+    head_cols = w_out.shape[3]
     any_space = pl.BlockSpec(memory_space=pl.ANY)
-    weight = pl.BlockSpec(
-        (rows, 1, units, width), lambda s: (0, jnp.minimum(s, cols - 1), 0, 0)
-    )
+
+    def weight_map(s):
+        c = jnp.minimum(s, cols - 1)
+        return (lax.rem(c, 2), c // 2, 0, 0, 0)
+
+    weight = pl.BlockSpec((1, 1, rows, units, width), weight_map)
     grad_spec = pl.BlockSpec(
         (rows, 1, units, width), lambda s: (0, jnp.maximum(s - cols - chips, 0), 0, 0)
     )
@@ -1020,17 +1147,12 @@
     return tokens.shape[0]
 
 
-def swap(x, axis, groups=None):
-    return lax.all_to_all(x, axis, 0, 0, tiled=True, axis_index_groups=groups)
-
-
 def body(
     tokens, blocks, w_qkv, b_qv, w_out, b_out, w_up, b_up, w_down, b_down,
     gain1, shift1, gain2, shift2, grad_out,
 ):
     rows, cols = lax.axis_size("row"), lax.axis_size("col")
-    local_rows, depth = tokens.shape
-    group_rows = local_rows * cols
+    depth = tokens.shape[1]
     head_cols = w_qkv.shape[2]
     heads = head_cols // HD
     units = w_up.shape[0]
@@ -1038,24 +1160,15 @@
     def vec(v):
         return v.reshape(1, -1)
 
-    xhat, _ = moments(tokens.astype(f32))
-    attn_input = (xhat * gain1.astype(f32) + shift1.astype(f32)).astype(bf16)
     w_qkv_flat = w_qkv.reshape(w_qkv.shape[0], 3 * head_cols)
 
-    def gather_all(w):
-        return lax.all_gather(w, ("row", "col"), axis=0, tiled=False).reshape(
-            (rows, cols) + w.shape
-        )
-
-    out_weight, up_weight, down_weight = gather_all(w_out), gather_all(w_up), gather_all(w_down)
-
-    attn_rows, block_ids, up_bias, qkv_here = gather_inputs(
-        attn_input, vec(blocks), vec(b_up), w_qkv_flat, rows, cols
-    )
-    block_ids = block_ids.reshape(group_rows // SEQ_LEN, 1, SEQ_LEN)
-    q, k, v = project_qkv(attn_rows.reshape(group_rows, depth), qkv_here, b_qv)
-    found, lse = attend(q, k, v, block_ids, local_rows)
-    arrived = swap(found, "col")
+    (
+        attn_rows, q, k, v, found, arrived, lse, block_ids, up_bias, out_weight, up_weight,
+        down_weight,
+    ) = front(
+        tokens, vec(gain1), vec(shift1), vec(blocks), vec(b_up), w_qkv_flat, b_qv, w_out, w_up,
+        w_down, rows, cols,
+    )
     grad_up, grad_down, grad_wout, grad_bup, output, d_resid, sums, d_heads, qkv_all = middle(
         arrived, tokens, grad_out, up_weight, down_weight, up_bias, vec(b_out), vec(gain2),
         vec(shift2), vec(b_down), out_weight, w_qkv_flat,

time: 516 us -> 462 us (0.90)
  waiting for transfers between devices: 63.1 us -> 0 us
  Pallas kernels: 409 us -> 437 us
  between operations: 13.9 us -> 0.73 us
    all_to_all x1 -> x0, waiting for transfers between devices: 35.3 us -> none  [swap(): return lax.all_to_all(x, axis, 0, 0, tiled=True, axis_index_groups=groups)]
    all_gather x3 -> x0, waiting for transfers between devices: 25.7 us -> none  [gather_all(): lax.all_gather(w, ('row', 'col'), axis=0, tiled=False)]
    pallas_call x3 -> x1, Pallas kernels: 161 us -> 177 us  [front(): pl.pallas_call(functools.partial(front_kernel, rows, cols, heads), in_spe...]
    pallas_call x1, Pallas kernels: 75.2 us -> 88.5 us  [middle(): pl.pallas_call(functools.partial(middle_kernel, rows, cols), grid=(2 * co...]
  transfers between devices with their start and end apart: 4 -> 0, of which waited for: 2 -> 0; matrix products, arithmetic and copies ran while one was open for 2% -> 0% of each run, Pallas kernels for 31% -> 0%
where the time goes in v3:
time: 462 us; the launch traced here: 461 us
  Pallas kernels  437 us (95%)
  local copies, waits for them, and re-layouts  21.3 us (5%)
    pallas_call x1, Pallas kernels, front(): pl.pallas_call(functools.partial(front_kernel, rows, cols, heads), in_spe...  177 us
    pallas_call x1, Pallas kernels, backward(): pl.pallas_call(functools.partial(back_kernel, rows, cols, heads, seqs, ti...  172 us
    pallas_call x1, Pallas kernels, middle(): pl.pallas_call(functools.partial(middle_kernel, rows, cols), grid=(2 * co...  88.5 us

profile of v3, /device:TPU:0, one launch (start us, length us, event | category | flops | bytes accessed | tf_op | source)
XLA Modules:
  0.0 460.9 jit_solution(4521443277855259112)
XLA Ops:
  0.6 1.1 copy.32
  1.7 0.8 copy.33.wq_ref
  2.5 1.3 reshape.71.gain_ref
  3.8 1.3 reshape.72.shift_ref
  5.1 1.3 reshape.74.bup_ref
  6.4 176.9 %front.1 = (bf16[8,512,1024]{2,1,0:T(8,128)(2,1)}, bf16[2,4096,64]{2,1,0:T(8,128)(2,1)}, bf16[2,4096,64]{2,1,0:T(8,128)(2,1)}, bf16[2,4096,64]{2,1,0:T(8,128)(2,...) custom-call(bf16[512,1024]{1,0:T(8,128)(2,1)} %tok_ref.5, ...), custom_call_target="tpu_custom_call" | custom-call | flops 21474836480 | bytes 8388608 | tf_op jit(solution)/shard_map/front/pallas_call | solution.py:483
  183.2 0.6 reshape.76.bout_ref
  183.8 0.6 reshape.77.gain_ref
  185.6 88.5 %middle.1 = (bf16[4,4,512,256]{3,2,1,0:T(8,128)(2,1)}, bf16[4,4,512,256]{3,2,1,0:T(8,128)(2,1)}, bf16[4,4,128,256]{3,2,1,0:T(8,128)(2,1)}, f32[8,1,512]{2,1,0:T(...) custom-call(bf16[8,128,512]{2,1,0:T(8,128)(2,1)} %get-tuple-element., ...), custom_call_target="tpu_custom_call" | custom-call | flops 25769803776 | bytes 41943040 | tf_op jit(solution)/shard_map/middle/pallas_call | solution.py:726
  274.2 0.8 reduce
  274.9 0.8 slice.17
  275.8 0.7 maximum_maximum_fusion.early_ref
  276.5 172.1 %backward.1 = (f32[512,1024]{1,0:T(8,128)}, f32[512,256]{1,0:T(8,128)}, f32[512,256]{1,0:T(8,128)}, f32[128,256]{1,0:T(8,128)}, f32[384,256]{1,0:T(8,128)}, /*index=5*/f32[16,1024]{1,0:T(8,128)}, f32[2,64,128]{2,1,0:T(8,128)}) custom-call(s32[1,1,4096]{2,1,0:T(1,128)} %get-tuple-element.48.blk_ref, bf16[2,4096,64]{2,1,0:T(8,128)(2,1)} %get-tuple-element.49.q_ref, ...), custom_call_target="tpu_custom_call" | custom-call | flops 53687091200 | bytes 8388608 | tf_op jit(solution)/shard_map/backward/pallas_call | solution.py:1096
  448.6 1.2 copy.35
  449.8 0.9 copy.37
  450.7 0.8 slice_bitcast_fusion
  451.4 0.7 dynamic_slice.3
  452.1 1.5 fusion
  453.6 1.5 copy.36
  455.1 2.3 copy.46
  457.4 1.3 copy.47
  458.7 0.7 copy.48
  459.4 0.8 copy.49
  460.1 0.8 copy.50
  (22 shorter events, 1.3 us)
Async XLA Ops:
  6.3 176.9 %copy-start.4 = (bf16[1024]{0:T(1024)(128)(2,1)S(1)}, bf16[1024]{0:T(1024)(128)(2,1)}, u32[]{:S(2)}) copy-start(bf16[1024]{0:T(1024)(128)(2,1)} %param.20) | copy-start | bytes 6148
  6.3 177.5 %copy-start.5 = (bf16[1024]{0:T(1024)(128)(2,1)S(1)}, bf16[1024]{0:T(1024)(128)(2,1)}, u32[]{:S(2)}) copy-start(bf16[1024]{0:T(1024)(128)(2,1)} %param.27) | copy-start | bytes 6148
  6.3 178.1 %copy-start.6 = (bf16[1024]{0:T(1024)(128)(2,1)S(1)}, bf16[1024]{0:T(1024)(128)(2,1)}, u32[]{:S(2)}) copy-start(bf16[1024]{0:T(1024)(128)(2,1)} %param.28) | copy-start | bytes 6148
  6.3 178.7 %copy-start.7 = (bf16[1024]{0:T(1024)(128)(2,1)S(1)}, bf16[1024]{0:T(1024)(128)(2,1)}, u32[]{:S(2)}) copy-start(bf16[1024]{0:T(1024)(128)(2,1)} %param.24) | copy-start | bytes 6148
  448.6 8.8 %copy-start = (f32[512,1024]{1,0:T(8,128)S(1)}, f32[512,1024]{1,0:T(8,128)}, u32[]{:S(2)}) copy-start(f32[512,1024]{1,0:T(8,128)} %get-tuple-element.105) | copy-start | bytes 6291460
  457.4 1.3 copy-start.3
  457.4 2.0 copy-start.2
  457.4 2.8 copy-start.1

commit v4 on v3

--- a/solution.py
+++ b/solution.py
@@ -150,7 +150,7 @@
 
 def front_kernel(
     rows, cols, heads,
-    tok_ref, gain_ref, shift_ref, blk_ref, bup_ref, wq_ref, bias_ref, wout_ref, wup_ref, wdown_ref,
+    tok_ref, vec_ref, blk_ref, bup_ref, wq_ref, bias_ref, wout_ref, wup_ref, wdown_ref,
     xo_ref, q_ref, k_ref, v_ref, found_ref, arrived_ref, lse_ref, blko_ref, bupo_ref,
     wouto_ref, wupo_ref, wdowno_ref,
     xs, wqs, qs, ks, vs, vt, totals, tops, founds, blks, bups,
@@ -167,7 +167,7 @@
     width = heads * HD
 
     xhat, _ = moments(tok_ref[...].astype(f32))
-    xs[me] = (xhat * gain_ref[...].astype(f32) + shift_ref[...].astype(f32)).astype(bf16)
+    xs[me] = (xhat * vec_ref[0:1] + vec_ref[1:2]).astype(bf16)
     blks[me] = blk_ref[...]
     bups[me] = bup_ref[...]
     own_rows = pl.ds(pl.multiple_of(row * depth, depth), depth)
@@ -200,10 +200,11 @@
     f_stage_out = lambda at: founds.at[at]
     f_stage = over_col(cols, f_stage_out, lambda at: arrived_ref.at[at], send_f, recv_f)
 
-    def w_line(n):
-        return over_line(
-            chips, lambda at: given[n], lambda at: gathered[n].at[lane, at, row], send_wz.at[n],
-            recv_wz.at[n],
+    def w_line(n, at, to, route):
+        block = gathered[n].at[lane, at, row]
+        out = given[n] if at is chip else block
+        return remote(
+            out, block, send_wz.at[n, route, at], recv_wz.at[n, at], (row, to * 2 + lane)
         )
 
     def w_row(n, c, out):
@@ -212,6 +213,44 @@
             recv_wr.at[n, c],
         )
 
+    square = rows == 4
+    next_x = row + 1 - 2 * lax.rem(row, 2)
+    next_y = lax.rem(row + 2, 4)
+    across_x = lax.rem(next_x + 2, 4)
+    relayed = jnp.where(lane == 0, next_y, next_x)
+    relay_to = jnp.where(lane == 0, next_x, next_y)
+
+    def w_step(n, c, slot, k, to):
+        block = gathered[n].at[lane, c, slot]
+        out = given[n] if (slot is row and c is chip) else block
+        return remote(out, block, send_wr.at[n, c, k], recv_wr.at[n, c, slot], (to, me))
+
+    def rows_start(n, c):
+        if square:
+            w_step(n, c, row, 0, next_x).start()
+            w_step(n, c, row, 1, next_y).start()
+        else:
+            w_row(n, c, given[n] if c is chip else gathered[n].at[lane, c, row]).start()
+
+    def rows_relay(n, c):
+        if square:
+            w_step(n, c, relayed, 2, relay_to).wait_recv()
+            w_step(n, c, relayed, 2, relay_to).start()
+
+    def rows_wait_recv(n, c):
+        if square:
+            w_step(n, c, relay_to, 0, next_x).wait_recv()
+            w_step(n, c, across_x, 0, next_x).wait_recv()
+        else:
+            w_row(n, c, given[n]).wait_recv()
+
+    def rows_wait_send(n, c):
+        if square:
+            for k in range(3):
+                w_step(n, c, row, k, next_x).wait_send()
+        else:
+            w_row(n, c, given[n]).wait_send()
+
     def w_own(n):
         return pltpu.make_async_copy(given[n], gathered[n].at[lane, chip, row], local_w.at[n])
 
@@ -219,23 +258,26 @@
         block = gathered[n].at[side, c]
         return remote(block, block, send_wm.at[n, c], recv_wm.at[n, c], mate())
 
+    to_mate(me, chip).start()
     q_stage.start()
     for exchange in small:
         exchange.start()
 
     @pl.when(chip + 1 < chips)
     def _():
+        for n in range(3):
+            w_line(n, chip, chip + 1, 0).start()
         chunk(me, me + 2, 0, chip).start()
 
     @pl.when(chip > 0)
     def _():
+        for n in range(3):
+            w_line(n, chip, chip - 1, 1).start()
         chunk(me, me - 2, 1, chip).start()
 
-    to_mate(me, chip).start()
     for n in range(3):
         w_own(n).start()
-        w_row(n, chip, given[n]).start()
-        w_line(n).start()
+        rows_start(n, chip)
     q_stage.wait_recv()
     for exchange in small:
         exchange.wait_recv()
@@ -324,11 +366,43 @@
             def _():
                 f_stage.copy(lax.rem(owner - me + cols, cols)).start()
 
+    def pass_weights():
+        for n in range(3):
+            w_own(n).wait()
+
+            def across(c, carry):
+                rows_wait_recv(n, c)
+                w_mate(n, c, lane).start()
+                return carry
+
+            lax.fori_loop(0, chips, across, 0)
+
     def event(e, carry):
         hop = (e + 1) // 2
         lower = lax.rem(e, 2) == 1
         p = jnp.where(lower, chip - hop, chip + hop)
 
+        @pl.when(e == 1)
+        def _():
+            for hop in range(1, chips):
+                for at, step, route in ((chip - hop, 1, 0), (chip + hop, -1, 1)):
+
+                    @pl.when((at >= 0) & (at < chips))
+                    def _():
+                        onward = chip + step
+                        for n in range(3):
+                            w_line(n, at, onward, route).wait_recv()
+
+                            @pl.when((onward >= 0) & (onward < chips))
+                            def _():
+                                w_line(n, at, onward, route).start()
+
+                            rows_start(n, at)
+
+        @pl.when(e == 2 * chips - 3)
+        def _():
+            pass_weights()
+
         @pl.when(lower)
         def _():
             below, above = chip - hop, chip + hop
@@ -355,24 +429,14 @@
 
                 to_mate(owner, above).start()
 
-        @pl.when(e == min(3, 2 * chips - 3))
+        @pl.when(e == 1)
         def _():
-            for n in range(3):
-                w_line(n).wait_recv()
-
-                def onward(k, carry):
-                    c = lax.rem(chip + k, chips)
-                    w_row(n, c, gathered[n].at[lane, c, row]).start()
-                    return carry
-
-                lax.fori_loop(1, chips, onward, 0)
-
-        @pl.when(e == 2 * chips - 3)
-        def _():
-            for n in range(3):
-                w_own(n).wait()
-                w_row(n, chip, given[n]).wait_recv()
-                w_mate(n, chip, lane).start()
+            def relay(c, carry):
+                for n in range(3):
+                    rows_relay(n, c)
+                return carry
+
+            lax.fori_loop(0, chips, relay, 0)
 
         @pl.when((p >= 0) & (p < chips))
         def _():
@@ -394,6 +458,14 @@
             def _():
                 conclude(p)
 
+            @pl.when(jnp.logical_not(lower) & (p > first) & (hop > 0))
+            def _():
+                boundary(p - 1)
+
+                @pl.when(low == first)
+                def _():
+                    conclude(p - 1)
+
             amount = jnp.where(lower, high - p, p - low)
 
             def pair(j, carry):
@@ -410,14 +482,6 @@
 
             lax.fori_loop(0, amount, pair, 0)
 
-            @pl.when(jnp.logical_not(lower) & (p > first) & (hop > 0))
-            def _():
-                boundary(p - 1)
-
-                @pl.when(low == first)
-                def _():
-                    conclude(p - 1)
-
             @pl.when(jnp.logical_not(lower) & (p == final) & (low == first))
             def _():
                 conclude(p)
@@ -426,15 +490,6 @@
 
     lax.fori_loop(0, 2 * chips - 1, event, 0)
 
-    for n in range(3):
-
-        def across(k, carry):
-            c = lax.rem(chip + k, chips)
-            w_row(n, c, given[n]).wait_recv()
-            w_mate(n, c, lane).start()
-            return carry
-
-        lax.fori_loop(1, chips, across, 0)
     for c in range(cols):
         bupo_ref[c] = bups[c]
         at = c * count
@@ -444,7 +499,16 @@
         for n in range(3):
             w_mate(n, c, 1 - lane).wait_recv()
             w_mate(n, c, lane).wait_send()
-            w_row(n, c, given[n]).wait_send()
+            rows_wait_send(n, c)
+
+            @pl.when((c <= chip) & (chip + 1 < chips))
+            def _():
+                w_line(n, c, chip, 0).wait_send()
+
+            @pl.when((c >= chip) & (chip > 0))
+            def _():
+                w_line(n, c, chip, 1).wait_send()
+
         for copy in keep(c):
             copy.wait()
         kept(2 * c).wait()
@@ -460,15 +524,13 @@
             chunk(me, me, 1, c).wait_send()
 
     own(me).wait()
-    for n in range(3):
-        w_line(n).wait_send()
     f_stage.wait_send()
     q_stage.wait_send()
     for exchange in small:
         exchange.wait_send()
 
 
-def front(tokens, gain, shift, blocks, b_up, w_qkv, b_qv, w_out, w_up, w_down, rows, cols):
+def front(tokens, vecs, blocks, b_up, w_qkv, b_qv, w_out, w_up, w_down, rows, cols):
     count, depth = tokens.shape
     head_cols = w_qkv.shape[1] // 3
     heads = head_cols // HD
@@ -482,7 +544,7 @@
     held = (heads, total, HD)
     return pl.pallas_call(
         functools.partial(front_kernel, rows, cols, heads),
-        in_specs=[in_vmem] * 10,
+        in_specs=[in_vmem] * 9,
         out_specs=[any_space] * 6 + [in_vmem] * 3 + [any_space] * 3,
         out_shape=[
             shape((cols, count, depth), bf16), shape(held, bf16), shape(held, bf16),
@@ -500,7 +562,7 @@
             vmem((cols,) + b_up.shape, bf16),
             dma((3, chips)), dma((3, chips)), dma((rows,)), dma((rows,)),
             dma((2, cols)), dma((2, cols)), dma((cols,)), dma((cols,)),
-            dma((3, chips)), dma((3, chips)), dma((3, chips, rows)), dma((3, chips, rows)),
+            dma((3, 2, chips)), dma((3, chips)), dma((3, chips, rows)), dma((3, chips, rows)),
             dma((3, chips)), dma((3, chips)),
             dma((cols,)), dma((3, chips)), dma((2, cols)), dma((3,)),
         ],
@@ -509,7 +571,7 @@
         ),
         cost_estimate=cost(16 * pairs * HD, 16 * heads * total * HD, pairs),
         name="front",
-    )(tokens, gain, shift, blocks, b_up, w_qkv, b_qv, w_out, w_up, w_down)
+    )(tokens, vecs, blocks, b_up, w_qkv, b_qv, w_out, w_up, w_down)
 
 
 def tile_mask(blk_ref, key_start, count, query_blocks):
@@ -523,8 +585,7 @@
 
 def middle_kernel(
     rows, cols,
-    heads_ref, tok_ref, g_ref, up_ref, down_ref, bup_ref, bout_ref, gain_ref, shift_ref, bdown_ref,
-    wout_ref, wq_ref,
+    heads_ref, tok_ref, g_ref, up_ref, down_ref, bup_ref, vec_ref, wout_ref, wq_ref,
     gup_ref, gdown_ref, gout_ref, gbup_ref, output_ref, dres_ref, sums_ref, dheads_ref, wqo_ref,
     x, heads_all, resid, out_acc, norm_acc, hiddens, d_ups, low, d_send,
     mine, other, out_mine, out_other,
@@ -541,6 +602,9 @@
     def part(r):
         return slice(r * width, (r + 1) * width)
 
+    def out_weight(r):
+        return jnp.concatenate([wout_ref[c % 2, c // 2, r] for c in range(cols)], axis=0)
+
     z_stage = over_line(
         chips, lambda at: wq_ref, lambda at: wqo_ref.at[lane, row, at], send_z, recv_z
     )
@@ -579,18 +643,10 @@
             heads_all[s * depth : (s + 1) * depth] = heads_ref[s]
         stacked = flip(heads_all[...])
         for r in range(rows):
-            branch = sum(
-                dot(
-                    stacked[:, c * depth : (c + 1) * depth],
-                    wout_ref[c % 2, c // 2, r],
-                )
-                for c in range(cols)
-            )
-            resid[:, part(r)] = (
-                tok_ref[:, part(r)].astype(f32) + branch + bout_ref[:, part(r)].astype(f32)
-            )
+            branch = dot(stacked, out_weight(r))
+            resid[:, part(r)] = tok_ref[:, part(r)].astype(f32) + branch + vec_ref[2:3, part(r)]
         xhat, _ = moments(resid[...])
-        x[...] = (xhat * gain_ref[...].astype(f32) + shift_ref[...].astype(f32)).astype(bf16)
+        x[...] = (xhat * vec_ref[3:4] + vec_ref[4:5]).astype(bf16)
         out_acc[...] = jnp.zeros_like(out_acc)
         norm_acc[...] = jnp.zeros_like(norm_acc)
 
@@ -624,11 +680,11 @@
 
     @pl.when(step == cols - 1)
     def _():
-        output_ref[...] = (resid[...] + out_acc[...] + bdown_ref[...].astype(f32)).astype(bf16)
+        output_ref[...] = (resid[...] + out_acc[...] + vec_ref[5:6]).astype(bf16)
         xhat, inv = moments(resid[...])
         d_norm = norm_acc[...]
         grad = g_ref[...].astype(f32)
-        d_resid = grad + norm_back(xhat, inv, d_norm * gain_ref[...].astype(f32))
+        d_resid = grad + norm_back(xhat, inv, d_norm * vec_ref[3:4])
         dres_ref[...] = d_resid
         low[...] = d_resid.astype(bf16)
         sums_ref[0:1] = jnp.sum(grad, axis=0, keepdims=True)
@@ -636,11 +692,12 @@
         sums_ref[2:3] = jnp.sum(d_norm, axis=0, keepdims=True)
         sums_ref[3:4] = jnp.sum(d_resid, axis=0, keepdims=True)
         sums_ref[4:] = jnp.zeros((4, sums_ref.shape[1]), f32)
+        found = 0.0
+        for r in range(rows):
+            found = found + dot(out_weight(r), low[:, part(r)], NT)
+        found = found.astype(bf16)
         for c in range(cols):
-            found = 0.0
-            for r in range(rows):
-                found = found + dot(wout_ref[c % 2, c // 2, r], low[:, part(r)], NT)
-            d_send[c] = found.astype(bf16)
+            d_send[c] = found[c * depth : (c + 1) * depth]
         own_d.start()
         d_stage.start()
         found = dot(heads_all[...], low[...])
@@ -703,7 +760,7 @@
         own_d.wait()
 
 
-def middle(heads, tokens, grad, w_up, w_down, b_up, b_out, gain, shift, b_down, w_out, w_qkv):
+def middle(heads, tokens, grad, w_up, w_down, b_up, vecs, w_out, w_qkv):
     count, depth = tokens.shape
     _, chips, rows, units, width = w_up.shape
     cols = 2 * chips
@@ -720,14 +777,14 @@
     )
     grad_shape = jax.ShapeDtypeStruct((rows, chips, units, width), bf16)
     bias = pl.BlockSpec((1, 1, units), lambda s: (jnp.minimum(s, cols - 1), 0, 0))
-    block, vec = whole((count, depth)), whole((1, depth))
+    block = whole((count, depth))
     dma = pltpu.SemaphoreType.DMA
     vmem = pltpu.VMEM
     return pl.pallas_call(
         functools.partial(middle_kernel, rows, cols),
         grid=(2 * cols,),
         in_specs=[
-            whole(heads.shape), block, block, weight, weight, bias, vec, vec, vec, vec,
+            whole(heads.shape), block, block, weight, weight, bias, whole(vecs.shape),
             whole(w_out.shape), any_space,
         ],
         out_specs=[
@@ -762,12 +819,12 @@
             12 * count * depth * cols * units, 8 * depth * cols * units + 16 * count * depth
         ),
         name="middle",
-    )(heads, tokens, grad, w_up, w_down, b_up, b_out, gain, shift, b_down, w_out, w_qkv)
+    )(heads, tokens, grad, w_up, w_down, b_up, vecs, w_out, w_qkv)
 
 
 def back_kernel(
     rows, cols, heads, seqs, tiles, sub,
-    blk_ref, q_ref, k_ref, v_ref, do_ref, o_ref, lse_ref, x_ref, w_ref, tok_ref, dres_ref, gain_ref,
+    blk_ref, q_ref, k_ref, v_ref, do_ref, o_ref, lse_ref, x_ref, w_ref, tok_ref, dres_ref, vec_ref,
     gup_ref, gdown_ref, gout_ref, early_ref,
     dtok_ref, wup_ref, wdown_ref, wout_ref, wqkv_ref, all_ref, bias_ref,
     d_mixed, d_arrived, key_grad, value_grad, bias_sum, qkv_acc, qkv_send, qkv_recv, norm_acc,
@@ -1010,7 +1067,7 @@
         small[0, late : late + 1] = jnp.sum(d_norm * xhat, axis=0, keepdims=True)
         small[0, late + 1 : late + 2] = jnp.sum(d_norm, axis=0, keepdims=True)
         s_core.start()
-        dtok_ref[...] = dres_ref[...] + norm_back(xhat, inv, d_norm * gain_ref[...].astype(f32))
+        dtok_ref[...] = dres_ref[...] + norm_back(xhat, inv, d_norm * vec_ref[0:1])
         s_core.wait_recv()
         small[1] = small[0] + small_core[...]
         small_row[row] = small[1]
@@ -1047,7 +1104,7 @@
 
 
 def backward(
-    blocks, q, k, v, d_heads, out, lse, x, w_qkv, tokens, d_resid, gain, grad_up, grad_down,
+    blocks, q, k, v, d_heads, out, lse, x, w_qkv, tokens, d_resid, vecs, grad_up, grad_down,
     grad_out, early,
 ):
     heads, total, _ = q.shape
@@ -1102,7 +1159,7 @@
             pl.BlockSpec((1, 1, 1, tile), lse_map),
             pl.BlockSpec((1, count, depth), lambda s: (jnp.clip(s - work, 0, cols - 1), 0, 0)),
             pl.BlockSpec((1, rows, 1) + w_qkv.shape[3:], w_map),
-            block, block, whole((1, depth)), any_space, any_space, any_space, whole(small),
+            block, block, whole(vecs.shape), any_space, any_space, any_space, whole(small),
         ],
         out_specs=[
             block, whole((units, width)), whole((units, width)), whole((head_cols, width)),
@@ -1138,7 +1195,7 @@
         cost_estimate=cost(40 * pairs * HD, 16 * heads * total * HD, pairs),
         name="backward",
     )(
-        blocks, q, k, v, d_heads, out, lse, x, w_qkv, tokens, d_resid, gain, grad_up, grad_down,
+        blocks, q, k, v, d_heads, out, lse, x, w_qkv, tokens, d_resid, vecs, grad_up, grad_down,
         grad_out, early,
     )
 
@@ -1160,18 +1217,18 @@
     def vec(v):
         return v.reshape(1, -1)
 
+    vecs = jnp.stack([gain1, shift1, b_out, gain2, shift2, b_down] + [gain1] * 2).astype(f32)
     w_qkv_flat = w_qkv.reshape(w_qkv.shape[0], 3 * head_cols)
 
     (
         attn_rows, q, k, v, found, arrived, lse, block_ids, up_bias, out_weight, up_weight,
         down_weight,
     ) = front(
-        tokens, vec(gain1), vec(shift1), vec(blocks), vec(b_up), w_qkv_flat, b_qv, w_out, w_up,
+        tokens, vecs, vec(blocks), vec(b_up), w_qkv_flat, b_qv, w_out, w_up,
         w_down, rows, cols,
     )
     grad_up, grad_down, grad_wout, grad_bup, output, d_resid, sums, d_heads, qkv_all = middle(
-        arrived, tokens, grad_out, up_weight, down_weight, up_bias, vec(b_out), vec(gain2),
-        vec(shift2), vec(b_down), out_weight, w_qkv_flat,
+        arrived, tokens, grad_out, up_weight, down_weight, up_bias, vecs, out_weight, w_qkv_flat,
     )
     hidden_units = units * cols
     used = 4 + hidden_units // depth
@@ -1180,7 +1237,7 @@
         [sums[:4], grad_bup.reshape(-1, depth), jnp.zeros((spare, depth), f32)]
     )
     grad_tokens, grad_wup, grad_wdown, grad_wout, grad_wqkv, small, bias = backward(
-        block_ids, q, k, v, d_heads, found, lse, attn_rows, qkv_all, tokens, d_resid, vec(gain1),
+        block_ids, q, k, v, d_heads, found, lse, attn_rows, qkv_all, tokens, d_resid, vecs,
         grad_up, grad_down, grad_wout, early,
     )
     grad_wqkv = (

time: 462 us -> 428 us (0.926)
  Pallas kernels: 437 us -> 404 us
    pallas_call x1, Pallas kernels: 177 us -> 153 us  [front(): pl.pallas_call(functools.partial(front_kernel, rows, cols, heads), in_spe...]
    pallas_call x1, Pallas kernels: 88.5 us -> 76.5 us  [middle(): pl.pallas_call(functools.partial(middle_kernel, rows, cols), grid=(2 * co...]
    reshape x7 -> x1, local copies, waits for them, and re-layouts: 6.2 us -> 1.26 us  [vec(): return v.reshape(1, -1)]
where the time goes in v4:
time: 428 us; the launch traced here: 427 us
  Pallas kernels  404 us (94%)
  local copies, waits for them, and re-layouts  20.5 us (5%)
    pallas_call x1, Pallas kernels, backward(): pl.pallas_call(functools.partial(back_kernel, rows, cols, heads, seqs, ti...  174 us
    pallas_call x1, Pallas kernels, front(): pl.pallas_call(functools.partial(front_kernel, rows, cols, heads), in_spe...  153 us
    pallas_call x1, Pallas kernels, middle(): pl.pallas_call(functools.partial(middle_kernel, rows, cols), grid=(2 * co...  76.5 us
    unnamed x17, local copies, waits for them, and re-layouts  8.58 us

profile of v4, /device:TPU:0, one launch (start us, length us, event | category | flops | bytes accessed | tf_op | source)
XLA Modules:
  0.0 427.2 jit_solution(7513851474753098111)
XLA Ops:
  0.6 0.7 stack.23
  1.3 0.7 stack.24
  2.0 0.7 stack.25
  2.7 0.7 stack.26
  3.4 0.7 stack.27
  4.1 0.7 stack.28
  5.4 1.1 copy.32
  6.5 0.8 copy.33.wq_ref
  7.3 1.3 reshape.53.bup_ref
  8.6 153.1 %front.1 = (bf16[8,512,1024]{2,1,0:T(8,128)(2,1)}, bf16[2,4096,64]{2,1,0:T(8,128)(2,1)}, bf16[2,4096,64]{2,1,0:T(8,128)(2,1)}, bf16[2,4096,64]{2,1,0:T(8,128)(2,...) custom-call(bf16[512,1024]{1,0:T(8,128)(2,1)} %tok_ref.5, ...), custom_call_target="tpu_custom_call" | custom-call | flops 21474836480 | bytes 8388608 | tf_op jit(solution)/shard_map/front/pallas_call | solution.py:545
  161.7 76.5 %middle.1 = (bf16[4,4,512,256]{3,2,1,0:T(8,128)(2,1)}, bf16[4,4,512,256]{3,2,1,0:T(8,128)(2,1)}, bf16[4,4,128,256]{3,2,1,0:T(8,128)(2,1)}, f32[8,1,512]{2,1,0:T(...) custom-call(bf16[8,128,512]{2,1,0:T(8,128)(2,1)} %get-tuple-element., ...), custom_call_target="tpu_custom_call" | custom-call | flops 25769803776 | bytes 41943040 | tf_op jit(solution)/shard_map/middle/pallas_call | solution.py:783
  238.3 0.8 reduce
  239.1 0.8 slice.17
  239.9 0.7 maximum_maximum_fusion.early_ref
  240.6 174.2 %backward.1 = (f32[512,1024]{1,0:T(8,128)}, f32[512,256]{1,0:T(8,128)}, f32[512,256]{1,0:T(8,128)}, f32[128,256]{1,0:T(8,128)}, f32[384,256]{1,0:T(8,128)}, /*index=5*/f32[16,1024]{1,0:T(8,128)}, f32[2,64,128]{2,1,0:T(8,128)}) custom-call(s32[1,1,4096]{2,1,0:T(1,128)} %get-tuple-element.48.blk_ref, bf16[2,4096,64]{2,1,0:T(8,128)(2,1)} %get-tuple-element.49.q_ref, ...), custom_call_target="tpu_custom_call" | custom-call | flops 53687091200 | bytes 8388608 | tf_op jit(solution)/shard_map/backward/pallas_call | solution.py:1153
  414.8 1.2 copy.35
  416.0 0.9 copy.37
  416.9 0.8 slice_bitcast_fusion
  418.3 1.5 fusion
  419.9 1.5 copy.36
  421.3 2.3 copy.46
  423.6 1.3 copy.47
  425.6 0.8 copy.49
  426.4 0.8 copy.50
  (16 shorter events, 2.1 us)
Async XLA Ops:
  414.8 8.8 %copy-start = (f32[512,1024]{1,0:T(8,128)S(1)}, f32[512,1024]{1,0:T(8,128)}, u32[]{:S(2)}) copy-start(f32[512,1024]{1,0:T(8,128)} %get-tuple-element.105) | copy-start | bytes 6291460
  423.6 1.3 copy-start.3
  423.6 2.0 copy-start.2
  423.6 2.8 copy-start.1

commit v5 on v4

--- a/solution.py
+++ b/solution.py
@@ -141,6 +141,17 @@
     chip, lane = col // 2, lax.rem(col, 2)
     slot = lambda k: lax.rem(chip + k, chips)
     return Exchange(chips, chip, slot, lambda k: (row, slot(k) * 2 + lane), out, into, send, recv)
+
+
+class Plane:
+    def __init__(self):
+        row, col = place()
+        lane = lax.rem(col, 2)
+        self.next_x = row + 1 - 2 * lax.rem(row, 2)
+        self.next_y = lax.rem(row + 2, 4)
+        self.across = lax.rem(self.next_x + 2, 4)
+        self.first = jnp.where(lane == 0, self.next_y, self.next_x)
+        self.second = jnp.where(lane == 0, self.next_x, self.next_y)
 
 
 def mate():
@@ -214,11 +225,9 @@
         )
 
     square = rows == 4
-    next_x = row + 1 - 2 * lax.rem(row, 2)
-    next_y = lax.rem(row + 2, 4)
-    across_x = lax.rem(next_x + 2, 4)
-    relayed = jnp.where(lane == 0, next_y, next_x)
-    relay_to = jnp.where(lane == 0, next_x, next_y)
+    plane = Plane()
+    next_x, next_y, across_x = plane.next_x, plane.next_y, plane.across
+    relayed, relay_to = plane.first, plane.second
 
     def w_step(n, c, slot, k, to):
         block = gathered[n].at[lane, c, slot]
@@ -586,7 +595,7 @@
 def middle_kernel(
     rows, cols,
     heads_ref, tok_ref, g_ref, up_ref, down_ref, bup_ref, vec_ref, wout_ref, wq_ref,
-    gup_ref, gdown_ref, gout_ref, gbup_ref, output_ref, dres_ref, sums_ref, dheads_ref, wqo_ref,
+    gup_ref, gdown_ref, gout_ref, output_ref, dres_ref, sums_ref, dheads_ref, wqo_ref,
     x, heads_all, resid, out_acc, norm_acc, hiddens, d_ups, low, d_send,
     mine, other, out_mine, out_other,
     send_d, recv_d, send_p, recv_p, send_o, recv_o, send_z, recv_z, send_r, recv_r, send_m, recv_m,
@@ -670,7 +679,10 @@
         hidden = (up * half).astype(bf16)
         slope = half + (0.5 * GELU_A) * up * (1.0 - bent * bent) * (1.0 + (3.0 * GELU_B) * square)
         d_up = d_hidden * slope
-        gbup_ref[0] = jnp.sum(d_up, axis=0, keepdims=True)
+        units = d_up.shape[1]
+        per = sums_ref.shape[1] // units
+        lanes = pl.ds(pl.multiple_of(lax.rem(step, per) * units, units), units)
+        sums_ref[pl.ds(4 + step // per, 1), lanes] = jnp.sum(d_up, axis=0, keepdims=True)
         d_up = d_up.astype(bf16)
         hiddens[step] = hidden
         d_ups[step] = d_up
@@ -691,7 +703,6 @@
         sums_ref[1:2] = jnp.sum(d_norm * xhat, axis=0, keepdims=True)
         sums_ref[2:3] = jnp.sum(d_norm, axis=0, keepdims=True)
         sums_ref[3:4] = jnp.sum(d_resid, axis=0, keepdims=True)
-        sums_ref[4:] = jnp.zeros((4, sums_ref.shape[1]), f32)
         found = 0.0
         for r in range(rows):
             found = found + dot(out_weight(r), low[:, part(r)], NT)
@@ -765,6 +776,7 @@
     _, chips, rows, units, width = w_up.shape
     cols = 2 * chips
     head_cols = w_out.shape[3]
+    sum_rows = 4 + cols * units // depth
     any_space = pl.BlockSpec(memory_space=pl.ANY)
 
     def weight_map(s):
@@ -788,16 +800,15 @@
             whole(w_out.shape), any_space,
         ],
         out_specs=[
-            grad_spec, grad_spec, whole((rows, chips, head_cols, width)), bias, block, block,
-            whole((8, depth)), any_space, any_space,
+            grad_spec, grad_spec, whole((rows, chips, head_cols, width)), block, block,
+            whole((sum_rows, depth)), any_space, any_space,
         ],
         out_shape=[
             grad_shape, grad_shape,
             jax.ShapeDtypeStruct((rows, chips, head_cols, width), bf16),
-            jax.ShapeDtypeStruct((cols, 1, units), f32),
             jax.ShapeDtypeStruct((count, depth), bf16),
             jax.ShapeDtypeStruct((count, depth), f32),
-            jax.ShapeDtypeStruct((8, depth), f32),
+            jax.ShapeDtypeStruct((sum_rows, depth), f32),
             jax.ShapeDtypeStruct((cols, head_cols, count), bf16),
             jax.ShapeDtypeStruct((2, rows, chips) + w_qkv.shape, bf16),
         ],
@@ -822,24 +833,224 @@
     )(heads, tokens, grad, w_up, w_down, b_up, vecs, w_out, w_qkv)
 
 
+class SmallSum:
+    def __init__(self, rows, chips, scratch):
+        row, col = place()
+        self.rows, self.chips, self.row, self.chip = rows, chips, row, col // 2
+        self.held, self.core, self.by_row, self.by_line, *sems = scratch
+        held = self.held
+        self.stages = [
+            remote(held.at[0], self.core, sems[0], sems[1], mate()),
+            over_row(
+                rows, lambda at: held.at[1], lambda at: self.by_row.at[at], sems[2], sems[3]
+            ),
+            over_line(
+                chips, lambda at: held.at[2], lambda at: self.by_line.at[at], sems[4], sems[5]
+            ),
+        ]
+
+    def first(self, value):
+        self.held[0] = value
+        self.stages[0].start()
+
+    def second(self):
+        self.stages[0].wait_recv()
+        value = self.held[0] + self.core[...]
+        self.held[1] = value
+        self.by_row[self.row] = value
+        self.stages[1].start()
+
+    def third(self):
+        self.stages[1].wait_recv()
+        value = sum(self.by_row[r] for r in range(1, self.rows)) + self.by_row[0]
+        self.held[2] = value
+        self.by_line[self.chip] = value
+        self.stages[2].start()
+
+    def result(self):
+        self.stages[2].wait_recv()
+        return sum(self.by_line[c] for c in range(1, self.chips)) + self.by_line[0]
+
+    def wait_send(self):
+        for stage in self.stages:
+            stage.wait_send()
+
+
+def sum_scratch(rows, chips, shapes):
+    dma, vmem = pltpu.SemaphoreType.DMA, pltpu.VMEM
+    found = []
+    for shape in shapes:
+        found += [
+            vmem((3,) + shape, f32), vmem(shape, f32), vmem((rows,) + shape, f32),
+            vmem((chips,) + shape, f32), dma, dma, dma((rows,)), dma((rows,)), dma((chips,)),
+            dma((chips,)),
+        ]
+    return found
+
+
+SUM_REFS = 10
+
+
+def add_into(into, other):
+    into[...] = (into[...].astype(f32) + other[...].astype(f32)).astype(bf16)
+
+
+class HalvedSum:
+    REFS = 16
+
+    @staticmethod
+    def scratch(rows, chips, block):
+        dma, vmem = pltpu.SemaphoreType.DMA, pltpu.VMEM
+        return [
+            vmem((2, chips) + block, bf16), vmem((2, chips) + block, bf16),
+            vmem((chips,) + block, bf16), vmem((2,) + block, bf16), vmem(block, bf16),
+            dma((2,)), dma((2,)), dma((2,)), dma, dma, dma((2,)), dma((2,)), dma, dma,
+        ]
+
+    def __init__(self, rows, chips, given, scratch):
+        self.own, self.came, self.came_row, self.came_line, self.came_far, *sems = scratch
+        local, send_a, recv_a, send_b, recv_b, send_c, recv_c, send_d, recv_d = sems
+        row, col = place()
+        plane = Plane()
+        chip, lane = col // 2, lax.rem(col, 2)
+        near = chip + 1 - 2 * lax.rem(chip, 2)
+        self.chip, self.far = chip, lax.rem(chip + 2, 4)
+        own = self.own
+        self.loads = [
+            pltpu.make_async_copy(given.at[at], own.at[k], local.at[k])
+            for k, at in enumerate((row, plane.second))
+        ]
+        self.a = [
+            remote(given.at[at], self.came.at[k], send_a.at[k], recv_a.at[k], (plane.first, col))
+            for k, at in enumerate((plane.first, plane.across))
+        ]
+        self.b = [remote(own.at[1], self.came_row, send_b, recv_b, (plane.second, col))]
+        self.c = [
+            remote(
+                own.at[0, at], self.came_line.at[k], send_c.at[k], recv_c.at[k],
+                (row, near * 2 + lane),
+            )
+            for k, at in enumerate((near, lax.rem(near + 2, 4)))
+        ]
+        self.d = [
+            remote(own.at[0, self.far], self.came_far, send_d, recv_d, (row, self.far * 2 + lane))
+        ]
+
+    def begin(self):
+        for copy in self.a + self.loads:
+            copy.start()
+
+    def step(self, n):
+        if n == 0:
+            for copy in self.loads:
+                copy.wait()
+            for copy in self.a:
+                copy.wait_recv()
+            for k in (1, 0):
+                for c in range(self.own.shape[1]):
+                    add_into(self.own.at[k, c], self.came.at[k, c])
+                if k == 1:
+                    self.b[0].start()
+        elif n == 1:
+            self.b[0].wait_recv()
+            for c in range(self.own.shape[1]):
+                add_into(self.own.at[0, c], self.came_row.at[c])
+            for copy in self.c:
+                copy.start()
+        else:
+            for copy in self.c:
+                copy.wait_recv()
+            add_into(self.own.at[0, self.far], self.came_line.at[1])
+            self.d[0].start()
+            add_into(self.own.at[0, self.chip], self.came_line.at[0])
+
+    def result(self):
+        self.d[0].wait_recv()
+        return self.own[0, self.chip].astype(f32) + self.came_far[...].astype(f32)
+
+    def wait_send(self):
+        for copy in self.a + self.b + self.c + self.d:
+            copy.wait_send()
+
+
+class DirectSum:
+    @staticmethod
+    def scratch(rows, chips, block):
+        dma, vmem = pltpu.SemaphoreType.DMA, pltpu.VMEM
+        return [
+            vmem((rows, chips) + block, bf16), vmem((chips,) + block, bf16),
+            vmem((chips,) + block, bf16),
+            dma, dma((rows,)), dma((rows,)), dma((chips,)), dma((chips,)),
+        ]
+
+    def __init__(self, rows, chips, given, scratch):
+        by_row, total, by_line, local, send_r, recv_r, send_l, recv_l = scratch
+        row, col = place()
+        self.rows, self.chips, self.chip = rows, chips, col // 2
+        self.by_row, self.total, self.by_line = by_row, total, by_line
+        self.load = pltpu.make_async_copy(given.at[row], by_row.at[row], local)
+        self.r = over_row(
+            rows, lambda at: given.at[at], lambda at: by_row.at[at], send_r, recv_r
+        )
+        self.l = over_line(
+            chips, lambda at: total.at[at], lambda at: by_line.at[at], send_l, recv_l
+        )
+
+    def begin(self):
+        self.load.start()
+        self.r.start()
+
+    def step(self, n):
+        if n != 1:
+            return
+        self.load.wait()
+        self.r.wait_recv()
+
+        def one(c, carry):
+            total = self.by_row[0, c].astype(f32)
+            for r in range(1, self.rows):
+                total = total + self.by_row[r, c].astype(f32)
+            self.total[c] = total.astype(bf16)
+            return carry
+
+        lax.fori_loop(0, self.chips, one, 0)
+        self.by_line[self.chip] = self.total[self.chip]
+        self.l.start()
+
+    def result(self):
+        self.l.wait_recv()
+        total = self.by_line[0].astype(f32)
+        for c in range(1, self.chips):
+            total = total + self.by_line[c].astype(f32)
+        return total
+
+    def wait_send(self):
+        self.r.wait_send()
+        self.l.wait_send()
+
+
+def weight_sum(rows, chips):
+    return HalvedSum if (rows, chips) == (4, 4) else DirectSum
+
+
+def weight_scratch(rows, chips, blocks):
+    return [ref for block in blocks for ref in weight_sum(rows, chips).scratch(rows, chips, block)]
+
+
 def back_kernel(
     rows, cols, heads, seqs, tiles, sub,
     blk_ref, q_ref, k_ref, v_ref, do_ref, o_ref, lse_ref, x_ref, w_ref, tok_ref, dres_ref, vec_ref,
     gup_ref, gdown_ref, gout_ref, early_ref,
-    dtok_ref, wup_ref, wdown_ref, wout_ref, wqkv_ref, all_ref, bias_ref,
+    dtok_ref, wup_ref, wdown_ref, wout_ref, wqkv_ref, all_ref, late_ref, bias_ref,
     d_mixed, d_arrived, key_grad, value_grad, bias_sum, qkv_acc, qkv_send, qkv_recv, norm_acc,
-    up_recv, down_recv, out_recv, up_send, down_send, out_send, up_line, down_line, out_line,
-    small, small_core, small_row, small_line, bias_send, bias_recv,
-    send_r, recv_r, send_z, recv_z, send_d, recv_d, send_q, recv_q, send_b, recv_b,
-    send_s0, recv_s0, send_s1, recv_s1, send_s2, recv_s2, local,
+    bias_send, bias_recv, send_d, recv_d, send_q, recv_q, send_b, recv_b, local_d, *rest,
 ):
     step = pl.program_id(0)
     chips = cols // 2
     row, col = place()
-    chip, lane = col // 2, lax.rem(col, 2)
     work = heads * seqs * tiles
     last = work + 2 * cols - 1
-    head = step // (seqs * tiles)
+    head = jnp.minimum(step // (seqs * tiles), heads - 1)
     seq = lax.rem(step // tiles, seqs)
     turn = lax.rem(step, tiles)
     i = tiles - 1 - turn
@@ -847,44 +1058,17 @@
     chunks, _, chunk = do_ref.shape
     chunks_seq = SEQ_LEN // chunk
     parts = tile // sub
-    steps = tile
     start = pl.multiple_of(i * tile, tile)
 
-    given = (gdown_ref, gup_ref, gout_ref)
-    by_row = (down_recv, up_recv, out_recv)
-    to_line = (down_send, up_send, out_send)
-    by_line = (down_line, up_line, out_line)
+    early = SmallSum(rows, chips, rest[:SUM_REFS])
+    late = SmallSum(rows, chips, rest[SUM_REFS : 2 * SUM_REFS])
+    rest = rest[2 * SUM_REFS :]
+    each_refs = len(rest) // 3
+    weights = [
+        weight_sum(rows, chips)(rows, chips, given, rest[n * each_refs : (n + 1) * each_refs])
+        for n, given in enumerate((gdown_ref, gup_ref, gout_ref))
+    ]
     results = (wdown_ref, wup_ref, wout_ref)
-
-    def row_stage(n):
-        return over_row(
-            rows, lambda at: given[n].at[at], lambda at: by_row[n].at[at], send_r.at[n],
-            recv_r.at[n],
-        )
-
-    def own_row(n):
-        return pltpu.make_async_copy(given[n].at[row], by_row[n].at[row], local.at[n])
-
-    def line_stage(n):
-        return over_line(
-            chips, lambda at: to_line[n].at[at], lambda at: by_line[n].at[at], send_z.at[n],
-            recv_z.at[n],
-        )
-
-    def add_rows(n):
-        own_row(n).wait()
-        row_stage(n).wait_recv()
-
-        def one(c, carry):
-            total = by_row[n][0, c].astype(f32)
-            for r in range(1, rows):
-                total = total + by_row[n][r, c].astype(f32)
-            to_line[n][c] = total.astype(bf16)
-            return carry
-
-        lax.fori_loop(0, chips, one, 0)
-        by_line[n][chip] = to_line[n][chip]
-        line_stage(n).start()
 
     def d_stage(h):
         return over_col(
@@ -893,30 +1077,34 @@
         )
 
     def own_d(h):
-        return pltpu.make_async_copy(d_mixed.at[h, col], d_arrived.at[h, col], local.at[3 + h])
+        return pltpu.make_async_copy(d_mixed.at[h, col], d_arrived.at[h, col], local_d.at[h])
 
     q_stage = over_row(
         rows, lambda at: qkv_send.at[at], lambda at: qkv_recv.at[at], send_q, recv_q
     )
     b_stage = over_row(rows, lambda at: bias_send, lambda at: bias_recv.at[at], send_b, recv_b)
-    s_core = remote(small.at[0], small_core, send_s0, recv_s0, mate())
-    s_row = over_row(
-        rows, lambda at: small.at[1], lambda at: small_row.at[at], send_s1, recv_s1
-    )
-    s_line = over_line(
-        chips, lambda at: small.at[2], lambda at: small_line.at[at], send_s2, recv_s2
-    )
+
+    def at_step(when, act):
+        @pl.when(step == when)
+        def _():
+            act()
 
     @pl.when(step == 0)
     def _():
         greet(rows, cols)
-        for n in range(3):
-            own_row(n).start()
-            row_stage(n).start()
-
-    @pl.when(step == work // 2 + 1)
-    def _():
-        add_rows(0)
+        weights[0].begin()
+        early.first(early_ref[...])
+
+    at_step(work // 8, early.second)
+    at_step(
+        work // 4, lambda: (weights[0].step(0), weights[1].begin(), weights[2].begin())
+    )
+    at_step(work * 3 // 8, early.third)
+    at_step(work * 5 // 8, lambda: weights[0].step(1))
+    at_step(work * 6 // 8, lambda: (weights[1].step(0), weights[2].step(0)))
+    at_step(work * 7 // 8, lambda: weights[0].step(2))
+    at_step(work + cols // 2, lambda: (weights[1].step(1), weights[2].step(1)))
+    at_step(work + cols + cols // 2, lambda: (weights[1].step(2), weights[2].step(2)))
 
     @pl.when((step < work) & (turn == 0))
     def _():
@@ -926,6 +1114,23 @@
     @pl.when((step < work) & (turn == 0) & (seq == 0))
     def _():
         bias_sum[head] = jnp.zeros((HD, 128), f32)
+
+    def hand_over(t):
+        for b in range(chunks):
+            where = pl.ds(pl.multiple_of(t * tile + b * chunk, chunk), chunk)
+            at = seq * chunks_seq + t * chunks + b
+            d_mixed[head, at, HD : 2 * HD] = (key_grad[where, :].T * SCALE).astype(bf16)
+            d_values = value_grad[where, :].T
+            d_mixed[head, at, 2 * HD :] = d_values.astype(bf16)
+            bias_sum[head, :, 1:2] += jnp.sum(d_values, axis=1, keepdims=True)
+
+            @pl.when(at == col)
+            def _():
+                own_d(head).start()
+
+            @pl.when(at != col)
+            def _():
+                d_stage(head).copy(lax.rem(at - col + cols, cols)).start()
 
     @pl.when(step < work)
     def _():
@@ -960,14 +1165,12 @@
             value_grad[pl.ds(key_start, count), :] += d_values
 
         def sweep(j, grads):
-            key_start = pl.multiple_of(j * steps, steps)
-            found = [update(a, grads[a], key_start, steps, False) for a in range(parts)]
-            add(key_start, steps, sum(f[1] for f in found), sum(f[2] for f in found))
+            key_start = pl.multiple_of(j * tile, tile)
+            found = [update(a, grads[a], key_start, tile, False) for a in range(parts)]
+            add(key_start, tile, sum(f[1] for f in found), sum(f[2] for f in found))
             return tuple(f[0] for f in found)
 
-        grads = list(
-            lax.fori_loop(0, start // steps, sweep, (jnp.zeros((HD, sub), f32),) * parts)
-        )
+        grads = list(lax.fori_loop(0, i, sweep, (jnp.zeros((HD, sub), f32),) * parts))
         for a in range(parts):
             todo = [(pl.multiple_of(start + a * sub, sub), sub, True)]
             if a > 0:
@@ -993,25 +1196,13 @@
                 :, b * chunk : (b + 1) * chunk
             ]
 
-    @pl.when((step < work) & (turn == tiles - 1))
-    def _():
-        def one(c, value_sum):
-            where = pl.ds(pl.multiple_of(c * chunk, chunk), chunk)
-            at = seq * chunks_seq + c
-            d_mixed[head, at, HD : 2 * HD] = (key_grad[where, :].T * SCALE).astype(bf16)
-            d_values = value_grad[where, :].T
-            d_mixed[head, at, 2 * HD :] = d_values.astype(bf16)
-            return value_sum + jnp.sum(d_values, axis=1, keepdims=True)
-
-        value_sum = lax.fori_loop(0, chunks_seq, one, jnp.zeros((HD, 1), f32))
-        bias_sum[head, :, 1:2] += value_sum
-
-    for h in range(heads):
-
-        @pl.when(step == (h + 1) * seqs * tiles - 1)
-        def _():
-            own_d(h).start()
-            d_stage(h).start()
+    @pl.when((step < work) & (turn > 0))
+    def _():
+        hand_over(i + 1)
+
+    @pl.when((step < work) & (i == 0))
+    def _():
+        hand_over(i)
 
     at = step - work
 
@@ -1034,8 +1225,6 @@
             qkv_send[r] = qkv_acc[:, r * width : (r + 1) * width].astype(bf16)
         qkv_recv[row] = qkv_send[row]
         q_stage.start()
-        add_rows(1)
-        add_rows(2)
         norm_acc[...] = jnp.zeros_like(norm_acc)
         for h in range(heads):
             own_d(h).wait()
@@ -1062,45 +1251,37 @@
     def _():
         xhat, inv = moments(tok_ref[...].astype(f32))
         d_norm = norm_acc[...]
-        late = early_ref.shape[0] - 2
-        small[0] = early_ref[...]
-        small[0, late : late + 1] = jnp.sum(d_norm * xhat, axis=0, keepdims=True)
-        small[0, late + 1 : late + 2] = jnp.sum(d_norm, axis=0, keepdims=True)
-        s_core.start()
+        late.first(
+            jnp.concatenate(
+                [
+                    jnp.sum(d_norm * xhat, axis=0, keepdims=True),
+                    jnp.sum(d_norm, axis=0, keepdims=True),
+                ],
+                axis=0,
+            )
+        )
         dtok_ref[...] = dres_ref[...] + norm_back(xhat, inv, d_norm * vec_ref[0:1])
-        s_core.wait_recv()
-        small[1] = small[0] + small_core[...]
-        small_row[row] = small[1]
-        s_row.start()
+        late.second()
         b_stage.wait_recv()
         bias_ref[...] = sum(bias_recv[r] for r in range(1, rows)) + bias_recv[0]
+        all_ref[...] = early.result()
+        late.third()
         q_stage.wait_recv()
         total = qkv_recv[0].astype(f32)
         for r in range(1, rows):
             total = total + qkv_recv[r].astype(f32)
         wqkv_ref[...] = total
-        s_row.wait_recv()
-        small[2] = sum(small_row[r] for r in range(1, rows)) + small_row[0]
-        small_line[chip] = small[2]
-        s_line.start()
-        for n in range(3):
-            line_stage(n).wait_recv()
-            total = by_line[n][0].astype(f32)
-            for c in range(1, chips):
-                total = total + by_line[n][c].astype(f32)
-            results[n][...] = total
-        s_line.wait_recv()
-        all_ref[...] = sum(small_line[c] for c in range(1, chips)) + small_line[0]
-        for n in range(3):
-            row_stage(n).wait_send()
-            line_stage(n).wait_send()
+        for weight, result in zip(weights, results):
+            result[...] = weight.result()
+        late_ref[...] = late.result()
+        for weight in weights:
+            weight.wait_send()
         for h in range(heads):
             d_stage(h).wait_send()
         q_stage.wait_send()
         b_stage.wait_send()
-        s_core.wait_send()
-        s_row.wait_send()
-        s_line.wait_send()
+        early.wait_send()
+        late.wait_send()
 
 
 def backward(
@@ -1163,11 +1344,11 @@
         ],
         out_specs=[
             block, whole((units, width)), whole((units, width)), whole((head_cols, width)),
-            whole((parts, width)), whole(small), whole((heads, HD, 128)),
+            whole((parts, width)), whole(small), whole((2, depth)), whole((heads, HD, 128)),
         ],
         out_shape=[
             shape((count, depth), f32), shape((units, width), f32), shape((units, width), f32),
-            shape((head_cols, width), f32), shape((parts, width), f32), shape(small, f32),
+            shape((head_cols, width), f32), shape((parts, width), f32), shape(small, f32), shape((2, depth), f32),
             shape((heads, HD, 128), f32),
         ],
         scratch_shapes=[
@@ -1175,20 +1356,12 @@
             vmem((SEQ_LEN, HD), f32), vmem((SEQ_LEN, HD), f32), vmem((heads, HD, 128), f32),
             vmem((parts, depth), f32), vmem((rows, parts, width), bf16),
             vmem((rows, parts, width), bf16), vmem((count, depth), f32),
-            vmem((rows, chips, units, width), bf16), vmem((rows, chips, units, width), bf16),
-            vmem((rows, chips, head_cols, width), bf16),
-            vmem((chips, units, width), bf16), vmem((chips, units, width), bf16),
-            vmem((chips, head_cols, width), bf16),
-            vmem((chips, units, width), bf16), vmem((chips, units, width), bf16),
-            vmem((chips, head_cols, width), bf16),
-            vmem((3,) + small, f32), vmem(small, f32), vmem((rows,) + small, f32),
-            vmem((chips,) + small, f32),
             vmem((heads, HD, 128), f32), vmem((rows, heads, HD, 128), f32),
-            dma((3, rows)), dma((3, rows)), dma((3, chips)), dma((3, chips)),
             dma((heads, cols)), dma((heads, cols)), dma((rows,)), dma((rows,)),
-            dma((rows,)), dma((rows,)), dma, dma, dma((rows,)), dma((rows,)),
-            dma((chips,)), dma((chips,)), dma((3 + heads,)),
-        ],
+            dma((rows,)), dma((rows,)), dma((heads,)),
+        ] + sum_scratch(rows, chips, [small, (2, depth)]) + weight_scratch(
+            rows, chips, [(units, width), (units, width), (head_cols, width)]
+        ),
         compiler_params=pltpu.CompilerParams(
             vmem_limit_bytes=63 << 20, collective_id=2, has_side_effects=True
         ),
@@ -1227,18 +1400,12 @@
         tokens, vecs, vec(blocks), vec(b_up), w_qkv_flat, b_qv, w_out, w_up,
         w_down, rows, cols,
     )
-    grad_up, grad_down, grad_wout, grad_bup, output, d_resid, sums, d_heads, qkv_all = middle(
+    grad_up, grad_down, grad_wout, output, d_resid, sums, d_heads, qkv_all = middle(
         arrived, tokens, grad_out, up_weight, down_weight, up_bias, vecs, out_weight, w_qkv_flat,
     )
-    hidden_units = units * cols
-    used = 4 + hidden_units // depth
-    spare = (used + 9) // 8 * 8 - used
-    early = jnp.concatenate(
-        [sums[:4], grad_bup.reshape(-1, depth), jnp.zeros((spare, depth), f32)]
-    )
-    grad_tokens, grad_wup, grad_wdown, grad_wout, grad_wqkv, small, bias = backward(
+    grad_tokens, grad_wup, grad_wdown, grad_wout, grad_wqkv, small, late, bias = backward(
         block_ids, q, k, v, d_heads, found, lse, attn_rows, qkv_all, tokens, d_resid, vecs,
-        grad_up, grad_down, grad_wout, early,
+        grad_up, grad_down, grad_wout, sums,
     )
     grad_wqkv = (
         grad_wqkv.reshape(heads, 3, HD, depth // rows)
@@ -1248,9 +1415,9 @@
     grad_bqv = bias[:, :, :2].reshape(head_cols, 2).T
     grad_bdown, grad_gain2, grad_shift2, grad_bout = small[:4]
     grad_bup = lax.dynamic_slice_in_dim(
-        small[4:used].reshape(-1), lax.axis_index("col") * units, units
-    )
-    grad_gain1, grad_shift1 = small[-2:]
+        small[4:].reshape(-1), lax.axis_index("col") * units, units
+    )
+    grad_gain1, grad_shift1 = late
     return (
         output, grad_tokens, grad_wqkv, grad_bqv, grad_wout, grad_bout, grad_wup, grad_bup,
         grad_wdown, grad_bdown, grad_gain1, grad_shift1, grad_gain2, grad_shift2,

time: 428 us -> 410 us (0.958)
  Pallas kernels: 404 us -> 387 us
    pallas_call x1, Pallas kernels: 174 us -> 157 us  [backward(): pl.pallas_call(functools.partial(back_kernel, rows, cols, heads, seqs, ti...]
where the time goes in v5:
time: 410 us; the launch traced here: 408 us
  Pallas kernels  387 us (94%)
  local copies, waits for them, and re-layouts  19.6 us (5%)
    pallas_call x1, Pallas kernels, backward(): pl.pallas_call(functools.partial(back_kernel, rows, cols, heads, seqs, ti...  157 us
    pallas_call x1, Pallas kernels, front(): pl.pallas_call(functools.partial(front_kernel, rows, cols, heads), in_spe...  153 us
    pallas_call x1, Pallas kernels, middle(): pl.pallas_call(functools.partial(middle_kernel, rows, cols), grid=(2 * co...  76.5 us
    unnamed x17, local copies, waits for them, and re-layouts  8.58 us

profile of v5, /device:TPU:0, one launch (start us, length us, event | category | flops | bytes accessed | tf_op | source)
XLA Modules:
  0.0 407.6 jit_solution(1322522758492229810)
XLA Ops:
  0.6 0.7 stack.23
  1.3 0.7 stack.24
  2.0 0.7 stack.25
  2.7 0.7 stack.26
  3.4 0.7 stack.27
  4.1 0.7 stack.28
  4.8 0.6 convert_element_type.3.vec_ref
  5.4 1.1 copy.32
  6.5 0.8 copy.33.wq_ref
  7.3 1.3 reshape.50.bup_ref
  8.6 153.1 %front.1 = (bf16[8,512,1024]{2,1,0:T(8,128)(2,1)}, bf16[2,4096,64]{2,1,0:T(8,128)(2,1)}, bf16[2,4096,64]{2,1,0:T(8,128)(2,1)}, bf16[2,4096,64]{2,1,0:T(8,128)(2,...) custom-call(bf16[512,1024]{1,0:T(8,128)(2,1)} %tok_ref.5, ...), custom_call_target="tpu_custom_call" | custom-call | flops 21474836480 | bytes 8388608 | tf_op jit(solution)/shard_map/front/pallas_call | solution.py:554
  161.7 76.5 %middle.1 = (bf16[4,4,512,256]{3,2,1,0:T(8,128)(2,1)}, bf16[4,4,512,256]{3,2,1,0:T(8,128)(2,1)}, bf16[4,4,128,256]{3,2,1,0:T(8,128)(2,1)}, bf16[512,1024]{1,0:T(...) custom-call(bf16[8,128,512]{2,1,0:T(8,128)(2,1)} %get-tuple-element., ...), custom_call_target="tpu_custom_call" | custom-call | flops 25769803776 | bytes 41943040 | tf_op jit(solution)/shard_map/middle/pallas_call | solution.py:795
  238.3 157.1 %backward.1 = (f32[512,1024]{1,0:T(8,128)}, f32[512,256]{1,0:T(8,128)}, f32[512,256]{1,0:T(8,128)}, f32[128,256]{1,0:T(8,128)}, f32[384,256]{1,0:T(8,128)}, /*in...) custom-call(s32[1,1,4096]{2,1,0:T(1,128)} %get-tuple-element.48.blk_ref, ...), custom_call_target="tpu_custom_call" | custom-call | flops 53687091200 | bytes 8388608 | tf_op jit(solution)/shard_map/backward/pallas_call | solution.py:1334
  395.4 1.6 fusion
  397.0 1.0 copy.35
  398.0 0.9 copy.37
  398.9 0.8 slice_bitcast_fusion
  399.7 0.7 dynamic_slice.3
  400.3 1.5 copy.36
  401.8 2.3 copy.46
  404.1 1.3 copy.47
  405.4 0.7 copy.48
  406.0 0.8 copy.49
  406.8 0.8 copy.50
  (10 shorter events, 0.1 us)
Async XLA Ops:
  395.4 8.7 %copy-start = (f32[512,1024]{1,0:T(8,128)S(1)}, f32[512,1024]{1,0:T(8,128)}, u32[]{:S(2)}) copy-start(f32[512,1024]{1,0:T(8,128)} %get-tuple-element.107) | copy-start | bytes 6291460
  404.1 1.3 copy-start.3
  404.1 2.0 copy-start.2
  404.1 2.8 copy-start.1

commit v6 on v5

--- a/solution.py
+++ b/solution.py
@@ -659,7 +659,7 @@
         out_acc[...] = jnp.zeros_like(out_acc)
         norm_acc[...] = jnp.zeros_like(norm_acc)
 
-    @pl.when(step == 1)
+    @pl.when(step == cols // 2)
     def _():
         own_wq.wait()
         z_stage.wait_recv()
@@ -731,7 +731,7 @@
         mine[1, at] = dot(d_ups[c], x[...], TN).astype(bf16)
         pair(at, 1).start()
 
-    @pl.when(at == 0)
+    @pl.when(step == 2 * cols - 1)
     def _():
         for c in range(chips):
             r_stage(c).wait_recv()
@@ -1093,18 +1093,17 @@
     def _():
         greet(rows, cols)
         weights[0].begin()
+        weights[2].begin()
         early.first(early_ref[...])
 
     at_step(work // 8, early.second)
     at_step(
-        work // 4, lambda: (weights[0].step(0), weights[1].begin(), weights[2].begin())
-    )
-    at_step(work * 3 // 8, early.third)
-    at_step(work * 5 // 8, lambda: weights[0].step(1))
-    at_step(work * 6 // 8, lambda: (weights[1].step(0), weights[2].step(0)))
-    at_step(work * 7 // 8, lambda: weights[0].step(2))
-    at_step(work + cols // 2, lambda: (weights[1].step(1), weights[2].step(1)))
-    at_step(work + cols + cols // 2, lambda: (weights[1].step(2), weights[2].step(2)))
+        work * 3 // 8,
+        lambda: (early.third(), weights[0].step(0), weights[2].step(0), weights[1].begin()),
+    )
+    at_step(work * 6 // 8, lambda: (weights[0].step(1), weights[2].step(1)))
+    at_step(work, lambda: weights[1].step(0))
+    at_step(work + cols // 2, lambda: (weights[0].step(2), weights[2].step(2)))
 
     @pl.when((step < work) & (turn == 0))
     def _():
@@ -1115,22 +1114,21 @@
     def _():
         bias_sum[head] = jnp.zeros((HD, 128), f32)
 
-    def hand_over(t):
-        for b in range(chunks):
-            where = pl.ds(pl.multiple_of(t * tile + b * chunk, chunk), chunk)
-            at = seq * chunks_seq + t * chunks + b
-            d_mixed[head, at, HD : 2 * HD] = (key_grad[where, :].T * SCALE).astype(bf16)
-            d_values = value_grad[where, :].T
-            d_mixed[head, at, 2 * HD :] = d_values.astype(bf16)
-            bias_sum[head, :, 1:2] += jnp.sum(d_values, axis=1, keepdims=True)
-
-            @pl.when(at == col)
-            def _():
-                own_d(head).start()
-
-            @pl.when(at != col)
-            def _():
-                d_stage(head).copy(lax.rem(at - col + cols, cols)).start()
+    def hand_over(c):
+        where = pl.ds(pl.multiple_of(c * chunk, chunk), chunk)
+        at = seq * chunks_seq + c
+        d_mixed[head, at, HD : 2 * HD] = (key_grad[where, :].T * SCALE).astype(bf16)
+        d_values = value_grad[where, :].T
+        d_mixed[head, at, 2 * HD :] = d_values.astype(bf16)
+        bias_sum[head, :, 1:2] += jnp.sum(d_values, axis=1, keepdims=True)
+
+        @pl.when(at == col)
+        def _():
+            own_d(head).start()
+
+        @pl.when(at != col)
+        def _():
+            d_stage(head).copy(lax.rem(at - col + cols, cols)).start()
 
     @pl.when(step < work)
     def _():
@@ -1196,13 +1194,18 @@
                 :, b * chunk : (b + 1) * chunk
             ]
 
+    @pl.when((step < work) & (i == 0))
+    def _():
+        hand_over(0)
+
+    @pl.when(step < work)
+    def _():
+        for b in range(1, chunks):
+            hand_over(i * chunks + b)
+
     @pl.when((step < work) & (turn > 0))
     def _():
-        hand_over(i + 1)
-
-    @pl.when((step < work) & (i == 0))
-    def _():
-        hand_over(i)
+        hand_over((i + 1) * chunks)
 
     at = step - work
 
@@ -1229,6 +1232,8 @@
         for h in range(heads):
             own_d(h).wait()
             d_stage(h).wait_recv()
+        for n, stage in ((1, 1),):
+            weights[n].step(stage)
 
     @pl.when(at >= cols)
     def _():
@@ -1249,6 +1254,8 @@
 
     @pl.when(step == last)
     def _():
+        for n, stage in ((1, 2),):
+            weights[n].step(stage)
         xhat, inv = moments(tok_ref[...].astype(f32))
         d_norm = norm_acc[...]
         late.first(

time: 410 us -> 387 us (0.944)
  Pallas kernels: 387 us -> 366 us
    pallas_call x1, Pallas kernels: 157 us -> 145 us  [backward(): pl.pallas_call(functools.partial(back_kernel, rows, cols, heads, seqs, ti...]
    pallas_call x1, Pallas kernels: 76.5 us -> 68 us  [middle(): pl.pallas_call(functools.partial(middle_kernel, rows, cols), grid=(2 * co...]
where the time goes in v6:
time: 387 us
  Pallas kernels  366 us (95%)
  local copies, waits for them, and re-layouts  19.6 us (5%)
    pallas_call x1, Pallas kernels, front(): pl.pallas_call(functools.partial(front_kernel, rows, cols, heads), in_spe...  153 us
    pallas_call x1, Pallas kernels, backward(): pl.pallas_call(functools.partial(back_kernel, rows, cols, heads, seqs, ti...  145 us
    pallas_call x1, Pallas kernels, middle(): pl.pallas_call(functools.partial(middle_kernel, rows, cols), grid=(2 * co...  68 us
    unnamed x17, local copies, waits for them, and re-layouts  8.58 us

profile of v6, /device:TPU:0, one launch (start us, length us, event | category | flops | bytes accessed | tf_op | source)
XLA Modules:
  0.0 386.6 jit_solution(9922544425580358541)
XLA Ops:
  0.6 0.7 stack.23
  1.3 0.7 stack.24
  2.0 0.7 stack.25
  2.7 0.7 stack.26
  3.4 0.7 stack.27
  4.1 0.7 stack.28
  4.8 0.6 convert_element_type.3.vec_ref
  5.4 1.1 copy.32
  6.5 0.8 copy.33.wq_ref
  7.3 1.3 reshape.50.bup_ref
  8.6 153.1 %front.1 = (bf16[8,512,1024]{2,1,0:T(8,128)(2,1)}, bf16[2,4096,64]{2,1,0:T(8,128)(2,1)}, bf16[2,4096,64]{2,1,0:T(8,128)(2,1)}, bf16[2,4096,64]{2,1,0:T(8,128)(2,...) custom-call(bf16[512,1024]{1,0:T(8,128)(2,1)} %tok_ref.5, ...), custom_call_target="tpu_custom_call" | custom-call | flops 21474836480 | bytes 8388608 | tf_op jit(solution)/shard_map/front/pallas_call | solution.py:554
  161.7 68.0 %middle.1 = (bf16[4,4,512,256]{3,2,1,0:T(8,128)(2,1)}, bf16[4,4,512,256]{3,2,1,0:T(8,128)(2,1)}, bf16[4,4,128,256]{3,2,1,0:T(8,128)(2,1)}, bf16[512,1024]{1,0:T(...) custom-call(bf16[8,128,512]{2,1,0:T(8,128)(2,1)} %get-tuple-element., ...), custom_call_target="tpu_custom_call" | custom-call | flops 25769803776 | bytes 41943040 | tf_op jit(solution)/shard_map/middle/pallas_call | solution.py:795
  229.8 144.5 %backward.1 = (f32[512,1024]{1,0:T(8,128)}, f32[512,256]{1,0:T(8,128)}, f32[512,256]{1,0:T(8,128)}, f32[128,256]{1,0:T(8,128)}, f32[384,256]{1,0:T(8,128)}, /*in...) custom-call(s32[1,1,4096]{2,1,0:T(1,128)} %get-tuple-element.48.blk_ref, ...), custom_call_target="tpu_custom_call" | custom-call | flops 53687091200 | bytes 8388608 | tf_op jit(solution)/shard_map/backward/pallas_call | solution.py:1341
  374.3 1.6 fusion
  375.9 1.0 copy.35
  376.9 0.9 copy.37
  377.8 0.8 slice_bitcast_fusion
  378.6 0.7 dynamic_slice.3
  379.2 1.5 copy.36
  380.7 2.3 copy.46
  383.0 1.3 copy.47
  384.3 0.7 copy.48
  385.0 0.8 copy.49
  385.8 0.8 copy.50
  (10 shorter events, 0.1 us)
Async XLA Ops:
  374.3 8.7 %copy-start = (f32[512,1024]{1,0:T(8,128)S(1)}, f32[512,1024]{1,0:T(8,128)}, u32[]{:S(2)}) copy-start(f32[512,1024]{1,0:T(8,128)} %get-tuple-element.107) | copy-start | bytes 6291460
  383.0 1.3 copy-start.3
  383.0 2.0 copy-start.2
  383.0 2.8 copy-start.1

commit v7 on v6

--- a/solution.py
+++ b/solution.py
@@ -375,42 +375,56 @@
             def _():
                 f_stage.copy(lax.rem(owner - me + cols, cols)).start()
 
-    def pass_weights():
+    def at_distance(hop, act):
+        for at, step, route in ((chip - hop, 1, 0), (chip + hop, -1, 1)):
+
+            @pl.when((at >= 0) & (at < chips))
+            def _():
+                act(at, chip + step, route)
+
+    def w_arrive(at, onward, route):
         for n in range(3):
-            w_own(n).wait()
-
-            def across(c, carry):
-                rows_wait_recv(n, c)
-                w_mate(n, c, lane).start()
-                return carry
-
-            lax.fori_loop(0, chips, across, 0)
+            w_line(n, at, onward, route).wait_recv()
+
+            @pl.when((onward >= 0) & (onward < chips))
+            def _():
+                w_line(n, at, onward, route).start()
+
+            rows_start(n, at)
+
+    def w_relay(at, onward=None, route=None):
+        for n in range(3):
+            rows_relay(n, at)
+
+    def w_pass(at, onward=None, route=None):
+        for n in range(3):
+            rows_wait_recv(n, at)
+            w_mate(n, at, lane).start()
+
+    def ahead(hop):
+        if hop == 1:
+            at_distance(1, w_arrive)
+        else:
+            if hop == 2:
+                w_relay(chip)
+            at_distance(hop - 1, w_relay)
+        if hop == chips - 1:
+            for n in range(3):
+                w_own(n).wait()
+            w_pass(chip)
+            for near in range(1, chips - 2):
+                at_distance(near, w_pass)
 
     def event(e, carry):
         hop = (e + 1) // 2
         lower = lax.rem(e, 2) == 1
         p = jnp.where(lower, chip - hop, chip + hop)
 
-        @pl.when(e == 1)
-        def _():
-            for hop in range(1, chips):
-                for at, step, route in ((chip - hop, 1, 0), (chip + hop, -1, 1)):
-
-                    @pl.when((at >= 0) & (at < chips))
-                    def _():
-                        onward = chip + step
-                        for n in range(3):
-                            w_line(n, at, onward, route).wait_recv()
-
-                            @pl.when((onward >= 0) & (onward < chips))
-                            def _():
-                                w_line(n, at, onward, route).start()
-
-                            rows_start(n, at)
-
-        @pl.when(e == 2 * chips - 3)
-        def _():
-            pass_weights()
+        for stage in range(1, chips):
+
+            @pl.when(e == 2 * stage - 1)
+            def _():
+                ahead(stage)
 
         @pl.when(lower)
         def _():
@@ -438,14 +452,11 @@
 
                 to_mate(owner, above).start()
 
-        @pl.when(e == 1)
-        def _():
-            def relay(c, carry):
-                for n in range(3):
-                    rows_relay(n, c)
-                return carry
-
-            lax.fori_loop(0, chips, relay, 0)
+        for stage in range(2, chips - 1):
+
+            @pl.when(e == 2 * stage - 1)
+            def _():
+                at_distance(stage, w_arrive)
 
         @pl.when((p >= 0) & (p < chips))
         def _():
@@ -480,6 +491,11 @@
             def pair(j, carry):
                 q_tile = jnp.where(lower, p + 1 + j, p)
                 key_tile = jnp.where(lower, p, low + j)
+
+                @pl.when((hop == chips - 1) & (j == amount - 2))
+                def _():
+                    at_distance(chips - 1, w_arrive)
+
                 for h in range(heads):
                     update(h, q_tile, 0, tile, key_tile * tile, tile, None)
 
@@ -498,6 +514,9 @@
         return carry
 
     lax.fori_loop(0, 2 * chips - 1, event, 0)
+    at_distance(chips - 2, w_pass)
+    at_distance(chips - 1, w_relay)
+    at_distance(chips - 1, w_pass)
 
     for c in range(cols):
         bupo_ref[c] = bups[c]
@@ -618,10 +637,10 @@
         chips, lambda at: wq_ref, lambda at: wqo_ref.at[lane, row, at], send_z, recv_z
     )
 
-    def r_stage(c):
+    def r_stage(c, out=None):
         return over_row(
             rows,
-            lambda at: wqo_ref.at[lane, row, c],
+            lambda at: wqo_ref.at[lane, row, c] if out is None else out,
             lambda at: wqo_ref.at[lane, at, c],
             send_r.at[c],
             recv_r.at[c],
@@ -648,6 +667,7 @@
         greet(rows, cols)
         own_wq.start()
         z_stage.start()
+        r_stage(chip, wq_ref).start()
         for s in range(cols):
             heads_all[s * depth : (s + 1) * depth] = heads_ref[s]
         stacked = flip(heads_all[...])
@@ -663,8 +683,7 @@
     def _():
         own_wq.wait()
         z_stage.wait_recv()
-        for c in range(chips):
-            r_stage(c).start()
+        each(chips, lambda k: r_stage(lax.rem(chip + k, chips)).start())
 
     @pl.when(step < cols)
     def _():
@@ -687,12 +706,10 @@
         hiddens[step] = hidden
         d_ups[step] = d_up
         for r in range(rows):
-            out_acc[:, part(r)] += dot(hidden, down_ref[0, 0, r])
             norm_acc[:, part(r)] += dot(d_up, up_ref[0, 0, r])
 
     @pl.when(step == cols - 1)
     def _():
-        output_ref[...] = (resid[...] + out_acc[...] + vec_ref[5:6]).astype(bf16)
         xhat, inv = moments(resid[...])
         d_norm = norm_acc[...]
         grad = g_ref[...].astype(f32)
@@ -718,10 +735,15 @@
             out_mine[c] = jnp.where(lane == 0, second, first).astype(bf16)
             kept = jnp.where(lane == 0, first, second)
             for r in range(rows):
-                out_acc[c * depth : (c + 1) * depth, part(r)] = kept[:, part(r)]
+                norm_acc[c * depth : (c + 1) * depth, part(r)] = kept[:, part(r)]
         pair_out.start()
 
     at = step - cols
+
+    @pl.when(at >= 0)
+    def _():
+        for r in range(rows):
+            out_acc[:, part(r)] += dot(hiddens[at], down_ref[0, 0, r])
 
     @pl.when((at >= 0) & (at < chips))
     def _():
@@ -753,10 +775,11 @@
 
     @pl.when(step == 2 * cols - 1)
     def _():
+        output_ref[...] = (resid[...] + out_acc[...] + vec_ref[5:6]).astype(bf16)
         pair_out.wait_recv()
         for c in range(chips):
             for r in range(rows):
-                kept = out_acc[c * depth : (c + 1) * depth, part(r)]
+                kept = norm_acc[c * depth : (c + 1) * depth, part(r)]
                 gout_ref[r, c] = (kept + out_other[c, :, part(r)].astype(f32)).astype(bf16)
         d_stage.wait_recv()
         m_arrival.wait_recv()
@@ -783,7 +806,12 @@
         c = jnp.minimum(s, cols - 1)
         return (lax.rem(c, 2), c // 2, 0, 0, 0)
 
+    def again_map(s):
+        c = lax.rem(s, cols)
+        return (lax.rem(c, 2), c // 2, 0, 0, 0)
+
     weight = pl.BlockSpec((1, 1, rows, units, width), weight_map)
+    again = pl.BlockSpec((1, 1, rows, units, width), again_map)
     grad_spec = pl.BlockSpec(
         (rows, 1, units, width), lambda s: (0, jnp.maximum(s - cols - chips, 0), 0, 0)
     )
@@ -796,7 +824,7 @@
         functools.partial(middle_kernel, rows, cols),
         grid=(2 * cols,),
         in_specs=[
-            whole(heads.shape), block, block, weight, weight, bias, whole(vecs.shape),
+            whole(heads.shape), block, block, weight, again, bias, whole(vecs.shape),
             whole(w_out.shape), any_space,
         ],
         out_specs=[
@@ -1229,11 +1257,21 @@
         qkv_recv[row] = qkv_send[row]
         q_stage.start()
         norm_acc[...] = jnp.zeros_like(norm_acc)
+
+    @pl.when(at >= cols)
+    def _():
+        c = at - cols
         for h in range(heads):
-            own_d(h).wait()
-            d_stage(h).wait_recv()
-        for n, stage in ((1, 1),):
-            weights[n].step(stage)
+
+            @pl.when(c == col)
+            def _():
+                own_d(h).wait()
+
+            @pl.when(c != col)
+            def _():
+                d_stage(h).arrival(lax.rem(c - col + cols, cols)).wait_recv()
+
+    at_step(work + cols, lambda: weights[1].step(1))
 
     @pl.when(at >= cols)
     def _():

time: 387 us -> 382 us (0.987)
  Pallas kernels: 366 us -> 360 us
    pallas_call x1, Pallas kernels: 68 us -> 62.8 us  [middle(): pl.pallas_call(functools.partial(middle_kernel, rows, cols), grid=(2 * co...]
where the time goes in v7:
time: 382 us; the launch traced here: 381 us
  Pallas kernels  360 us (94%)
  local copies, waits for them, and re-layouts  19.6 us (5%)
    pallas_call x1, Pallas kernels, front(): pl.pallas_call(functools.partial(front_kernel, rows, cols, heads), in_spe...  154 us
    pallas_call x1, Pallas kernels, backward(): pl.pallas_call(functools.partial(back_kernel, rows, cols, heads, seqs, ti...  143 us
    pallas_call x1, Pallas kernels, middle(): pl.pallas_call(functools.partial(middle_kernel, rows, cols), grid=(2 * co...  62.8 us
    unnamed x17, local copies, waits for them, and re-layouts  8.58 us

profile of v7, /device:TPU:0, one launch (start us, length us, event | category | flops | bytes accessed | tf_op | source)
XLA Modules:
  0.0 381.1 jit_solution(16902337413728091057)
XLA Ops:
  0.6 0.7 stack.23
  1.3 0.7 stack.24
  2.0 0.7 stack.25
  2.7 0.7 stack.26
  3.4 0.7 stack.27
  4.1 0.7 stack.28
  4.8 0.6 convert_element_type.3.vec_ref
  5.4 1.1 copy.32
  6.5 0.8 copy.33.wq_ref
  7.3 1.3 reshape.50.bup_ref
  8.6 154.2 %front.1 = (bf16[8,512,1024]{2,1,0:T(8,128)(2,1)}, bf16[2,4096,64]{2,1,0:T(8,128)(2,1)}, bf16[2,4096,64]{2,1,0:T(8,128)(2,1)}, bf16[2,4096,64]{2,1,0:T(8,128)(2,...) custom-call(bf16[512,1024]{1,0:T(8,128)(2,1)} %tok_ref.5, ...), custom_call_target="tpu_custom_call" | custom-call | flops 21474836480 | bytes 8388608 | tf_op jit(solution)/shard_map/front/pallas_call | solution.py:573
  162.8 62.8 %middle.1 = (bf16[4,4,512,256]{3,2,1,0:T(8,128)(2,1)}, bf16[4,4,512,256]{3,2,1,0:T(8,128)(2,1)}, bf16[4,4,128,256]{3,2,1,0:T(8,128)(2,1)}, bf16[512,1024]{1,0:T(...) custom-call(bf16[8,128,512]{2,1,0:T(8,128)(2,1)} %get-tuple-element., ...), custom_call_target="tpu_custom_call" | custom-call | flops 25769803776 | bytes 41943040 | tf_op jit(solution)/shard_map/middle/pallas_call | solution.py:823
  225.6 143.2 %backward.1 = (f32[512,1024]{1,0:T(8,128)}, f32[512,256]{1,0:T(8,128)}, f32[512,256]{1,0:T(8,128)}, f32[128,256]{1,0:T(8,128)}, f32[384,256]{1,0:T(8,128)}, /*in...) custom-call(s32[1,1,4096]{2,1,0:T(1,128)} %get-tuple-element.48.blk_ref, ...), custom_call_target="tpu_custom_call" | custom-call | flops 53687091200 | bytes 8388608 | tf_op jit(solution)/shard_map/backward/pallas_call | solution.py:1379
  368.8 1.6 fusion
  370.4 1.0 copy.35
  371.4 0.9 copy.37
  372.3 0.8 slice_bitcast_fusion
  373.1 0.7 dynamic_slice.3
  373.8 1.5 copy.36
  375.2 2.3 copy.46
  377.5 1.3 copy.47
  378.8 0.7 copy.48
  379.5 0.8 copy.49
  380.3 0.8 copy.50
  (10 shorter events, 0.1 us)
Async XLA Ops:
  368.8 8.7 %copy-start = (f32[512,1024]{1,0:T(8,128)S(1)}, f32[512,1024]{1,0:T(8,128)}, u32[]{:S(2)}) copy-start(f32[512,1024]{1,0:T(8,128)} %get-tuple-element.107) | copy-start | bytes 6291460
  377.5 1.3 copy-start.3
  377.5 2.0 copy-start.2
  377.5 2.8 copy-start.1

commit v8 on v7

--- a/solution.py
+++ b/solution.py
@@ -60,6 +60,10 @@
     )
 
 
+def line(ref):
+    return ref[...].astype(f32).reshape(1, -1)
+
+
 def place():
     return lax.axis_index("row"), lax.axis_index("col")
 
@@ -161,7 +165,7 @@
 
 def front_kernel(
     rows, cols, heads,
-    tok_ref, vec_ref, blk_ref, bup_ref, wq_ref, bias_ref, wout_ref, wup_ref, wdown_ref,
+    tok_ref, gain_ref, shift_ref, bup_ref, blk_ref, wq_ref, bias_ref, wout_ref, wup_ref, wdown_ref,
     xo_ref, q_ref, k_ref, v_ref, found_ref, arrived_ref, lse_ref, blko_ref, bupo_ref,
     wouto_ref, wupo_ref, wdowno_ref,
     xs, wqs, qs, ks, vs, vt, totals, tops, founds, blks, bups,
@@ -174,15 +178,15 @@
     count = tok_ref.shape[0]
     tile = 2 * count
     seq_chips = SEQ_LEN // tile
-    depth = wq_ref.shape[0]
+    depth = wq_ref.shape[1]
     width = heads * HD
 
     xhat, _ = moments(tok_ref[...].astype(f32))
-    xs[me] = (xhat * vec_ref[0:1] + vec_ref[1:2]).astype(bf16)
+    xs[me] = (xhat * line(gain_ref) + line(shift_ref)).astype(bf16)
     blks[me] = blk_ref[...]
-    bups[me] = bup_ref[...]
+    bups[me] = line(bup_ref).astype(bf16)
     own_rows = pl.ds(pl.multiple_of(row * depth, depth), depth)
-    wqs[own_rows] = wq_ref[...]
+    wqs[:, own_rows] = wq_ref[...]
     vt[:, HD:, :] = jnp.ones((heads, ONES, vt.shape[2]), bf16)
     greet(rows, cols)
 
@@ -200,13 +204,15 @@
     q_stage = over_row(
         rows,
         lambda at: wq_ref,
-        lambda at: wqs.at[pl.ds(pl.multiple_of(at * depth, depth), depth)],
+        lambda at: wqs.at[:, pl.ds(pl.multiple_of(at * depth, depth), depth)],
         send_q,
         recv_q,
     )
     small = [
         over_col(cols, lambda at: blk_ref, lambda at: blks.at[at], send_s.at[0], recv_s.at[0]),
-        over_col(cols, lambda at: bup_ref, lambda at: bups.at[at], send_s.at[1], recv_s.at[1]),
+        over_col(
+            cols, lambda at: bups.at[me], lambda at: bups.at[at], send_s.at[1], recv_s.at[1]
+        ),
     ]
     f_stage_out = lambda at: founds.at[at]
     f_stage = over_col(cols, f_stage_out, lambda at: arrived_ref.at[at], send_f, recv_f)
@@ -323,7 +329,7 @@
 
     def project(p):
         both = jnp.concatenate([xs[2 * p], xs[2 * p + 1]], axis=0)
-        mixed = dot(both, wqs[...])
+        mixed = dot(both, jnp.concatenate([wqs[j] for j in range(3)], axis=1))
         bias = bias_ref[...].astype(f32)
         where = pl.ds(pl.multiple_of(p * tile, tile), tile)
         for h in range(heads):
@@ -558,9 +564,9 @@
         exchange.wait_send()
 
 
-def front(tokens, vecs, blocks, b_up, w_qkv, b_qv, w_out, w_up, w_down, rows, cols):
+def front(tokens, gain, shift, b_up, blocks, w_qkv, b_qv, w_out, w_up, w_down, rows, cols):
     count, depth = tokens.shape
-    head_cols = w_qkv.shape[1] // 3
+    head_cols = w_qkv.shape[2]
     heads = head_cols // HD
     chips = cols // 2
     total = count * cols
@@ -572,22 +578,22 @@
     held = (heads, total, HD)
     return pl.pallas_call(
         functools.partial(front_kernel, rows, cols, heads),
-        in_specs=[in_vmem] * 9,
+        in_specs=[in_vmem] * 10,
         out_specs=[any_space] * 6 + [in_vmem] * 3 + [any_space] * 3,
         out_shape=[
             shape((cols, count, depth), bf16), shape(held, bf16), shape(held, bf16),
             shape(held, bf16), shape((cols, head_cols, count), bf16),
             shape((cols, head_cols, count), bf16),
             shape((heads, total // SEQ_LEN, 1, SEQ_LEN), f32),
-            shape((total // SEQ_LEN, 1, SEQ_LEN), jnp.int32), shape((cols,) + b_up.shape, bf16),
+            shape((total // SEQ_LEN, 1, SEQ_LEN), jnp.int32), shape((cols, 1) + b_up.shape, bf16),
         ] + [shape((2, chips, rows) + w.shape, bf16) for w in (w_out, w_up, w_down)],
         scratch_shapes=[
-            vmem((cols, count, depth), bf16), vmem((depth, 3 * head_cols), bf16),
+            vmem((cols, count, depth), bf16), vmem((3, depth, head_cols), bf16),
             vmem(held, bf16), vmem(held, bf16), vmem(held, bf16),
             vmem((heads, HD + ONES, total), bf16),
             vmem((heads, chips, HD + ONES, tile), f32), vmem((heads, chips, 1, tile), f32),
             vmem((cols, head_cols, count), bf16), vmem((cols,) + blocks.shape, jnp.int32),
-            vmem((cols,) + b_up.shape, bf16),
+            vmem((cols, 1) + b_up.shape, bf16),
             dma((3, chips)), dma((3, chips)), dma((rows,)), dma((rows,)),
             dma((2, cols)), dma((2, cols)), dma((cols,)), dma((cols,)),
             dma((3, 2, chips)), dma((3, chips)), dma((3, chips, rows)), dma((3, chips, rows)),
@@ -599,7 +605,7 @@
         ),
         cost_estimate=cost(16 * pairs * HD, 16 * heads * total * HD, pairs),
         name="front",
-    )(tokens, vecs, blocks, b_up, w_qkv, b_qv, w_out, w_up, w_down)
+    )(tokens, gain, shift, b_up, blocks, w_qkv, b_qv, w_out, w_up, w_down)
 
 
 def tile_mask(blk_ref, key_start, count, query_blocks):
@@ -613,7 +619,8 @@
 
 def middle_kernel(
     rows, cols,
-    heads_ref, tok_ref, g_ref, up_ref, down_ref, bup_ref, vec_ref, wout_ref, wq_ref,
+    heads_ref, tok_ref, g_ref, up_ref, down_ref, bup_ref, bout_ref, gain_ref, shift_ref, bdown_ref,
+    wout_ref, wq_ref,
     gup_ref, gdown_ref, gout_ref, output_ref, dres_ref, sums_ref, dheads_ref, wqo_ref,
     x, heads_all, resid, out_acc, norm_acc, hiddens, d_ups, low, d_send,
     mine, other, out_mine, out_other,
@@ -673,9 +680,9 @@
         stacked = flip(heads_all[...])
         for r in range(rows):
             branch = dot(stacked, out_weight(r))
-            resid[:, part(r)] = tok_ref[:, part(r)].astype(f32) + branch + vec_ref[2:3, part(r)]
+            resid[:, part(r)] = tok_ref[:, part(r)].astype(f32) + branch + line(bout_ref)[:, part(r)]
         xhat, _ = moments(resid[...])
-        x[...] = (xhat * vec_ref[3:4] + vec_ref[4:5]).astype(bf16)
+        x[...] = (xhat * line(gain_ref) + line(shift_ref)).astype(bf16)
         out_acc[...] = jnp.zeros_like(out_acc)
         norm_acc[...] = jnp.zeros_like(norm_acc)
 
@@ -713,7 +720,7 @@
         xhat, inv = moments(resid[...])
         d_norm = norm_acc[...]
         grad = g_ref[...].astype(f32)
-        d_resid = grad + norm_back(xhat, inv, d_norm * vec_ref[3:4])
+        d_resid = grad + norm_back(xhat, inv, d_norm * line(gain_ref))
         dres_ref[...] = d_resid
         low[...] = d_resid.astype(bf16)
         sums_ref[0:1] = jnp.sum(grad, axis=0, keepdims=True)
@@ -775,7 +782,7 @@
 
     @pl.when(step == 2 * cols - 1)
     def _():
-        output_ref[...] = (resid[...] + out_acc[...] + vec_ref[5:6]).astype(bf16)
+        output_ref[...] = (resid[...] + out_acc[...] + line(bdown_ref)).astype(bf16)
         pair_out.wait_recv()
         for c in range(chips):
             for r in range(rows):
@@ -794,7 +801,7 @@
         own_d.wait()
 
 
-def middle(heads, tokens, grad, w_up, w_down, b_up, vecs, w_out, w_qkv):
+def middle(heads, tokens, grad, w_up, w_down, b_up, b_out, gain, shift, b_down, w_out, w_qkv):
     count, depth = tokens.shape
     _, chips, rows, units, width = w_up.shape
     cols = 2 * chips
@@ -824,7 +831,7 @@
         functools.partial(middle_kernel, rows, cols),
         grid=(2 * cols,),
         in_specs=[
-            whole(heads.shape), block, block, weight, again, bias, whole(vecs.shape),
+            whole(heads.shape), block, block, weight, again, bias, *[whole((depth,))] * 4,
             whole(w_out.shape), any_space,
         ],
         out_specs=[
@@ -858,7 +865,7 @@
             12 * count * depth * cols * units, 8 * depth * cols * units + 16 * count * depth
         ),
         name="middle",
-    )(heads, tokens, grad, w_up, w_down, b_up, vecs, w_out, w_qkv)
+    )(heads, tokens, grad, w_up, w_down, b_up, b_out, gain, shift, b_down, w_out, w_qkv)
 
 
 class SmallSum:
@@ -1067,7 +1074,7 @@
 
 def back_kernel(
     rows, cols, heads, seqs, tiles, sub,
-    blk_ref, q_ref, k_ref, v_ref, do_ref, o_ref, lse_ref, x_ref, w_ref, tok_ref, dres_ref, vec_ref,
+    blk_ref, q_ref, k_ref, v_ref, do_ref, o_ref, lse_ref, x_ref, w_ref, tok_ref, dres_ref, gain_ref,
     gup_ref, gdown_ref, gout_ref, early_ref,
     dtok_ref, wup_ref, wdown_ref, wout_ref, wqkv_ref, all_ref, late_ref, bias_ref,
     d_mixed, d_arrived, key_grad, value_grad, bias_sum, qkv_acc, qkv_send, qkv_recv, norm_acc,
@@ -1276,7 +1283,7 @@
     @pl.when(at >= cols)
     def _():
         c = at - cols
-        width = w_ref.shape[3]
+        width = w_ref.shape[4]
         found = flip(
             jnp.concatenate(
                 [
@@ -1288,7 +1295,9 @@
             )
         )
         for r in range(rows):
-            norm_acc[:, r * width : (r + 1) * width] += dot(found, w_ref[0, r, 0], NT)
+            norm_acc[:, r * width : (r + 1) * width] += dot(
+                found, jnp.concatenate([w_ref[0, r, 0, j] for j in range(3)], axis=1), NT
+            )
 
     @pl.when(step == last)
     def _():
@@ -1305,7 +1314,7 @@
                 axis=0,
             )
         )
-        dtok_ref[...] = dres_ref[...] + norm_back(xhat, inv, d_norm * vec_ref[0:1])
+        dtok_ref[...] = dres_ref[...] + norm_back(xhat, inv, d_norm * line(gain_ref))
         late.second()
         b_stage.wait_recv()
         bias_ref[...] = sum(bias_recv[r] for r in range(1, rows)) + bias_recv[0]
@@ -1315,7 +1324,9 @@
         total = qkv_recv[0].astype(f32)
         for r in range(1, rows):
             total = total + qkv_recv[r].astype(f32)
-        wqkv_ref[...] = total
+        for j in range(3):
+            part = [total[(h * 3 + j) * HD : (h * 3 + j + 1) * HD] for h in range(heads)]
+            wqkv_ref[j] = jnp.concatenate(part, axis=0).T
         for weight, result in zip(weights, results):
             result[...] = weight.result()
         late_ref[...] = late.result()
@@ -1330,7 +1341,7 @@
 
 
 def backward(
-    blocks, q, k, v, d_heads, out, lse, x, w_qkv, tokens, d_resid, vecs, grad_up, grad_down,
+    blocks, q, k, v, d_heads, out, lse, x, w_qkv, tokens, d_resid, gain, grad_up, grad_down,
     grad_out, early,
 ):
     heads, total, _ = q.shape
@@ -1366,7 +1377,7 @@
 
     def w_map(s):
         c = jnp.maximum(s - work - cols, 0)
-        return (lax.rem(c, 2), 0, c // 2, 0, 0)
+        return (lax.rem(c, 2), 0, c // 2, 0, 0, 0)
 
     keys = pl.BlockSpec((1, SEQ_LEN, HD), keys_map)
     heads_spec = pl.BlockSpec((tile // chunk_of(tokens), HD, count), heads_map)
@@ -1385,15 +1396,15 @@
             pl.BlockSpec((1, 1, 1, tile), lse_map),
             pl.BlockSpec((1, count, depth), lambda s: (jnp.clip(s - work, 0, cols - 1), 0, 0)),
             pl.BlockSpec((1, rows, 1) + w_qkv.shape[3:], w_map),
-            block, block, whole(vecs.shape), any_space, any_space, any_space, whole(small),
+            block, block, whole((depth,)), any_space, any_space, any_space, whole(small),
         ],
         out_specs=[
             block, whole((units, width)), whole((units, width)), whole((head_cols, width)),
-            whole((parts, width)), whole(small), whole((2, depth)), whole((heads, HD, 128)),
+            whole((3, width, heads * HD)), whole(small), whole((2, depth)), whole((heads, HD, 128)),
         ],
         out_shape=[
             shape((count, depth), f32), shape((units, width), f32), shape((units, width), f32),
-            shape((head_cols, width), f32), shape((parts, width), f32), shape(small, f32), shape((2, depth), f32),
+            shape((head_cols, width), f32), shape((3, width, heads * HD), f32), shape(small, f32), shape((2, depth), f32),
             shape((heads, HD, 128), f32),
         ],
         scratch_shapes=[
@@ -1413,7 +1424,7 @@
         cost_estimate=cost(40 * pairs * HD, 16 * heads * total * HD, pairs),
         name="backward",
     )(
-        blocks, q, k, v, d_heads, out, lse, x, w_qkv, tokens, d_resid, vecs, grad_up, grad_down,
+        blocks, q, k, v, d_heads, out, lse, x, w_qkv, tokens, d_resid, gain, grad_up, grad_down,
         grad_out, early,
     )
 
@@ -1435,28 +1446,24 @@
     def vec(v):
         return v.reshape(1, -1)
 
-    vecs = jnp.stack([gain1, shift1, b_out, gain2, shift2, b_down] + [gain1] * 2).astype(f32)
-    w_qkv_flat = w_qkv.reshape(w_qkv.shape[0], 3 * head_cols)
+    w_qkv_parts = w_qkv.transpose(1, 0, 2)
 
     (
         attn_rows, q, k, v, found, arrived, lse, block_ids, up_bias, out_weight, up_weight,
         down_weight,
     ) = front(
-        tokens, vecs, vec(blocks), vec(b_up), w_qkv_flat, b_qv, w_out, w_up,
+        tokens, gain1, shift1, b_up, vec(blocks), w_qkv_parts, b_qv, w_out, w_up,
         w_down, rows, cols,
     )
     grad_up, grad_down, grad_wout, output, d_resid, sums, d_heads, qkv_all = middle(
-        arrived, tokens, grad_out, up_weight, down_weight, up_bias, vecs, out_weight, w_qkv_flat,
+        arrived, tokens, grad_out, up_weight, down_weight, up_bias, b_out, gain2, shift2, b_down,
+        out_weight, w_qkv_parts,
     )
     grad_tokens, grad_wup, grad_wdown, grad_wout, grad_wqkv, small, late, bias = backward(
-        block_ids, q, k, v, d_heads, found, lse, attn_rows, qkv_all, tokens, d_resid, vecs,
+        block_ids, q, k, v, d_heads, found, lse, attn_rows, qkv_all, tokens, d_resid, gain1,
         grad_up, grad_down, grad_wout, sums,
     )
-    grad_wqkv = (
-        grad_wqkv.reshape(heads, 3, HD, depth // rows)
-        .transpose(3, 1, 0, 2)
-        .reshape(depth // rows, 3, head_cols)
-    )
+    grad_wqkv = grad_wqkv.transpose(1, 0, 2)
     grad_bqv = bias[:, :, :2].reshape(head_cols, 2).T
     grad_bdown, grad_gain2, grad_shift2, grad_bout = small[:4]
     grad_bup = lax.dynamic_slice_in_dim(

time: 382 us -> 373 us (0.976)
  local copies, waits for them, and re-layouts: 19.6 us -> 11.1 us
    another operation x7 -> x0, local copies, waits for them, and re-layouts: 4.17 us -> none  [body(): jnp.stack([gain1, shift1, b_out, gain2, shift2, b_down] + [gain1] * 2)]
    unnamed x17 -> x18, local copies, waits for them, and re-layouts: 8.58 us -> 7.36 us
where the time goes in v8:
time: 373 us
  Pallas kernels  361 us (97%)
  local copies, waits for them, and re-layouts  11.1 us (3%)
    pallas_call x1, Pallas kernels, front(): pl.pallas_call(functools.partial(front_kernel, rows, cols, heads), in_spe...  154 us
    pallas_call x1, Pallas kernels, backward(): pl.pallas_call(functools.partial(back_kernel, rows, cols, heads, seqs, ti...  143 us
    pallas_call x1, Pallas kernels, middle(): pl.pallas_call(functools.partial(middle_kernel, rows, cols), grid=(2 * co...  63.2 us

profile of v8, /device:TPU:0, one launch (start us, length us, event | category | flops | bytes accessed | tf_op | source)
XLA Modules:
  0.0 372.5 jit_solution(1911936875478778036)
XLA Ops:
  0.6 154.4 %front.1 = (bf16[8,512,1024]{2,1,0:T(8,128)(2,1)}, bf16[2,4096,64]{2,1,0:T(8,128)(2,1)}, bf16[2,4096,64]{2,1,0:T(8,128)(2,1)}, bf16[2,4096,64]{2,1,0:T(8,128)(2,...) custom-call(bf16[512,1024]{1,0:T(8,128)(2,1)} %tok_ref.5, ...), custom_call_target="tpu_custom_call" | custom-call | flops 21474836480 | bytes 8388608 | tf_op jit(solution)/shard_map/front/pallas_call | solution.py:579
  155.0 63.2 %middle.1 = (bf16[4,4,512,256]{3,2,1,0:T(8,128)(2,1)}, bf16[4,4,512,256]{3,2,1,0:T(8,128)(2,1)}, bf16[4,4,128,256]{3,2,1,0:T(8,128)(2,1)}, bf16[512,1024]{1,0:T(...) custom-call(bf16[8,128,512]{2,1,0:T(8,128)(2,1)} %get-tuple-element., ...), custom_call_target="tpu_custom_call" | custom-call | flops 25769803776 | bytes 41943040 | tf_op jit(solution)/shard_map/middle/pallas_call | solution.py:830
  218.2 143.2 %backward.1 = (f32[512,1024]{1,0:T(8,128)}, f32[512,256]{1,0:T(8,128)}, f32[512,256]{1,0:T(8,128)}, f32[128,256]{1,0:T(8,128)}, f32[3,256,128]{2,1,0:T(8,128)}, ...) custom-call(s32[1,1,4096]{2,1,0:T(1,128)} %get-tuple-element.48.blk_ref, ...), custom_call_target="tpu_custom_call" | custom-call | flops 53687091200 | bytes 8388608 | tf_op jit(solution)/shard_map/backward/pallas_call | solution.py:1390
  361.4 0.0 copy-start
  361.4 1.6 fusion
  363.0 0.8 slice_bitcast_fusion
  363.8 0.7 dynamic_slice.3
  364.4 1.5 copy.29
  365.9 2.3 copy.39
  368.2 0.0 copy-done
  368.2 0.0 copy-start.3
  368.2 0.0 copy-start.4
  368.2 0.0 copy-start.2
  368.2 0.0 copy-start.1
  368.2 1.3 copy.40
  369.5 0.0 copy-done.3
  369.5 0.7 copy.41
  370.3 0.0 copy-done.4
  370.3 0.7 copy.42
  370.9 0.0 copy-done.2
  370.9 0.8 copy.43
  371.7 0.0 copy-done.1
  371.7 0.8 copy.44
  (1 shorter events, 0.0 us)
Async XLA Ops:
  361.4 6.8 %copy-start = (f32[512,1024]{1,0:T(8,128)S(1)}, f32[512,1024]{1,0:T(8,128)}, u32[]{:S(2)}) copy-start(f32[512,1024]{1,0:T(8,128)} %get-tuple-element.93) | copy-start | bytes 6291460
  368.2 1.3 copy-start.3
  368.2 2.1 copy-start.4
  368.2 2.7 copy-start.2
  368.2 3.5 copy-start.1

commit v9 on v8

--- a/solution.py
+++ b/solution.py
@@ -686,7 +686,7 @@
         out_acc[...] = jnp.zeros_like(out_acc)
         norm_acc[...] = jnp.zeros_like(norm_acc)
 
-    @pl.when(step == cols // 2)
+    @pl.when(step == cols * 6 // 8)
     def _():
         own_wq.wait()
         z_stage.wait_recv()

time: 373 us -> 368 us (0.987)
  Pallas kernels: 361 us -> 356 us
where the time goes in v9:
time: 368 us; the launch traced here: 367 us
  Pallas kernels  356 us (97%)
  local copies, waits for them, and re-layouts  11.1 us (3%)
    pallas_call x1, Pallas kernels, front(): pl.pallas_call(functools.partial(front_kernel, rows, cols, heads), in_spe...  154 us
    pallas_call x1, Pallas kernels, backward(): pl.pallas_call(functools.partial(back_kernel, rows, cols, heads, seqs, ti...  142 us
    pallas_call x1, Pallas kernels, middle(): pl.pallas_call(functools.partial(middle_kernel, rows, cols), grid=(2 * co...  59.8 us

profile of v9, /device:TPU:0, one launch (start us, length us, event | category | flops | bytes accessed | tf_op | source)
XLA Modules:
  0.0 367.5 jit_solution(3251966934520386113)
XLA Ops:
  0.6 154.4 %front.1 = (bf16[8,512,1024]{2,1,0:T(8,128)(2,1)}, bf16[2,4096,64]{2,1,0:T(8,128)(2,1)}, bf16[2,4096,64]{2,1,0:T(8,128)(2,1)}, bf16[2,4096,64]{2,1,0:T(8,128)(2,...) custom-call(bf16[512,1024]{1,0:T(8,128)(2,1)} %tok_ref.5, ...), custom_call_target="tpu_custom_call" | custom-call | flops 21474836480 | bytes 8388608 | tf_op jit(solution)/shard_map/front/pallas_call | solution.py:579
  155.0 59.8 %middle.1 = (bf16[4,4,512,256]{3,2,1,0:T(8,128)(2,1)}, bf16[4,4,512,256]{3,2,1,0:T(8,128)(2,1)}, bf16[4,4,128,256]{3,2,1,0:T(8,128)(2,1)}, bf16[512,1024]{1,0:T(...) custom-call(bf16[8,128,512]{2,1,0:T(8,128)(2,1)} %get-tuple-element., ...), custom_call_target="tpu_custom_call" | custom-call | flops 25769803776 | bytes 41943040 | tf_op jit(solution)/shard_map/middle/pallas_call | solution.py:830
  214.8 141.5 %backward.1 = (f32[512,1024]{1,0:T(8,128)}, f32[512,256]{1,0:T(8,128)}, f32[512,256]{1,0:T(8,128)}, f32[128,256]{1,0:T(8,128)}, f32[3,256,128]{2,1,0:T(8,128)}, ...) custom-call(s32[1,1,4096]{2,1,0:T(1,128)} %get-tuple-element.48.blk_ref, ...), custom_call_target="tpu_custom_call" | custom-call | flops 53687091200 | bytes 8388608 | tf_op jit(solution)/shard_map/backward/pallas_call | solution.py:1390
  356.4 0.0 copy-start
  356.4 1.6 fusion
  358.0 0.8 slice_bitcast_fusion
  358.7 0.7 dynamic_slice.3
  359.4 1.5 copy.29
  360.8 2.3 copy.39
  363.1 0.0 copy-done
  363.1 0.0 copy-start.3
  363.1 0.0 copy-start.4
  363.1 0.0 copy-start.2
  363.1 0.0 copy-start.1
  363.1 1.3 copy.40
  364.5 0.0 copy-done.3
  364.5 0.7 copy.41
  365.2 0.0 copy-done.4
  365.2 0.7 copy.42
  365.9 0.0 copy-done.2
  365.9 0.8 copy.43
  366.7 0.0 copy-done.1
  366.7 0.8 copy.44
  (1 shorter events, 0.0 us)
Async XLA Ops:
  356.4 6.8 %copy-start = (f32[512,1024]{1,0:T(8,128)S(1)}, f32[512,1024]{1,0:T(8,128)}, u32[]{:S(2)}) copy-start(f32[512,1024]{1,0:T(8,128)} %get-tuple-element.93) | copy-start | bytes 6291460
  363.1 1.3 copy-start.3
  363.1 2.1 copy-start.4
  363.1 2.7 copy-start.2
  363.1 3.5 copy-start.1
